TPU v7x, 256 devices: a whole 4x4x8 slice. The times are simulated.
256 devices in a mesh: layer: 16 (over z_lo, x), ctx: 16 (over y, z_hi, core).
Axes of the slice: x: 4, y: 4, z: 8 (z_hi: 2, z_lo: 4; z = z_hi * 4 + z_lo), core: 2. Of those that a mesh axis runs over, the one named last changes fastest.
Arguments:
- queries: bfloat16 [16, 2048, 1536], P('layer', 'ctx'), may hold values from -9 to 9
- keys: bfloat16 [2048, 512], P(('ctx', 'layer')), may hold values from -4 to 4
- values: bfloat16 [2048, 512], P(('ctx', 'layer')), may hold values from -6 to 6
- head: float32 [16, 1536, 2], P('layer'), may hold values from -1.5 to 1.5
- segments: int32 [2048], replicated, may hold values from 0 to 4, as said below
- label_mask: int32 [2048], P('ctx'), may hold values 0 or 1
- labels: int32 [2048], P('ctx'), may hold values from 0 to 1
Outputs:
- loss: float32 [16], P('layer')
- query_gradient: float32 [16, 2048, 1536], P('layer', 'ctx')
- grad_keys: float32 [2048, 512], P(('ctx', 'layer'))
- grad_values: float32 [2048, 512], P(('ctx', 'layer'))
- head_gradient_rows: float32 [16, 1536, 2], P('layer')
Inputs may be any that keep to these rules, and one draw needn't show every extreme that they name: `segments`: document ids never fall; the first document spans exactly 1536 positions and the positions after it form exactly four more documents, each of one position or more.
All inputs are finite; a program needn't handle non-finite values. No bound on the sum of `label_mask` on one device may be relied on, other than what follows from the above.
Results may differ from a plain program's by a relative error of at most 0.019.
Values may be sent and summed in bfloat16 or wider, within the bound.
No kernel may reach another device: no remote copies, remote signals or barrier semaphores. Data moves between devices by JAX's collectives and lax.ppermute only.
A program may use at most 128 MiB of HBM per device.

v0:
```python
import jax
import jax.numpy as jnp
from jax import lax
from jax.experimental import pallas as pl
from jax.experimental.pallas import tpu as pltpu
from jax.sharding import Mesh, PartitionSpec as P

HEAD_WIDTH = 128
GROUP = 3
WIDE = GROUP * HEAD_WIDTH
BLOCK = 128
CHUNK = 512
TOKENS = 2048
SCALE = HEAD_WIDTH ** -0.5
LOG2E = 1.4426950408889634
NEG = -1.0e30
F32 = jnp.float32
BF16 = jnp.bfloat16
CHUNKS = ((0,), (0, 1), (0, 1, 2), (3,))
P_AT = (0, 1, 3, 6)
YZ_AXES = ("zl", "y", "zh")


VMEM = pl.BlockSpec(memory_space=pltpu.VMEM)
HBM = pl.BlockSpec(memory_space=pltpu.HBM)
SMEM = pl.BlockSpec(memory_space=pltpu.SMEM)


def coords(did_ref):
    d = did_ref[0]
    return d // 64, (d // 16) % 4, (d // 4) % 4, (d // 2) % 2, d % 2


def prep_kernel(did, keys, values, labels, mask, queries, w, seg, kv_out, q0, q1, q2, q3, w_out, seg_out, kb, vb, lb, mb, sems):
    _, _, y, _, _ = coords(did)
    outs = (q0, q1, q2, q3)
    early = [
        pltpu.make_async_copy(keys, kb, sems.at[0]),
        pltpu.make_async_copy(values, vb, sems.at[1]),
        pltpu.make_async_copy(labels, lb, sems.at[2]),
        pltpu.make_async_copy(mask, mb, sems.at[3]),
    ]
    late = [pltpu.make_async_copy(w, w_out, sems.at[4]), pltpu.make_async_copy(seg, seg_out, sems.at[5])]
    for k in range(4):
        g = pl.multiple_of(((y + k) % 4) * WIDE, HEAD_WIDTH)
        late.append(pltpu.make_async_copy(queries.at[:, pl.ds(g, WIDE)], outs[k].at[pl.ds(0, BLOCK)], sems.at[6 + k]))
    for copy in early + late:
        copy.start()
    for copy in early:
        copy.wait()
    for g in range(4):
        cols = slice(g * HEAD_WIDTH, (g + 1) * HEAD_WIDTH)
        both = jnp.concatenate([kb[:, cols], vb[:, cols]], axis=1)
        for zl_to in range(4):
            for zh_to in range(2):
                kv_out[zl_to, g, zh_to] = both
    lab = jnp.broadcast_to(lb[...].astype(F32), (16, BLOCK))
    msk = jnp.broadcast_to(mb[...].astype(F32), (16, BLOCK))
    tail = jnp.concatenate([lab, msk, lab], axis=1).astype(BF16)
    for k in range(4):
        outs[k][BLOCK:, :] = tail
    for copy in late:
        copy.wait()


def head_diff(w, y, h):
    at = pl.multiple_of(y * WIDE + h * HEAD_WIDTH, HEAD_WIDTH)
    return w[0:1, pl.ds(at, HEAD_WIDTH)] - w[1:2, pl.ds(at, HEAD_WIDTH)]


def halves(v):
    high = v.astype(BF16).astype(F32)
    return high, v - high


def stack8(rows):
    at = lax.broadcasted_iota(jnp.int32, (8, rows[0].shape[1]), 0)
    out = jnp.zeros((8, rows[0].shape[1]), F32)
    for r, row in enumerate(rows):
        out = jnp.where(at == r, row, out)
    return out


def on_both(v):
    high, low = halves(v)
    return jnp.concatenate([high, low], axis=0).astype(BF16)


def forward_kernel(did, seg, w, q0, q1, q2, q3, *rest):
    kvs = rest[:8]
    plog, p_out, inv_out, delta_out, qt, kv_out, kt_out, u_out = rest[8:16]
    kvf, _, s_buf, u_rows = rest[16:]
    _, x, y, zh, c = coords(did)
    for k, ref in enumerate((q0, q1, q2, q3)):
        slot = (y - k + 4) % 4
        for h in range(GROUP):
            one = ref[:BLOCK, h * HEAD_WIDTH : (h + 1) * HEAD_WIDTH]
            qt[slot, :, h * BLOCK : (h + 1) * BLOCK] = one.astype(F32).T.astype(BF16)
    for cc in range(2):
        cs = (c + cc) % 2
        for kx in range(4):
            ref = kvs[cc * 4 + kx]
            xs = (x - kx + 4) % 4

            def place(zl_from, carry, ref=ref, cs=cs, xs=xs):
                for ys in range(4):
                    for zh_from in range(2):
                        row = (ys * 4 + zh_from * 2 + cs) * BLOCK + (zl_from * 4 + xs) * 8
                        kvf[pl.ds(pl.multiple_of(row, 8), 8), :] = ref[zl_from, ys, zh_from].astype(F32)
                return carry

            lax.fori_loop(0, 4, place, 0)
    diffs = stack8([head_diff(w, y, h) for h in range(GROUP)])
    diffs16 = on_both(diffs)
    ones = stack8([jnp.zeros((1, BLOCK), F32)] * GROUP + [jnp.ones((1, BLOCK), F32)])

    def turn(b, carry):
        at = pl.multiple_of(b * BLOCK, BLOCK)
        both = kvf[pl.ds(at, BLOCK), :]
        kv_out[pl.ds(at, BLOCK), :] = both.astype(BF16)
        kt_out[:, pl.ds(at, BLOCK)] = both[:, :HEAD_WIDTH].T.astype(BF16)
        part = jnp.dot(diffs16, both[:, HEAD_WIDTH:].T.astype(BF16), preferred_element_type=F32)
        u = part[:8] + part[8:]
        high, low = halves(u)
        u_rows[:, pl.ds(at, BLOCK)] = jnp.concatenate([high + ones, low], axis=0).astype(BF16)
        wide = jnp.concatenate([u, jnp.zeros((BLOCK - 8, BLOCK), F32)], axis=0)
        u_out[pl.ds(at, BLOCK), :] = wide.T
        return carry

    lax.fori_loop(0, TOKENS // BLOCK, turn, 0)
    j = zh * 2 + c
    key_at = lax.broadcasted_iota(jnp.int32, (BLOCK, BLOCK), 0)
    query_at = lax.broadcasted_iota(jnp.int32, (BLOCK, BLOCK), 1) + j * BLOCK
    for ys in range(4):
        qs = seg[:, pl.ds(pl.multiple_of(ys * CHUNK + j * BLOCK, BLOCK), BLOCK)]
        top = jnp.full((1, WIDE), NEG, F32)
        for i, ch in enumerate(CHUNKS[ys]):
            for b in range(CHUNK // BLOCK):
                row = ch * CHUNK + b * BLOCK
                s = jnp.dot(kv_out[row : row + BLOCK, :HEAD_WIDTH], qt[ys], preferred_element_type=F32)
                if ch == ys:
                    ks = jnp.broadcast_to(seg[:, row : row + BLOCK], (BLOCK, BLOCK)).T
                    ok = (key_at + b * BLOCK <= query_at) & (ks == qs)
                    s = jnp.where(jnp.concatenate([ok] * GROUP, axis=1), s, NEG)
                top = jnp.maximum(top, jnp.max(s, axis=0, keepdims=True))
                at = i * CHUNK + b * BLOCK
                s_buf[at : at + BLOCK, :] = s
        sums = jnp.zeros((16, WIDE), F32)
        for i, ch in enumerate(CHUNKS[ys]):
            at_p = (P_AT[ys] + i) * CHUNK
            for b in range(CHUNK // BLOCK):
                at = i * CHUNK + b * BLOCK
                p = jnp.exp2((s_buf[at : at + BLOCK, :] - top) * (SCALE * LOG2E))
                p_out[at_p + b * BLOCK : at_p + (b + 1) * BLOCK, :] = p.astype(BF16)
            sums = sums + jnp.dot(
                u_rows[:, ch * CHUNK : (ch + 1) * CHUNK], p_out[at_p : at_p + CHUNK, :], preferred_element_type=F32
            )
        inv = 1.0 / sums[GROUP : GROUP + 1, :]
        both = (sums[:8] + sums[8:]) * inv
        delta = jnp.concatenate([both[h : h + 1, h * BLOCK : (h + 1) * BLOCK] for h in range(GROUP)], axis=1)
        inv_out[ys] = jnp.broadcast_to(inv, (8, WIDE))
        delta_out[ys] = jnp.broadcast_to(delta, (8, WIDE))
        lg = delta[:, :BLOCK] + delta[:, BLOCK : 2 * BLOCK] + delta[:, 2 * BLOCK :]
        plog[(y - ys + 4) % 4] = jnp.broadcast_to(lg, (8, BLOCK))


def middle_kernel(p, delta, u, kt, g_out, dq_out):
    for ys in range(4):
        dqt = jnp.zeros((HEAD_WIDTH, WIDE), F32)
        for i, ch in enumerate(CHUNKS[ys]):
            at_p = (P_AT[ys] + i) * CHUNK
            for b in range(CHUNK // BLOCK):
                row = ch * CHUNK + b * BLOCK
                at = slice(at_p + b * BLOCK, at_p + (b + 1) * BLOCK)
                ub = jnp.concatenate(
                    [jnp.broadcast_to(u[row : row + BLOCK, h : h + 1], (BLOCK, BLOCK)) for h in range(GROUP)], axis=1
                )
                g_out[at, :] = (p[at, :].astype(F32) * (ub - delta[ys, 0:1, :])).astype(BF16)
            dqt = dqt + jnp.dot(
                kt[:, ch * CHUNK : (ch + 1) * CHUNK], g_out[at_p : at_p + CHUNK, :], preferred_element_type=F32
            )
        dq_out[ys] = dqt


NT = (((1,), (1,)), ((), ()))


def backward_kernel(did, w, l0, l1, l2, l3, g0, g1, g2, g3, p, g, inv, qt, kv, dqt, *rest):
    dq_outs = rest[:4]
    dkv_outs = rest[4:6]
    lgs, labs, dqb, acc, ct = rest[6:]
    _, x, y, _, c = coords(did)
    for k, ref in enumerate((l0, l1, l2, l3)):
        src = (y - k + 4) % 4
        for m in range(4):
            ys = (y - m + 4) % 4
            lgs[src, ys] = ref[(m - k) % 4]
    for k, ref in enumerate((g0, g1, g2, g3)):
        labs[(y - k + 4) % 4] = ref[BLOCK:, :256].astype(F32)[8:16, :]
    diffs = [head_diff(w, y, h) for h in range(GROUP)]
    wt = jnp.concatenate([jnp.broadcast_to(d, (BLOCK, HEAD_WIDTH)).T for d in diffs], axis=1)
    head_of = lax.broadcasted_iota(jnp.int32, (8, WIDE), 1) // BLOCK
    head_at = lax.broadcasted_iota(jnp.int32, (8, WIDE), 0)
    loss = jnp.zeros((1, BLOCK), F32)
    seen = set()
    for ys in range(4):
        z = (lgs[0, ys] + lgs[1, ys] + lgs[2, ys] + lgs[3, ys])[0:1, :]
        one = labs[ys, 0:1, :BLOCK] > 0.5
        mask = labs[ys, 0:1, BLOCK:]
        a = jnp.where(one, z, -z)
        e = jnp.exp(-jnp.abs(a))
        loss = loss + mask * (jnp.maximum(a, 0.0) + jnp.log(1.0 + e))
        sig = jnp.where(a >= 0.0, 1.0, e) / (1.0 + e)
        d0 = mask * jnp.where(one, sig, -sig)
        f = jnp.concatenate([d0] * GROUP, axis=1) * inv[ys, 0:1, :]
        fs = f * SCALE
        at16 = (wt * f).astype(BF16)
        qf = (qt[ys].astype(F32) * fs).astype(BF16)
        fm = on_both(jnp.where(head_of == head_at, f, 0.0))
        for i, ch in enumerate(CHUNKS[ys]):
            at = slice((P_AT[ys] + i) * CHUNK, (P_AT[ys] + i + 1) * CHUNK)
            rows = slice(ch * CHUNK, (ch + 1) * CHUNK)
            dk = lax.dot_general(g[at, :], qf, NT, preferred_element_type=F32)
            dv = lax.dot_general(p[at, :], at16, NT, preferred_element_type=F32)
            cs = lax.dot_general(fm, p[at, :], NT, preferred_element_type=F32)
            cs = cs[:8] + cs[8:]
            if ch in seen:
                acc[rows, :HEAD_WIDTH] += dk
                acc[rows, HEAD_WIDTH:] += dv
                ct[:, rows] += cs
            else:
                seen.add(ch)
                acc[rows, :HEAD_WIDTH] = dk
                acc[rows, HEAD_WIDTH:] = dv
                ct[:, rows] = cs
        slot = (y - ys + 4) % 4
        dqs = dqt[ys] * fs
        for h in range(GROUP):
            cols = slice(h * BLOCK, (h + 1) * BLOCK)
            dqb[slot, :, cols] = dqs[:, cols].T.astype(BF16)
    for k in range(4):
        dq_outs[k][...] = dqb[k]
    hg = jnp.dot(on_both(ct[...]), kv[:, HEAD_WIDTH:], preferred_element_type=F32)
    hg = hg[:8] + hg[8:]
    row8 = lax.broadcasted_iota(jnp.int32, (8, BLOCK), 0)
    hg = jnp.where(row8 == GROUP, loss, hg)
    high, low = halves(hg)
    tail = jnp.concatenate([high, low], axis=1).astype(BF16)
    for cc in range(2):
        cs = (c + cc) % 2
        ref = dkv_outs[cc]
        ref[128] = tail

        def place(zl_to, carry, ref=ref, cs=cs):
            for kx in range(4):
                xs = (x - kx + 4) % 4
                for ys in range(4):
                    for zh_to in range(2):
                        row = (ys * 4 + zh_to * 2 + cs) * BLOCK + (zl_to * 4 + xs) * 8
                        piece = acc[pl.ds(pl.multiple_of(row, 8), 8), :]
                        ref[kx * 32 + zl_to * 8 + ys * 2 + zh_to] = piece.astype(BF16)
            return carry

        lax.fori_loop(0, 4, place, 0)


def core_kernel(own, far, b0, b1, b2, b3, hg):
    outs = (b0, b1, b2, b3)

    def add(z, carry):
        for kx in range(4):
            at = pl.ds(kx * 32 + z * 8, 8)
            outs[kx][pl.ds(z * 8, 8)] = (own[at].astype(F32) + far[at].astype(F32)).astype(BF16)
        return carry

    lax.fori_loop(0, 4, add, 0)
    a, b = own[128].astype(F32), far[128].astype(F32)
    hg[...] = (a[:, :BLOCK] + a[:, BLOCK:]) + (b[:, :BLOCK] + b[:, BLOCK:])


def x_kernel(b0, b1, b2, b3, hg, out):
    high, low = halves(hg[...])
    tail = jnp.concatenate([high[:4], low[:4]], axis=0).astype(BF16)
    tail = jnp.broadcast_to(tail[None], (8, 8, BLOCK))

    def add(z, carry):
        at = pl.ds(z * 8, 8)
        v = b0[at].astype(F32) + b1[at].astype(F32) + b2[at].astype(F32) + b3[at].astype(F32)
        out[z, :, :, :256] = v.astype(BF16)
        out[z, :, :, 256:] = tail
        return carry

    lax.fori_loop(0, 4, add, 0)


def finish_kernel(did, pieces, d0, d1, d2, d3, qg, gk, gv, hg, loss):
    zl, _, y, _, _ = coords(did)
    for g in range(4):
        v = jnp.zeros((8, 256), F32)
        for z in range(4):
            for k in range(2):
                v = v + pieces[z, g * 2 + k, :, :256].astype(F32)
        gk[:, g * HEAD_WIDTH : (g + 1) * HEAD_WIDTH] = v[:, :HEAD_WIDTH]
        gv[:, g * HEAD_WIDTH : (g + 1) * HEAD_WIDTH] = v[:, HEAD_WIDTH:]
        v = pieces[zl, g * 2, :, 256:].astype(F32)
        t = pieces[zl, g * 2 + 1, :, 256:].astype(F32)
        v = (v[:4] + v[4:]) + (t[:4] + t[4:])
        for h in range(GROUP):
            cols = slice(g * WIDE + h * HEAD_WIDTH, g * WIDE + (h + 1) * HEAD_WIDTH)
            hg[0:1, cols] = v[h : h + 1]
            hg[1:2, cols] = -v[h : h + 1]
        if g == 0:
            loss[0] = jnp.sum(v[GROUP : GROUP + 1]) * (1.0 / TOKENS)
    for k, d in enumerate((d0, d1, d2, d3)):
        wide = pl.ds(pl.multiple_of(((y + k) % 4) * WIDE, HEAD_WIDTH), WIDE)
        qg[:, wide] = d[...].astype(F32)


def shift(v, axis, size, k):
    return lax.ppermute(v, axis, [(i, (i + k) % size) for i in range(size)])


def like(shape, dtype):
    return jax.ShapeDtypeStruct(shape, dtype)


def in_hbm(v):
    return pltpu.with_memory_space_constraint(v, pltpu.HBM)


def call(kernel, out_shape, specs, out_specs=None, scratch=()):
    return pl.pallas_call(
        kernel,
        out_shape=out_shape,
        in_specs=specs,
        out_specs=out_specs or [VMEM] * len(out_shape),
        scratch_shapes=list(scratch),
        compiler_params=pltpu.CompilerParams(vmem_limit_bytes=20 << 20),
    )


def per_device(queries, keys, values, head, segments, label_mask, labels):
    did = lax.axis_index(("zl", "x", "y", "zh", "c")).astype(jnp.int32).reshape(1)
    copies, *packs, w, seg = call(
        prep_kernel,
        [like((4, 4, 2, 8, 256), BF16)]
        + [like((BLOCK + 16, WIDE), BF16)] * 4
        + [like((2, 4 * WIDE), F32), like((1, TOKENS), jnp.int32)],
        [SMEM] + [HBM] * 7,
        scratch=[
            pltpu.VMEM((8, 512), BF16),
            pltpu.VMEM((8, 512), BF16),
            pltpu.VMEM((1, BLOCK), jnp.int32),
            pltpu.VMEM((1, BLOCK), jnp.int32),
            pltpu.SemaphoreType.DMA((10,)),
        ],
    )(
        did,
        in_hbm(keys),
        in_hbm(values),
        in_hbm(labels.reshape(1, BLOCK)),
        in_hbm(label_mask.reshape(1, BLOCK)),
        in_hbm(queries[0]),
        in_hbm(head[0].T),
        in_hbm(segments.reshape(1, TOKENS)),
    )
    own = lax.all_to_all(copies.reshape(32, 8, 256), YZ_AXES, 0, 0, tiled=True).reshape(4, 4, 2, 8, 256)
    over_x = [own]
    for k in range(1, 4):
        over_x.append(shift(own, "x", 4, k))
    over_c = [shift(a, "c", 2, 1) for a in over_x]
    for k in range(1, 4):
        packs[k] = shift(packs[k], "y", 4, k)
    plog, p, inv, delta, qt, kv, kt, u = call(
        forward_kernel,
        [
            like((4, 8, BLOCK), F32),
            like((7 * CHUNK, WIDE), BF16),
            like((4, 8, WIDE), F32),
            like((4, 8, WIDE), F32),
            like((4, HEAD_WIDTH, WIDE), BF16),
            like((TOKENS, 256), BF16),
            like((HEAD_WIDTH, TOKENS), BF16),
            like((TOKENS, BLOCK), F32),
        ],
        [SMEM] + [VMEM] * 14,
        scratch=[
            pltpu.VMEM((TOKENS, 256), F32),
            pltpu.VMEM((HEAD_WIDTH, TOKENS), BF16),
            pltpu.VMEM((3 * CHUNK, WIDE), F32),
            pltpu.VMEM((16, TOKENS), BF16),
        ],
    )(did, seg, w, *packs, *over_x, *over_c)
    logs = [plog] + [shift(plog, "y", 4, k) for k in range(1, 4)]
    g, dqt = call(
        middle_kernel, [like((7 * CHUNK, WIDE), BF16), like((4, HEAD_WIDTH, WIDE), F32)], [VMEM] * 4
    )(p, delta, u, kt)
    *dq, own_d, far_d = call(
        backward_kernel,
        [like((BLOCK, WIDE), BF16)] * 4 + [like((129, 8, 256), BF16)] * 2,
        [SMEM] + [VMEM] * 15,
        scratch=[
            pltpu.VMEM((4, 4, 8, BLOCK), F32),
            pltpu.VMEM((4, 8, 256), F32),
            pltpu.VMEM((4, BLOCK, WIDE), BF16),
            pltpu.VMEM((TOKENS, 256), F32),
            pltpu.VMEM((8, TOKENS), F32),
        ],
    )(did, w, *logs, *packs, p, g, inv, qt, kv, dqt)
    far = shift(far_d, "c", 2, 1)
    *by_x, hg = call(core_kernel, [like((32, 8, 256), BF16)] * 4 + [like((8, BLOCK), F32)], [VMEM] * 2)(own_d, far)
    got = [by_x[0]] + [shift(by_x[k], "x", 4, -k) for k in range(1, 4)]
    (by_z,) = call(x_kernel, [like((4, 8, 8, WIDE), BF16)], [VMEM] * 5)(*got, hg)
    pieces = lax.all_to_all(by_z.reshape(32, 8, WIDE), YZ_AXES, 0, 0, tiled=True).reshape(4, 8, 8, WIDE)
    back = [dq[0]]
    for k in range(1, 4):
        back.append(shift(dq[k], "y", 4, -k))
    query_gradient, grad_keys, grad_values, head_t, loss = call(
        finish_kernel,
        [
            like((BLOCK, 4 * WIDE), F32),
            like((8, 512), F32),
            like((8, 512), F32),
            like((2, 4 * WIDE), F32),
            like((1,), F32),
        ],
        [SMEM] + [VMEM] * 5,
        [VMEM] * 4 + [SMEM],
    )(did, pieces, *back)
    return loss, query_gradient[None], grad_keys, grad_values, head_t.T[None]


def solution(mesh):
    fine = Mesh(mesh.devices.reshape(4, 4, 4, 2, 2), ("zl", "x", "y", "zh", "c"))
    layer, ctx = ("zl", "x"), ("y", "zh", "c")
    return jax.shard_map(
        per_device,
        mesh=fine,
        in_specs=(
            P(layer, ctx, None),
            P(ctx + layer, None),
            P(ctx + layer, None),
            P(layer, None, None),
            P(),
            P(ctx),
            P(ctx),
        ),
        out_specs=(
            P(layer),
            P(layer, ctx, None),
            P(ctx + layer, None),
            P(ctx + layer, None),
            P(layer, None, None),
        ),
        check_vma=False,
    )
```

profile of v0, /device:TPU:1, one launch (start us, length us, event | category | flops | bytes accessed | tf_op | source)
XLA Modules:
  0.0 91.4 jit_solution(13134055030184819591)
XLA Ops:
  0.6 1.2 %shard_map.110 = (bf16[4,4,2,8,256]{4,3,2,1,0:T(8,128)(2,1)S(1)}, bf16[144,384]{1,0:T(8,128)(2,1)S(1)}, bf16[144,384]{1,0:T(8,128)(2,1)S(1)}, bf16[144,384]{1,0:...) custom-call(s32[1]{0:T(128)} %bitcast.did, bf16[8,512]{1,0:T(8,128)(2,1)} %keys.1, ...), custom_call_target="tpu_custom_call" | custom-call | tf_op jit(solution)/shard_map/pallas_call | solution.py:344
  1.9 21.0 %all_to_all.10 = bf16[32,8,256]{2,1,0:T(8,128)(2,1)S(1)} all-to-all(bf16[32,8,256]{2,1,0:T(8,128)(2,1)S(1)} %bitcast.22), channel_id=1, replica_groups=mesh['zl'=4,'x'=4,'y'=4,'zh'=2,'c'=2] {'zl','y','zh'}, dimensions={0} | all-to-all | bytes 262144 | tf_op jit(solution)/shard_map/all_to_all | solution.py:367
  22.8 1.2 %collective-permute-start.3 = (bf16[4,4,2,8,256]{4,3,2,1,0:T(8,128)(2,1)S(1)}, bf16[4,4,2,8,256]{4,3,2,1,0:T(8,128)(2,1)S(1)}, u32[]{:S(2)}, u32[]{:S(2)}) collective-permute-start(bf16[4,4,2,8,256]{4,3,2,1,0:T(8,128)(2,1)S(1)} %bitcast.17), channel_id=1, source_target_pairs={{0,16},{16,32},{32,48},{48,0},{1,17},{17,33},{33,49},{49,1},{2,18}... | collective-permute-start | bytes 393224 | tf_op jit(solution)/shard_map/ppermute | solution.py:320
  24.0 2.5 %collective-permute-start.4 = (bf16[4,4,2,8,256]{4,3,2,1,0:T(8,128)(2,1)S(1)}, bf16[4,4,2,8,256]{4,3,2,1,0:T(8,128)(2,1)S(1)}, u32[]{:S(2)}, u32[]{:S(2)}) collective-permute-start(bf16[4,4,2,8,256]{4,3,2,1,0:T(8,128)(2,1)S(1)} %bitcast.18), channel_id=1, source_target_pairs={{0,32},{16,48},{32,0},{48,16},{1,33},{17,49},{33,1},{49,17},{2,34}... | collective-permute-start | bytes 393224 | tf_op jit(solution)/shard_map/ppermute | solution.py:320
  26.5 1.2 %collective-permute-start.5 = (bf16[4,4,2,8,256]{4,3,2,1,0:T(8,128)(2,1)S(1)}, bf16[4,4,2,8,256]{4,3,2,1,0:T(8,128)(2,1)S(1)}, u32[]{:S(2)}, u32[]{:S(2)}) collective-permute-start(bf16[4,4,2,8,256]{4,3,2,1,0:T(8,128)(2,1)S(1)} %bitcast.19), channel_id=1, source_target_pairs={{0,48},{16,0},{32,16},{48,32},{1,49},{17,1},{33,17},{49,33},{2,50}... | collective-permute-start | bytes 393224 | tf_op jit(solution)/shard_map/ppermute | solution.py:320
  27.7 2.5 %collective-permute-start.1 = (bf16[144,384]{1,0:T(8,128)(2,1)S(1)}, bf16[144,384]{1,0:T(8,128)(2,1)S(1)}, u32[]{:S(2)}, u32[]{:S(2)}) collective-permute-start(bf16[144,384]{1,0:T(8,128)(2,1)S(1)} %get-tuple-element.42), channel_id=1, source_target_pairs={{0,8},{4,12},{8,0},{12,4},{1,9},{5,13},{9,1},{13,5},{2,10},{6,14},... | collective-permute-start | bytes 331784 | tf_op jit(solution)/shard_map/ppermute | solution.py:320
  30.3 2.5 %collective-permute-done.q1.g1 = bf16[144,384]{1,0:T(8,128)(2,1)S(1)} collective-permute-done((bf16[144,384]{1,0:T(8,128)(2,1)S(1)}, bf16[144,384]{1,0:T(8,128)(2,1)S(1)}, u32[]{:S(2)}, u32[]{:S(2)}) %collective-permute-start) | collective-permute-done | bytes 110624 | tf_op jit(solution)/shard_map/ppermute | solution.py:320
  32.8 3.7 %collective-permute-start.6 = (bf16[4,4,2,8,256]{4,3,2,1,0:T(8,128)(2,1)S(1)}, bf16[4,4,2,8,256]{4,3,2,1,0:T(8,128)(2,1)S(1)}, u32[]{:S(2)}, u32[]{:S(2)}) collective-permute-start(bf16[4,4,2,8,256]{4,3,2,1,0:T(8,128)(2,1)S(1)} %bitcast.20), channel_id=1, source_target_pairs={{0,1},{1,0},{2,3},{3,2},{4,5},{5,4},{6,7},{7,6},{8,9},{9,8},{10,11... | collective-permute-start | bytes 393224 | tf_op jit(solution)/shard_map/ppermute | solution.py:320
  36.5 0.5 collective-permute-start.8
  37.1 0.5 collective-permute-start.2
  37.6 3.1 %collective-permute-done.2.q3.g3 = bf16[144,384]{1,0:T(8,128)(2,1)S(1)} collective-permute-done((bf16[144,384]{1,0:T(8,128)(2,1)S(1)}, bf16[144,384]{1,0:T(8,128)(2,1)S(1)}, u32[]{:S(2)}, u32[]{:S(2)}) %collective-permute-start.2) | collective-permute-done | bytes 110624 | tf_op jit(solution)/shard_map/ppermute | solution.py:320
  40.7 8.3 %shard_map.111 = (f32[4,8,128]{2,1,0:T(8,128)S(1)}, bf16[3584,384]{1,0:T(8,128)(2,1)S(1)}, f32[4,8,384]{2,1,0:T(8,128)S(1)}, f32[4,8,384]{2,1,0:T(8,128)S(1)}, b...) custom-call(s32[1]{0:T(128)} %bitcast.did, ...), custom_call_target="tpu_custom_call" | custom-call | tf_op jit(solution)/shard_map/pallas_call | solution.py:374
  49.1 2.9 %collective-permute-start.11 = (f32[4,8,128]{2,1,0:T(8,128)S(1)}, f32[4,8,128]{2,1,0:T(8,128)S(1)}, u32[]{:S(2)}, u32[]{:S(2)}) collective-permute-start(f32[4,8,128]{2,1,0:T(8,128)S(1)} %get-tuple-element.45.l0), channel_id=1, source_target_pairs={{0,8},{4,12},{8,0},{12,4},{1,9},{5,13},{9,1},{13,5},{2,10},{6,14},... | collective-permute-start | bytes 49160 | tf_op jit(solution)/shard_map/ppermute | solution.py:320
  52.0 2.0 %shard_map.112 = (bf16[3584,384]{1,0:T(8,128)(2,1)S(1)}, f32[4,128,384]{2,1,0:T(8,128)S(1)}) custom-call(bf16[3584,384]{1,0:T(8,128)(2,1)S(1)} %get-tuple-element.46.p, f32[4,8,384]{2,1,0:T(8,128)S(1)} %get-tuple-element.47.delta, f32[2048,128]{1,0:T(8,128)S(1)} %get-tuple-element.48.u, bf16[128,2048]{1,0:T(8,128)(2,1)S(1)} %get-tuple-element.49.kt), custom_call_target="tpu_custom_call" | custom-call | tf_op jit(solution)/shard_map/pallas_call | solution.py:395
  54.0 0.6 collective-permute-done.12.l3
  54.6 2.8 %shard_map.113 = (bf16[128,384]{1,0:T(8,128)(2,1)S(1)}, bf16[128,384]{1,0:T(8,128)(2,1)S(1)}, bf16[128,384]{1,0:T(8,128)(2,1)S(1)}, bf16[128,384]{1,0:T(8,128)(2...) custom-call(s32[1]{0:T(128)} %bitcast.did, f32[2,1536]{1,0:T(2,128)S(1)} %get-tuple-element.38.w, ...), custom_call_target="tpu_custom_call" | custom-call | tf_op jit(solution)/shard_map/pallas_call | solution.py:398
  57.4 5.1 %collective-permute-start.13 = (bf16[129,8,256]{2,1,0:T(8,128)(2,1)S(1)}, bf16[129,8,256]{2,1,0:T(8,128)(2,1)S(1)}, u32[]{:S(2)}, u32[]{:S(2)}) collective-permute-start(bf16[129,8,256]{2,1,0:T(8,128)(2,1)S(1)} %get-tuple-element.56), channel_id=1, source_target_pairs={{0,1},{1,0},{2,3},{3,2},{4,5},{5,4},{6,7},{7,6},{8,9},{9,8},{10,11... | collective-permute-start | bytes 1585160 | tf_op jit(solution)/shard_map/ppermute | solution.py:320
  62.5 1.5 %collective-permute-done.13.far = bf16[129,8,256]{2,1,0:T(8,128)(2,1)S(1)} collective-permute-done((bf16[129,8,256]{2,1,0:T(8,128)(2,1)S(1)}, bf16[129,8,256]{2,1,0:T(8,128)(2,1)S(1)}, u32[]{:S(2)}, u32[]{:S(2)}) %collective-permute-start.13) | collective-permute-done | bytes 528416 | tf_op jit(solution)/shard_map/ppermute | solution.py:320
  64.0 0.1 shard_map.114
  64.3 2.1 %collective-permute-start.15 = (bf16[32,8,256]{2,1,0:T(8,128)(2,1)S(1)}, bf16[32,8,256]{2,1,0:T(8,128)(2,1)S(1)}, u32[]{:S(2)}, u32[]{:S(2)}) collective-permute-start(bf16[32,8,256]{2,1,0:T(8,128)(2,1)S(1)} %get-tuple-element.59), channel_id=1, source_target_pairs={{0,32},{16,48},{32,0},{48,16},{1,33},{17,49},{33,1},{49,17},{2,34}... | collective-permute-start | bytes 393224 | tf_op jit(solution)/shard_map/ppermute | solution.py:320
  66.3 2.6 %collective-permute-done.14.b1 = bf16[32,8,256]{2,1,0:T(8,128)(2,1)S(1)} collective-permute-done((bf16[32,8,256]{2,1,0:T(8,128)(2,1)S(1)}, bf16[32,8,256]{2,1,0:T(8,128)(2,1)S(1)}, u32[]{:S(2)}, u32[]{:S(2)}) %collective-permute-start.14) | collective-permute-done | bytes 131104 | tf_op jit(solution)/shard_map/ppermute | solution.py:320
  68.9 1.6 %collective-permute-done.15.b2 = bf16[32,8,256]{2,1,0:T(8,128)(2,1)S(1)} collective-permute-done((bf16[32,8,256]{2,1,0:T(8,128)(2,1)S(1)}, bf16[32,8,256]{2,1,0:T(8,128)(2,1)S(1)}, u32[]{:S(2)}, u32[]{:S(2)}) %collective-permute-start.15) | collective-permute-done | bytes 131104 | tf_op jit(solution)/shard_map/ppermute | solution.py:320
  70.5 3.1 %collective-permute-done.16.b3 = bf16[32,8,256]{2,1,0:T(8,128)(2,1)S(1)} collective-permute-done((bf16[32,8,256]{2,1,0:T(8,128)(2,1)S(1)}, bf16[32,8,256]{2,1,0:T(8,128)(2,1)S(1)}, u32[]{:S(2)}, u32[]{:S(2)}) %collective-permute-start.16) | collective-permute-done | bytes 131104 | tf_op jit(solution)/shard_map/ppermute | solution.py:320
  73.6 0.8 shard_map.115
  74.4 3.9 %all-to-all-start.1 = ((bf16[32,8,384]{2,1,0:T(8,128)(2,1)}), bf16[32,8,384]{2,1,0:T(8,128)(2,1)S(1)}, u32[]{:S(2)}, u32[]{:S(2)}) async-start(bf16[32,8,384]{2,1,0:T(8,128)(2,1)} %bitcast.9), calls=%async_computation.1 | async-start | bytes 393216 | tf_op jit(solution)/shard_map/all_to_all | solution.py:414
  78.3 2.5 %collective-permute-start.17 = (bf16[128,384]{1,0:T(8,128)(2,1)S(1)}, bf16[128,384]{1,0:T(8,128)(2,1)S(1)}, u32[]{:S(2)}, u32[]{:S(2)}) collective-permute-start(bf16[128,384]{1,0:T(8,128)(2,1)S(1)} %get-tuple-element.63), channel_id=1, source_target_pairs={{0,12},{4,0},{8,4},{12,8},{1,13},{5,1},{9,5},{13,9},{2,14},{6,2},{... | collective-permute-start | bytes 294920 | tf_op jit(solution)/shard_map/ppermute | solution.py:320
  80.8 0.6 collective-permute-start.18
  81.4 0.6 collective-permute-start.19
  81.9 2.0 %collective-permute-done.17.d1 = bf16[128,384]{1,0:T(8,128)(2,1)S(1)} collective-permute-done((bf16[128,384]{1,0:T(8,128)(2,1)S(1)}, bf16[128,384]{1,0:T(8,128)(2,1)S(1)}, u32[]{:S(2)}, u32[]{:S(2)}) %collective-permute-start.17) | collective-permute-done | bytes 98336 | tf_op jit(solution)/shard_map/ppermute | solution.py:320
  83.9 2.9 %collective-permute-done.18.d2 = bf16[128,384]{1,0:T(8,128)(2,1)S(1)} collective-permute-done((bf16[128,384]{1,0:T(8,128)(2,1)S(1)}, bf16[128,384]{1,0:T(8,128)(2,1)S(1)}, u32[]{:S(2)}, u32[]{:S(2)}) %collective-permute-start.18) | collective-permute-done | bytes 98336 | tf_op jit(solution)/shard_map/ppermute | solution.py:320
  86.8 3.5 %collective-permute-done.19.d3 = bf16[128,384]{1,0:T(8,128)(2,1)S(1)} collective-permute-done((bf16[128,384]{1,0:T(8,128)(2,1)S(1)}, bf16[128,384]{1,0:T(8,128)(2,1)S(1)}, u32[]{:S(2)}, u32[]{:S(2)}) %collective-permute-start.19) | collective-permute-done | bytes 98336 | tf_op jit(solution)/shard_map/ppermute | solution.py:320
  90.2 1.0 %shard_map.116 = (f32[128,1536]{1,0:T(8,128)}, f32[8,512]{1,0:T(8,128)}, f32[8,512]{1,0:T(8,128)}, f32[2,1536]{1,0:T(2,128)}, f32[1]{0:T(128)}) custom-call(s32[1]{0:T(128)} %bitcast.did, bf16[4,8,8,384]{3,2,1,0:T(8,128)(2,1)S(1)} %bitcast.16, bf16[128,384]{1,0:T(8,128)(2,1)S(1)} %get-tuple-element.62.d0, bf16[128,384]{1,0:T(8,128)(2,1)S(1)} %collective-permute-done.17.d1, ...), custom_call_target="tpu_custom_call" | custom-call | tf_op jit(solution)/shard_map/pallas_call | solution.py:418
  (18 shorter events, 0.4 us)
Async XLA Ops:
  22.8 13.6 %collective-permute-start.3 = (bf16[4,4,2,8,256]{4,3,2,1,0:T(8,128)(2,1)S(1)}, bf16[4,4,2,8,256]{4,3,2,1,0:T(8,128)(2,1)S(1)}, u32[]{:S(2)}, u32[]{:S(2)}) collective-permute-start(bf16[4,4,2,8,256]{4,3,2,1,0:T(8,128)(2,1)S(1)} %bitcast.17), channel_id=1, source_target_pairs={{0,16},{16,32},{32,48},{48,0},{1,17},{17,33},{33,49},{49,1},{2,18}... | collective-permute-start | bytes 393224 | tf_op jit(solution)/shard_map/ppermute | solution.py:320
  24.0 12.4 %collective-permute-start.4 = (bf16[4,4,2,8,256]{4,3,2,1,0:T(8,128)(2,1)S(1)}, bf16[4,4,2,8,256]{4,3,2,1,0:T(8,128)(2,1)S(1)}, u32[]{:S(2)}, u32[]{:S(2)}) collective-permute-start(bf16[4,4,2,8,256]{4,3,2,1,0:T(8,128)(2,1)S(1)} %bitcast.18), channel_id=1, source_target_pairs={{0,32},{16,48},{32,0},{48,16},{1,33},{17,49},{33,1},{49,17},{2,34}... | collective-permute-start | bytes 393224 | tf_op jit(solution)/shard_map/ppermute | solution.py:320
  26.5 10.5 %collective-permute-start.5 = (bf16[4,4,2,8,256]{4,3,2,1,0:T(8,128)(2,1)S(1)}, bf16[4,4,2,8,256]{4,3,2,1,0:T(8,128)(2,1)S(1)}, u32[]{:S(2)}, u32[]{:S(2)}) collective-permute-start(bf16[4,4,2,8,256]{4,3,2,1,0:T(8,128)(2,1)S(1)} %bitcast.19), channel_id=1, source_target_pairs={{0,48},{16,0},{32,16},{48,32},{1,49},{17,1},{33,17},{49,33},{2,50}... | collective-permute-start | bytes 393224 | tf_op jit(solution)/shard_map/ppermute | solution.py:320
  27.7 5.1 %collective-permute-start = (bf16[144,384]{1,0:T(8,128)(2,1)S(1)}, bf16[144,384]{1,0:T(8,128)(2,1)S(1)}, u32[]{:S(2)}, u32[]{:S(2)}) collective-permute-start(bf16[144,384]{1,0:T(8,128)(2,1)S(1)} %get-tuple-element.41), channel_id=1, source_target_pairs={{0,4},{4,8},{8,12},{12,0},{1,5},{5,9},{9,13},{13,1},{2,6},{6,10},{... | collective-permute-start | bytes 331784 | tf_op jit(solution)/shard_map/ppermute | solution.py:320
  27.7 9.3 %collective-permute-start.1 = (bf16[144,384]{1,0:T(8,128)(2,1)S(1)}, bf16[144,384]{1,0:T(8,128)(2,1)S(1)}, u32[]{:S(2)}, u32[]{:S(2)}) collective-permute-start(bf16[144,384]{1,0:T(8,128)(2,1)S(1)} %get-tuple-element.42), channel_id=1, source_target_pairs={{0,8},{4,12},{8,0},{12,4},{1,9},{5,13},{9,1},{13,5},{2,10},{6,14},... | collective-permute-start | bytes 331784 | tf_op jit(solution)/shard_map/ppermute | solution.py:320
  32.8 7.9 %collective-permute-start.6 = (bf16[4,4,2,8,256]{4,3,2,1,0:T(8,128)(2,1)S(1)}, bf16[4,4,2,8,256]{4,3,2,1,0:T(8,128)(2,1)S(1)}, u32[]{:S(2)}, u32[]{:S(2)}) collective-permute-start(bf16[4,4,2,8,256]{4,3,2,1,0:T(8,128)(2,1)S(1)} %bitcast.20), channel_id=1, source_target_pairs={{0,1},{1,0},{2,3},{3,2},{4,5},{5,4},{6,7},{7,6},{8,9},{9,8},{10,11... | collective-permute-start | bytes 393224 | tf_op jit(solution)/shard_map/ppermute | solution.py:320
  36.5 4.2 %collective-permute-start.7 = (bf16[4,4,2,8,256]{4,3,2,1,0:T(8,128)(2,1)S(1)}, bf16[4,4,2,8,256]{4,3,2,1,0:T(8,128)(2,1)S(1)}, u32[]{:S(2)}, u32[]{:S(2)}) collective-permute-start(bf16[4,4,2,8,256]{4,3,2,1,0:T(8,128)(2,1)S(1)} %collective-permute-done.3.rest_1_), channel_id=1, source_target_pairs={{0,1},{1,0},{2,3},{3,2},{4,5},{5,4},{6,7},{7,6},{8,9},{9,8},{10,11... | collective-permute-start | bytes 393224 | tf_op jit(solution)/shard_map/ppermute | solution.py:320
  36.5 4.2 %collective-permute-start.8 = (bf16[4,4,2,8,256]{4,3,2,1,0:T(8,128)(2,1)S(1)}, bf16[4,4,2,8,256]{4,3,2,1,0:T(8,128)(2,1)S(1)}, u32[]{:S(2)}, u32[]{:S(2)}) collective-permute-start(bf16[4,4,2,8,256]{4,3,2,1,0:T(8,128)(2,1)S(1)} %collective-permute-done.4.rest_2_), channel_id=1, source_target_pairs={{0,1},{1,0},{2,3},{3,2},{4,5},{5,4},{6,7},{7,6},{8,9},{9,8},{10,11... | collective-permute-start | bytes 393224 | tf_op jit(solution)/shard_map/ppermute | solution.py:320
  37.0 3.7 %collective-permute-start.9 = (bf16[4,4,2,8,256]{4,3,2,1,0:T(8,128)(2,1)S(1)}, bf16[4,4,2,8,256]{4,3,2,1,0:T(8,128)(2,1)S(1)}, u32[]{:S(2)}, u32[]{:S(2)}) collective-permute-start(bf16[4,4,2,8,256]{4,3,2,1,0:T(8,128)(2,1)S(1)} %collective-permute-done.5.rest_3_), channel_id=1, source_target_pairs={{0,1},{1,0},{2,3},{3,2},{4,5},{5,4},{6,7},{7,6},{8,9},{9,8},{10,11... | collective-permute-start | bytes 393224 | tf_op jit(solution)/shard_map/ppermute | solution.py:320
  37.1 3.6 %collective-permute-start.2 = (bf16[144,384]{1,0:T(8,128)(2,1)S(1)}, bf16[144,384]{1,0:T(8,128)(2,1)S(1)}, u32[]{:S(2)}, u32[]{:S(2)}) collective-permute-start(bf16[144,384]{1,0:T(8,128)(2,1)S(1)} %get-tuple-element.43), channel_id=1, source_target_pairs={{0,12},{4,0},{8,4},{12,8},{1,13},{5,1},{9,5},{13,9},{2,14},{6,2},{... | collective-permute-start | bytes 331784 | tf_op jit(solution)/shard_map/ppermute | solution.py:320
  49.0 5.0 %collective-permute-start.10 = (f32[4,8,128]{2,1,0:T(8,128)S(1)}, f32[4,8,128]{2,1,0:T(8,128)S(1)}, u32[]{:S(2)}, u32[]{:S(2)}) collective-permute-start(f32[4,8,128]{2,1,0:T(8,128)S(1)} %get-tuple-element.45.l0), channel_id=1, source_target_pairs={{0,4},{4,8},{8,12},{12,0},{1,5},{5,9},{9,13},{13,1},{2,6},{6,10},{... | collective-permute-start | bytes 49160 | tf_op jit(solution)/shard_map/ppermute | solution.py:320
  49.1 4.9 %collective-permute-start.11 = (f32[4,8,128]{2,1,0:T(8,128)S(1)}, f32[4,8,128]{2,1,0:T(8,128)S(1)}, u32[]{:S(2)}, u32[]{:S(2)}) collective-permute-start(f32[4,8,128]{2,1,0:T(8,128)S(1)} %get-tuple-element.45.l0), channel_id=1, source_target_pairs={{0,8},{4,12},{8,0},{12,4},{1,9},{5,13},{9,1},{13,5},{2,10},{6,14},... | collective-permute-start | bytes 49160 | tf_op jit(solution)/shard_map/ppermute | solution.py:320
  52.0 2.6 %collective-permute-start.12 = (f32[4,8,128]{2,1,0:T(8,128)S(1)}, f32[4,8,128]{2,1,0:T(8,128)S(1)}, u32[]{:S(2)}, u32[]{:S(2)}) collective-permute-start(f32[4,8,128]{2,1,0:T(8,128)S(1)} %get-tuple-element.45.l0), channel_id=1, source_target_pairs={{0,12},{4,0},{8,4},{12,8},{1,13},{5,1},{9,5},{13,9},{2,14},{6,2},{... | collective-permute-start | bytes 49160 | tf_op jit(solution)/shard_map/ppermute | solution.py:320
  57.4 6.6 %collective-permute-start.13 = (bf16[129,8,256]{2,1,0:T(8,128)(2,1)S(1)}, bf16[129,8,256]{2,1,0:T(8,128)(2,1)S(1)}, u32[]{:S(2)}, u32[]{:S(2)}) collective-permute-start(bf16[129,8,256]{2,1,0:T(8,128)(2,1)S(1)} %get-tuple-element.56), channel_id=1, source_target_pairs={{0,1},{1,0},{2,3},{3,2},{4,5},{5,4},{6,7},{7,6},{8,9},{9,8},{10,11... | collective-permute-start | bytes 1585160 | tf_op jit(solution)/shard_map/ppermute | solution.py:320
  64.2 4.8 %collective-permute-start.14 = (bf16[32,8,256]{2,1,0:T(8,128)(2,1)S(1)}, bf16[32,8,256]{2,1,0:T(8,128)(2,1)S(1)}, u32[]{:S(2)}, u32[]{:S(2)}) collective-permute-start(bf16[32,8,256]{2,1,0:T(8,128)(2,1)S(1)} %get-tuple-element.58), channel_id=1, source_target_pairs={{0,48},{16,0},{32,16},{48,32},{1,49},{17,1},{33,17},{49,33},{2,50}... | collective-permute-start | bytes 393224 | tf_op jit(solution)/shard_map/ppermute | solution.py:320
  64.3 6.3 %collective-permute-start.15 = (bf16[32,8,256]{2,1,0:T(8,128)(2,1)S(1)}, bf16[32,8,256]{2,1,0:T(8,128)(2,1)S(1)}, u32[]{:S(2)}, u32[]{:S(2)}) collective-permute-start(bf16[32,8,256]{2,1,0:T(8,128)(2,1)S(1)} %get-tuple-element.59), channel_id=1, source_target_pairs={{0,32},{16,48},{32,0},{48,16},{1,33},{17,49},{33,1},{49,17},{2,34}... | collective-permute-start | bytes 393224 | tf_op jit(solution)/shard_map/ppermute | solution.py:320
  66.3 7.3 %collective-permute-start.16 = (bf16[32,8,256]{2,1,0:T(8,128)(2,1)S(1)}, bf16[32,8,256]{2,1,0:T(8,128)(2,1)S(1)}, u32[]{:S(2)}, u32[]{:S(2)}) collective-permute-start(bf16[32,8,256]{2,1,0:T(8,128)(2,1)S(1)} %get-tuple-element.60), channel_id=1, source_target_pairs={{0,16},{16,32},{32,48},{48,0},{1,17},{17,33},{33,49},{49,1},{2,18}... | collective-permute-start | bytes 393224 | tf_op jit(solution)/shard_map/ppermute | solution.py:320
  74.4 15.9 %all-to-all-start.1 = ((bf16[32,8,384]{2,1,0:T(8,128)(2,1)}), bf16[32,8,384]{2,1,0:T(8,128)(2,1)S(1)}, u32[]{:S(2)}, u32[]{:S(2)}) async-start(bf16[32,8,384]{2,1,0:T(8,128)(2,1)} %bitcast.9), calls=%async_computation.1 | async-start | bytes 393216 | tf_op jit(solution)/shard_map/all_to_all | solution.py:414
  78.3 5.6 %collective-permute-start.17 = (bf16[128,384]{1,0:T(8,128)(2,1)S(1)}, bf16[128,384]{1,0:T(8,128)(2,1)S(1)}, u32[]{:S(2)}, u32[]{:S(2)}) collective-permute-start(bf16[128,384]{1,0:T(8,128)(2,1)S(1)} %get-tuple-element.63), channel_id=1, source_target_pairs={{0,12},{4,0},{8,4},{12,8},{1,13},{5,1},{9,5},{13,9},{2,14},{6,2},{... | collective-permute-start | bytes 294920 | tf_op jit(solution)/shard_map/ppermute | solution.py:320
  80.8 6.0 %collective-permute-start.18 = (bf16[128,384]{1,0:T(8,128)(2,1)S(1)}, bf16[128,384]{1,0:T(8,128)(2,1)S(1)}, u32[]{:S(2)}, u32[]{:S(2)}) collective-permute-start(bf16[128,384]{1,0:T(8,128)(2,1)S(1)} %get-tuple-element.64), channel_id=1, source_target_pairs={{0,8},{4,12},{8,0},{12,4},{1,9},{5,13},{9,1},{13,5},{2,10},{6,14},... | collective-permute-start | bytes 294920 | tf_op jit(solution)/shard_map/ppermute | solution.py:320
  81.4 8.9 %collective-permute-start.19 = (bf16[128,384]{1,0:T(8,128)(2,1)S(1)}, bf16[128,384]{1,0:T(8,128)(2,1)S(1)}, u32[]{:S(2)}, u32[]{:S(2)}) collective-permute-start(bf16[128,384]{1,0:T(8,128)(2,1)S(1)} %get-tuple-element.65), channel_id=1, source_target_pairs={{0,4},{4,8},{8,12},{12,0},{1,5},{5,9},{9,13},{13,1},{2,6},{6,10},{... | collective-permute-start | bytes 294920 | tf_op jit(solution)/shard_map/ppermute | solution.py:320
where the time goes:
time: 91.7 us; the launch traced here: 91.4 us
  starting transfers between devices  30 us (33%)
  waiting for transfers between devices  23.3 us (25%)
  blocking collectives  21 us (23%)
  Pallas kernels  16.2 us (18%)
  between operations  0.92 us (1%)
    ppermute x20, starting transfers between devices, shift(): return lax.ppermute(v, axis, [(i, (i + k) % size) for i in range(size)])  26.1 us
    ppermute x20, waiting for transfers between devices, shift(): return lax.ppermute(v, axis, [(i, (i + k) % size) for i in range(size)])  23.3 us
    all_to_all x1, blocking collectives, per_device(): lax.all_to_all(copies.reshape(32, 8, 256), YZ_AXES, 0, 0, tiled=True)  21 us
    pallas_call x1, Pallas kernels, per_device(): call(forward_kernel, [like((4, 8, BLOCK), F32), like((7 * CHUNK, WIDE), B...  8.29 us
    all_to_all x1, starting transfers between devices, per_device(): lax.all_to_all(by_z.reshape(32, 8, WIDE), YZ_AXES, 0, 0, tiled=True)  3.87 us
    pallas_call x1, Pallas kernels, per_device(): call(backward_kernel, [like((BLOCK, WIDE), BF16)] * 4 + [like((129, 8, 25...  2.82 us
    pallas_call x1, Pallas kernels, per_device(): call(middle_kernel, [like((7 * CHUNK, WIDE), BF16), like((4, HEAD_WIDTH,...  2 us
  transfers between devices with their start and end apart: 21, of which 10 were waited for; matrix products, arithmetic and copies ran while one was open for 0% of the time, Pallas kernels for 2%

commit v1 on v0

v1 whole, which is shorter than its diff:
```python
import jax
import jax.numpy as jnp
from jax import lax
from jax.experimental import pallas as pl
from jax.experimental.pallas import tpu as pltpu
from jax.sharding import Mesh, PartitionSpec as P

HEAD_WIDTH = 128
GROUP = 3
WIDE = GROUP * HEAD_WIDTH
BLOCK = 128
CHUNK = 512
TOKENS = 2048
SCALE = HEAD_WIDTH ** -0.5
LOG2E = 1.4426950408889634
NEG = -1.0e30
F32 = jnp.float32
BF16 = jnp.bfloat16
CHUNKS = ((0,), (0, 1), (0, 1, 2), (3,))
P_AT = (0, 1, 3, 6)
YZ_AXES = ("y", "zh", "zl")


VMEM = pl.BlockSpec(memory_space=pltpu.VMEM)
HBM = pl.BlockSpec(memory_space=pltpu.HBM)
SMEM = pl.BlockSpec(memory_space=pltpu.SMEM)


def coords(did_ref):
    d = did_ref[0]
    return d // 64, (d // 16) % 4, (d // 4) % 4, (d // 2) % 2, d % 2


def keys_kernel(keys, values, kv_out, kb, vb, sems):
    copies = [pltpu.make_async_copy(keys, kb, sems.at[0]), pltpu.make_async_copy(values, vb, sems.at[1])]
    for copy in copies:
        copy.start()
    for copy in copies:
        copy.wait()
    for g in range(4):
        cols = slice(g * HEAD_WIDTH, (g + 1) * HEAD_WIDTH)
        both = jnp.concatenate([kb[:, cols], vb[:, cols]], axis=1)
        for z in range(8):
            kv_out[g, z] = both


def queries_kernel(did, labels, mask, queries, w, seg, q0, q1, q2, q3, w_out, seg_out, lb, mb, sems):
    _, _, y, _, _ = coords(did)
    outs = (q0, q1, q2, q3)
    early = [pltpu.make_async_copy(labels, lb, sems.at[0]), pltpu.make_async_copy(mask, mb, sems.at[1])]
    late = [pltpu.make_async_copy(w, w_out, sems.at[2]), pltpu.make_async_copy(seg, seg_out, sems.at[3])]
    for k in range(4):
        g = pl.multiple_of(((y + k) % 4) * WIDE, HEAD_WIDTH)
        late.append(pltpu.make_async_copy(queries.at[:, pl.ds(g, WIDE)], outs[k].at[pl.ds(0, BLOCK)], sems.at[4 + k]))
    for copy in early + late:
        copy.start()
    for copy in early:
        copy.wait()
    lab = jnp.broadcast_to(lb[...].astype(F32), (16, BLOCK))
    msk = jnp.broadcast_to(mb[...].astype(F32), (16, BLOCK))
    tail = jnp.concatenate([lab, msk, lab], axis=1).astype(BF16)
    for k in range(4):
        outs[k][BLOCK:, :] = tail
    for copy in late:
        copy.wait()


def head_diff(w, y, h):
    at = pl.multiple_of(y * WIDE + h * HEAD_WIDTH, HEAD_WIDTH)
    return w[0:1, pl.ds(at, HEAD_WIDTH)] - w[1:2, pl.ds(at, HEAD_WIDTH)]


def halves(v):
    high = v.astype(BF16).astype(F32)
    return high, v - high


def stack8(rows):
    at = lax.broadcasted_iota(jnp.int32, (8, rows[0].shape[1]), 0)
    out = jnp.zeros((8, rows[0].shape[1]), F32)
    for r, row in enumerate(rows):
        out = jnp.where(at == r, row, out)
    return out


def on_both(v):
    high, low = halves(v)
    return jnp.concatenate([high, low], axis=0).astype(BF16)


NT = (((1,), (1,)), ((), ()))


def times_t(a, b):
    return lax.dot_general(a, b, NT, preferred_element_type=F32)


def forward_kernel(did, seg, w, q0, q1, q2, q3, *rest):
    kvs = rest[:8]
    plog, p_out, inv_out, delta_out, q_out, kv_out = rest[8:14]
    s_buf, u_rows = rest[14:]
    _, x, y, zh, c = coords(did)
    for cc in range(2):
        for kx in range(4):
            for ys in range(4):
                for z in range(2):
                    row = ys * CHUNK + cc * 256 + z * BLOCK + kx * 32
                    kv_out[row : row + 32, :] = kvs[cc * 4 + kx][ys, z]
    for k, ref in enumerate((q0, q1, q2, q3)):
        slot = (y - k + 4) % 4
        for h in range(GROUP):
            q_out[slot, h * BLOCK : (h + 1) * BLOCK, :] = ref[:BLOCK, h * HEAD_WIDTH : (h + 1) * HEAD_WIDTH]
    diffs16 = on_both(stack8([head_diff(w, y, h) for h in range(GROUP)]))
    ones = stack8([jnp.zeros((1, CHUNK), F32)] * GROUP + [jnp.ones((1, CHUNK), F32)])
    for ch in range(4):
        rows = slice(ch * CHUNK, (ch + 1) * CHUNK)
        part = times_t(diffs16, kv_out[rows, HEAD_WIDTH:])
        high, low = halves(part[:8] + part[8:])
        u_rows[:, rows] = jnp.concatenate([high + ones, low], axis=0).astype(BF16)
    j = zh * 2 + c
    r = lax.broadcasted_iota(jnp.int32, (BLOCK, BLOCK), 0)
    from_x = jnp.bitwise_and(x + 4 - jnp.right_shift(r, 5), 3)
    inner = jnp.bitwise_and(jnp.right_shift(r, 3), 3) * 32 + from_x * 8 + jnp.bitwise_and(r, 7)
    query_at = lax.broadcasted_iota(jnp.int32, (BLOCK, BLOCK), 1) + j * BLOCK
    last = seg[:, pl.ds(pl.multiple_of(3 * CHUNK + j * BLOCK, BLOCK), BLOCK)]
    start = jnp.zeros((1, BLOCK), F32)
    for b in range(4):
        row = 3 * CHUNK + b * BLOCK
        ids = jnp.broadcast_to(seg[:, row : row + BLOCK], (BLOCK, BLOCK)).T
        start = start + jnp.sum(jnp.where(ids < last, 1.0, 0.0), axis=0, keepdims=True)
    start = start.astype(jnp.int32)
    for ys in range(4):
        top = jnp.full((1, WIDE), NEG, F32)
        for i, ch in enumerate(CHUNKS[ys]):
            for b in range(CHUNK // BLOCK):
                row = ch * CHUNK + b * BLOCK
                s = times_t(kv_out[row : row + BLOCK, :HEAD_WIDTH], q_out[ys])
                if ch == ys:
                    key_at = inner + ((b % 2) * 256 + ((c + b // 2) % 2) * BLOCK)
                    ok = key_at <= query_at
                    if ys == 3:
                        ok = ok & (key_at >= start)
                    s = jnp.where(jnp.concatenate([ok] * GROUP, axis=1), s, NEG)
                top = jnp.maximum(top, jnp.max(s, axis=0, keepdims=True))
                at = i * CHUNK + b * BLOCK
                s_buf[at : at + BLOCK, :] = s
        sums = jnp.zeros((16, WIDE), F32)
        for i, ch in enumerate(CHUNKS[ys]):
            at_p = (P_AT[ys] + i) * CHUNK
            for b in range(CHUNK // BLOCK):
                at = i * CHUNK + b * BLOCK
                p = jnp.exp2((s_buf[at : at + BLOCK, :] - top) * (SCALE * LOG2E))
                p_out[at_p + b * BLOCK : at_p + (b + 1) * BLOCK, :] = p.astype(BF16)
            sums = sums + jnp.dot(
                u_rows[:, ch * CHUNK : (ch + 1) * CHUNK], p_out[at_p : at_p + CHUNK, :], preferred_element_type=F32
            )
        inv = 1.0 / sums[GROUP : GROUP + 1, :]
        both = (sums[:8] + sums[8:]) * inv
        delta = jnp.concatenate([both[h : h + 1, h * BLOCK : (h + 1) * BLOCK] for h in range(GROUP)], axis=1)
        inv_out[ys] = jnp.broadcast_to(inv, (8, WIDE))
        delta_out[ys] = jnp.broadcast_to(delta, (8, WIDE))
        lg = delta[:, :BLOCK] + delta[:, BLOCK : 2 * BLOCK] + delta[:, 2 * BLOCK :]
        plog[(y - ys + 4) % 4] = jnp.broadcast_to(lg, (8, BLOCK))


def middle_kernel(did, w, p, delta, q, kv, g_out, dq_out, qt_out, kt, u):
    _, _, y, _, _ = coords(did)
    eye = jnp.where(
        lax.broadcasted_iota(jnp.int32, (BLOCK, BLOCK), 0) == lax.broadcasted_iota(jnp.int32, (BLOCK, BLOCK), 1), 1.0, 0.0
    ).astype(BF16)
    pad = jnp.zeros((BLOCK - 8, HEAD_WIDTH), F32)
    high, low = halves(jnp.concatenate([stack8([head_diff(w, y, h) for h in range(GROUP)]), pad], axis=0))
    high, low = high.astype(BF16), low.astype(BF16)
    for ch in range(4):
        rows = slice(ch * CHUNK, (ch + 1) * CHUNK)
        kt[:, rows] = times_t(eye, kv[rows, :HEAD_WIDTH]).astype(BF16)
        u[rows, :] = times_t(kv[rows, HEAD_WIDTH:], high) + times_t(kv[rows, HEAD_WIDTH:], low)
    for ys in range(4):
        qt_out[ys] = times_t(eye, q[ys]).astype(BF16)
        dqt = jnp.zeros((HEAD_WIDTH, WIDE), F32)
        for i, ch in enumerate(CHUNKS[ys]):
            at_p = (P_AT[ys] + i) * CHUNK
            for b in range(CHUNK // BLOCK):
                row = ch * CHUNK + b * BLOCK
                at = slice(at_p + b * BLOCK, at_p + (b + 1) * BLOCK)
                ub = jnp.concatenate(
                    [jnp.broadcast_to(u[row : row + BLOCK, h : h + 1], (BLOCK, BLOCK)) for h in range(GROUP)], axis=1
                )
                g_out[at, :] = (p[at, :].astype(F32) * (ub - delta[ys, 0:1, :])).astype(BF16)
            dqt = dqt + jnp.dot(
                kt[:, ch * CHUNK : (ch + 1) * CHUNK], g_out[at_p : at_p + CHUNK, :], preferred_element_type=F32
            )
        dq_out[ys] = dqt


def key_terms(out, half, p, g, qf, at16):
    for ch in range(4):
        dk = jnp.zeros((256, HEAD_WIDTH), F32)
        dv = jnp.zeros((256, HEAD_WIDTH), F32)
        for ys in range(4):
            if ch in CHUNKS[ys]:
                at = (P_AT[ys] + CHUNKS[ys].index(ch)) * CHUNK + half * 256
                dk = dk + times_t(g[at : at + 256, :], qf[ys])
                dv = dv + times_t(p[at : at + 256, :], at16[ys])
        both = jnp.concatenate([dk, dv], axis=1).astype(BF16)
        for z in range(2):
            for kx in range(4):
                row = z * BLOCK + kx * 32
                out[kx, ch, z] = both[row : row + 32]


def far_kernel(did, w, l0, l1, l2, l3, g0, g1, g2, g3, p, g, inv, qt, out, f_out, qf, at16, loss_out, lgs, labs):
    _, _, y, _, _ = coords(did)
    for k, ref in enumerate((l0, l1, l2, l3)):
        src = (y - k + 4) % 4
        for m in range(4):
            ys = (y - m + 4) % 4
            lgs[src, ys] = ref[(m - k) % 4]
    for k, ref in enumerate((g0, g1, g2, g3)):
        labs[(y - k + 4) % 4] = ref[BLOCK:, :256].astype(F32)[8:16, :]
    wt = jnp.concatenate([jnp.broadcast_to(head_diff(w, y, h), (BLOCK, HEAD_WIDTH)).T for h in range(GROUP)], axis=1)
    loss = jnp.zeros((1, BLOCK), F32)
    for ys in range(4):
        z = (lgs[0, ys] + lgs[1, ys] + lgs[2, ys] + lgs[3, ys])[0:1, :]
        one = labs[ys, 0:1, :BLOCK] > 0.5
        mask = labs[ys, 0:1, BLOCK:]
        a = jnp.where(one, z, -z)
        e = jnp.exp(-jnp.abs(a))
        loss = loss + mask * (jnp.maximum(a, 0.0) + jnp.log(1.0 + e))
        sig = jnp.where(a >= 0.0, 1.0, e) / (1.0 + e)
        d0 = mask * jnp.where(one, sig, -sig)
        f = jnp.concatenate([d0] * GROUP, axis=1) * inv[ys, 0:1, :]
        f_out[ys] = jnp.broadcast_to(f, (8, WIDE))
        at16[ys] = (wt * f).astype(BF16)
        qf[ys] = (qt[ys].astype(F32) * (f * SCALE)).astype(BF16)
    loss_out[...] = jnp.broadcast_to(loss, (8, BLOCK))
    key_terms(out, 1, p, g, qf, at16)


def own_kernel(did, p, g, qf, at16, f, loss, kv, dqt, out, hg_out, d0, d1, d2, d3, dqb, ct):
    _, _, y, _, _ = coords(did)
    key_terms(out, 0, p, g, qf, at16)
    head_of = lax.broadcasted_iota(jnp.int32, (8, WIDE), 1) // BLOCK
    head_at = lax.broadcasted_iota(jnp.int32, (8, WIDE), 0)
    seen = set()
    for ys in range(4):
        fm = on_both(jnp.where(head_of == head_at, f[ys, 0:1, :], 0.0))
        for i, ch in enumerate(CHUNKS[ys]):
            at = (P_AT[ys] + i) * CHUNK
            rows = slice(ch * CHUNK, (ch + 1) * CHUNK)
            cs = times_t(fm, p[at : at + CHUNK, :])
            cs = cs[:8] + cs[8:]
            ct[:, rows] = ct[:, rows] + cs if ch in seen else cs
            seen.add(ch)
        dqs = dqt[ys] * (f[ys, 0:1, :] * SCALE)
        slot = (y - ys + 4) % 4
        for h in range(GROUP):
            cols = slice(h * BLOCK, (h + 1) * BLOCK)
            dqb[slot, :, cols] = dqs[:, cols].T.astype(BF16)
    for k, ref in enumerate((d0, d1, d2, d3)):
        ref[...] = dqb[k]
    hg = jnp.dot(on_both(ct[...]), kv[:, HEAD_WIDTH:], preferred_element_type=F32)
    row8 = lax.broadcasted_iota(jnp.int32, (8, BLOCK), 0)
    hg_out[...] = jnp.where(row8 == GROUP, loss[...], hg[:8] + hg[8:])


def core_kernel(own, far, b0, b1, b2, b3):
    for kx, out in enumerate((b0, b1, b2, b3)):

        def add(ys, carry, kx=kx, out=out):
            out[ys] = (own[kx, ys].astype(F32) + far[kx, ys].astype(F32)).astype(BF16)
            return carry

        lax.fori_loop(0, 4, add, 0)


def x_kernel(b0, b1, b2, b3, hg, hg_far, out):
    high, low = halves(hg[...] + hg_far[...])
    tail = jnp.concatenate([high[:4], low[:4]], axis=0).astype(BF16)
    tail = jnp.broadcast_to(tail[None, None], (2, 4, 8, BLOCK))

    def add(ys, carry):
        v = b0[ys].astype(F32) + b1[ys].astype(F32) + b2[ys].astype(F32) + b3[ys].astype(F32)
        out[ys, :, :, :, :256] = v.reshape(2, 4, 8, 256).astype(BF16)
        out[ys, :, :, :, 256:] = tail
        return carry

    lax.fori_loop(0, 4, add, 0)


def finish_kernel(did, pieces, d0, d1, d2, d3, qg, gk, gv, hg, loss):
    zl, _, y, _, _ = coords(did)
    for g in range(4):
        v = jnp.zeros((8, 256), F32)
        for k in range(2):
            for z in range(4):
                v = v + pieces[g, k, z, :, :256].astype(F32)
        gk[:, g * HEAD_WIDTH : (g + 1) * HEAD_WIDTH] = v[:, :HEAD_WIDTH]
        gv[:, g * HEAD_WIDTH : (g + 1) * HEAD_WIDTH] = v[:, HEAD_WIDTH:]
        v = pieces[g, 0, zl, :, 256:].astype(F32)
        t = pieces[g, 1, zl, :, 256:].astype(F32)
        v = (v[:4] + v[4:]) + (t[:4] + t[4:])
        for h in range(GROUP):
            cols = slice(g * WIDE + h * HEAD_WIDTH, g * WIDE + (h + 1) * HEAD_WIDTH)
            hg[0:1, cols] = v[h : h + 1]
            hg[1:2, cols] = -v[h : h + 1]
        if g == 0:
            loss[0] = jnp.sum(v[GROUP : GROUP + 1]) * (1.0 / TOKENS)
    for k, d in enumerate((d0, d1, d2, d3)):
        wide = pl.ds(pl.multiple_of(((y + k) % 4) * WIDE, HEAD_WIDTH), WIDE)
        qg[:, wide] = d[...].astype(F32)


def shift(v, axis, size, k):
    return lax.ppermute(v, axis, [(i, (i + k) % size) for i in range(size)])


def like(shape, dtype):
    return jax.ShapeDtypeStruct(shape, dtype)


def in_hbm(v):
    return pltpu.with_memory_space_constraint(v, pltpu.HBM)


def call(kernel, out_shape, specs, out_specs=None, scratch=()):
    return pl.pallas_call(
        kernel,
        out_shape=out_shape,
        in_specs=specs,
        out_specs=out_specs or [VMEM] * len(out_shape),
        scratch_shapes=list(scratch),
        compiler_params=pltpu.CompilerParams(vmem_limit_bytes=20 << 20),
    )


def per_device(queries, keys, values, head, segments, label_mask, labels):
    did = lax.axis_index(("zl", "x", "y", "zh", "c")).astype(jnp.int32).reshape(1)
    (copies,) = call(
        keys_kernel,
        [like((4, 8, 8, 256), BF16)],
        [HBM] * 2,
        scratch=[pltpu.VMEM((8, 512), BF16), pltpu.VMEM((8, 512), BF16), pltpu.SemaphoreType.DMA((2,))],
    )(in_hbm(keys), in_hbm(values))
    own = lax.all_to_all(copies.reshape(32, 8, 256), YZ_AXES, 0, 0, tiled=True).reshape(4, 2, 32, 256)
    *packs, w, seg = call(
        queries_kernel,
        [like((BLOCK + 16, WIDE), BF16)] * 4 + [like((2, 4 * WIDE), F32), like((1, TOKENS), jnp.int32)],
        [SMEM] + [HBM] * 5,
        scratch=[
            pltpu.VMEM((1, BLOCK), jnp.int32),
            pltpu.VMEM((1, BLOCK), jnp.int32),
            pltpu.SemaphoreType.DMA((8,)),
        ],
    )(
        did,
        in_hbm(labels.reshape(1, BLOCK)),
        in_hbm(label_mask.reshape(1, BLOCK)),
        in_hbm(queries[0]),
        in_hbm(head[0].T),
        in_hbm(segments.reshape(1, TOKENS)),
    )
    over_x = [own]
    for k in range(1, 4):
        over_x.append(shift(own, "x", 4, k))
    over_c = [shift(a, "c", 2, 1) for a in over_x]
    for k in range(1, 4):
        packs[k] = shift(packs[k], "y", 4, k)
    plog, p, inv, delta, q, kv = call(
        forward_kernel,
        [
            like((4, 8, BLOCK), F32),
            like((7 * CHUNK, WIDE), BF16),
            like((4, 8, WIDE), F32),
            like((4, 8, WIDE), F32),
            like((4, WIDE, HEAD_WIDTH), BF16),
            like((TOKENS, 256), BF16),
        ],
        [SMEM] + [VMEM] * 14,
        scratch=[pltpu.VMEM((3 * CHUNK, WIDE), F32), pltpu.VMEM((16, TOKENS), BF16)],
    )(did, seg, w, *packs, *over_x, *over_c)
    logs = [plog] + [shift(plog, "y", 4, k) for k in range(1, 4)]
    g, dqt, qt = call(
        middle_kernel,
        [
            like((7 * CHUNK, WIDE), BF16),
            like((4, HEAD_WIDTH, WIDE), F32),
            like((4, HEAD_WIDTH, WIDE), BF16),
        ],
        [SMEM] + [VMEM] * 5,
        scratch=[pltpu.VMEM((HEAD_WIDTH, TOKENS), BF16), pltpu.VMEM((TOKENS, BLOCK), F32)],
    )(did, w, p, delta, q, kv)
    far_d, f, qf, at16, loss_rows = call(
        far_kernel,
        [
            like((4, 4, 2, 32, 256), BF16),
            like((4, 8, WIDE), F32),
            like((4, HEAD_WIDTH, WIDE), BF16),
            like((4, HEAD_WIDTH, WIDE), BF16),
            like((8, BLOCK), F32),
        ],
        [SMEM] + [VMEM] * 13,
        scratch=[pltpu.VMEM((4, 4, 8, BLOCK), F32), pltpu.VMEM((4, 8, 256), F32)],
    )(did, w, *logs, *packs, p, g, inv, qt)
    far = shift(far_d, "c", 2, 1)
    own_d, hg, *dq = call(
        own_kernel,
        [like((4, 4, 2, 32, 256), BF16), like((8, BLOCK), F32)] + [like((BLOCK, WIDE), BF16)] * 4,
        [SMEM] + [VMEM] * 8,
        scratch=[pltpu.VMEM((4, BLOCK, WIDE), BF16), pltpu.VMEM((8, TOKENS), F32)],
    )(did, p, g, qf, at16, f, loss_rows, kv, dqt)
    by_x = call(core_kernel, [like((4, 2, 32, 256), BF16)] * 4, [VMEM] * 2)(own_d, far)
    got = [by_x[0]] + [shift(by_x[k], "x", 4, -k) for k in range(1, 4)]
    hg_far = shift(hg, "c", 2, 1)
    (by_z,) = call(x_kernel, [like((4, 2, 4, 8, WIDE), BF16)], [VMEM] * 6)(*got, hg, hg_far)
    pieces = lax.all_to_all(by_z.reshape(32, 8, WIDE), YZ_AXES, 0, 0, tiled=True).reshape(4, 2, 4, 8, WIDE)
    back = [dq[0]]
    for k in range(1, 4):
        back.append(shift(dq[k], "y", 4, -k))
    query_gradient, grad_keys, grad_values, head_t, loss = call(
        finish_kernel,
        [
            like((BLOCK, 4 * WIDE), F32),
            like((8, 512), F32),
            like((8, 512), F32),
            like((2, 4 * WIDE), F32),
            like((1,), F32),
        ],
        [SMEM] + [VMEM] * 5,
        [VMEM] * 4 + [SMEM],
    )(did, pieces, *back)
    return loss, query_gradient[None], grad_keys, grad_values, head_t.T[None]


def solution(mesh):
    fine = Mesh(mesh.devices.reshape(4, 4, 4, 2, 2), ("zl", "x", "y", "zh", "c"))
    layer, ctx = ("zl", "x"), ("y", "zh", "c")
    return jax.shard_map(
        per_device,
        mesh=fine,
        in_specs=(
            P(layer, ctx, None),
            P(ctx + layer, None),
            P(ctx + layer, None),
            P(layer, None, None),
            P(),
            P(ctx),
            P(ctx),
        ),
        out_specs=(
            P(layer),
            P(layer, ctx, None),
            P(ctx + layer, None),
            P(ctx + layer, None),
            P(layer, None, None),
        ),
        check_vma=False,
    )
```

time: 91.7 us -> 87.7 us (0.956)
  Pallas kernels: 16.2 us -> 12 us
  waiting for transfers between devices: 23.3 us -> 25.9 us
  starting transfers between devices: 30 us -> 27.5 us
    pallas_call x1, Pallas kernels: 8.29 us -> 3.11 us  [per_device(): call(forward_kernel, [like((4, 8, BLOCK), F32), like((7 * CHUNK, WIDE), B...]
    ppermute x20 -> x21, starting transfers between devices: 26.1 us -> 23.3 us  [shift(): return lax.ppermute(v, axis, [(i, (i + k) % size) for i in range(size)])]
    ppermute x20 -> x21, waiting for transfers between devices: 23.3 us -> 25.9 us  [shift(): return lax.ppermute(v, axis, [(i, (i + k) % size) for i in range(size)])]
    pallas_call x4 -> x6, Pallas kernels: 4.94 us -> 5.62 us  [the longest x1 1.74 us: per_device(): call(own_kernel, [like((4, 4, 2, 32, 256), BF16), like((8, BLOCK), F32)]...]
  transfers between devices with their start and end apart: 21 -> 22, of which waited for: 10 -> 11; matrix products, arithmetic and copies ran while one was open for 0% -> 0% of each run, Pallas kernels for 2% -> 6%
where the time goes in v1:
time: 87.7 us; the launch traced here: 87.3 us
  starting transfers between devices  27.5 us (31%)
  waiting for transfers between devices  25.9 us (30%)
  blocking collectives  21 us (24%)
  Pallas kernels  12 us (14%)
  between operations  0.89 us (1%)
    ppermute x21, waiting for transfers between devices, shift(): return lax.ppermute(v, axis, [(i, (i + k) % size) for i in range(size)])  25.9 us
    ppermute x21, starting transfers between devices, shift(): return lax.ppermute(v, axis, [(i, (i + k) % size) for i in range(size)])  23.3 us
    all_to_all x1, blocking collectives, per_device(): lax.all_to_all(copies.reshape(32, 8, 256), YZ_AXES, 0, 0, tiled=True)  21 us
    all_to_all x1, starting transfers between devices, per_device(): lax.all_to_all(by_z.reshape(32, 8, WIDE), YZ_AXES, 0, 0, tiled=True)  4.24 us
    pallas_call x1, Pallas kernels, per_device(): call(forward_kernel, [like((4, 8, BLOCK), F32), like((7 * CHUNK, WIDE), B...  3.11 us
    pallas_call x1, Pallas kernels, per_device(): call(middle_kernel, [like((7 * CHUNK, WIDE), BF16), like((4, HEAD_WIDTH,...  2.33 us
  transfers between devices with their start and end apart: 22, of which 11 were waited for; matrix products, arithmetic and copies ran while one was open for 0% of the time, Pallas kernels for 6%

profile of v1, /device:TPU:1, one launch (start us, length us, event | category | flops | bytes accessed | tf_op | source)
XLA Modules:
  0.0 87.3 jit_solution(14758051622791907676)
XLA Ops:
  0.6 0.7 shard_map.111
  1.4 21.0 %all_to_all.10 = bf16[32,8,256]{2,1,0:T(8,128)(2,1)S(1)} all-to-all(bf16[32,8,256]{2,1,0:T(8,128)(2,1)S(1)} %bitcast.17), channel_id=1, replica_groups=mesh['zl'=4,'x'=4,'y'=4,'zh'=2,'c'=2] {'y','zh','zl'}, dimensions={0} | all-to-all | bytes 262144 | tf_op jit(solution)/shard_map/all_to_all | solution.py:345
  22.4 2.5 %collective-permute-start.5 = (bf16[4,2,32,256]{3,2,1,0:T(8,128)(2,1)S(1)}, bf16[4,2,32,256]{3,2,1,0:T(8,128)(2,1)S(1)}, u32[]{:S(2)}, u32[]{:S(2)}) collective-permute-start(bf16[4,2,32,256]{3,2,1,0:T(8,128)(2,1)S(1)} %bitcast.18), channel_id=1, source_target_pairs={{0,48},{16,0},{32,16},{48,32},{1,49},{17,1},{33,17},{49,33},{2,50}... | collective-permute-start | bytes 393224 | tf_op jit(solution)/shard_map/ppermute | solution.py:315
  24.8 0.5 collective-permute-start.4
  25.4 0.6 collective-permute-start.3
  26.0 1.2 %shard_map.110 = (bf16[144,384]{1,0:T(8,128)(2,1)S(1)}, bf16[144,384]{1,0:T(8,128)(2,1)S(1)}, bf16[144,384]{1,0:T(8,128)(2,1)S(1)}, bf16[144,384]{1,0:T(8,128)(2...) custom-call(s32[1]{0:T(128)} %bitcast.did, s32[1,128]{1,0:T(1,128)} %bitcast.26, s32[1,128]{1,0:T(1,128)} %bitcast.27, ...), custom_call_target="tpu_custom_call" | custom-call | tf_op jit(solution)/shard_map/pallas_call | solution.py:346
  27.5 1.7 %collective-permute-start.1 = (bf16[144,384]{1,0:T(8,128)(2,1)S(1)}, bf16[144,384]{1,0:T(8,128)(2,1)S(1)}, u32[]{:S(2)}, u32[]{:S(2)}) collective-permute-start(bf16[144,384]{1,0:T(8,128)(2,1)S(1)} %get-tuple-element.44), channel_id=1, source_target_pairs={{0,8},{4,12},{8,0},{12,4},{1,9},{5,13},{9,1},{13,5},{2,10},{6,14},... | collective-permute-start | bytes 331784 | tf_op jit(solution)/shard_map/ppermute | solution.py:315
  29.3 4.2 %collective-permute-done.q1.g1 = bf16[144,384]{1,0:T(8,128)(2,1)S(1)} collective-permute-done((bf16[144,384]{1,0:T(8,128)(2,1)S(1)}, bf16[144,384]{1,0:T(8,128)(2,1)S(1)}, u32[]{:S(2)}, u32[]{:S(2)}) %collective-permute-start) | collective-permute-done | bytes 110624 | tf_op jit(solution)/shard_map/ppermute | solution.py:315
  33.5 3.8 %collective-permute-start.6 = (bf16[4,2,32,256]{3,2,1,0:T(8,128)(2,1)S(1)}, bf16[4,2,32,256]{3,2,1,0:T(8,128)(2,1)S(1)}, u32[]{:S(2)}, u32[]{:S(2)}) collective-permute-start(bf16[4,2,32,256]{3,2,1,0:T(8,128)(2,1)S(1)} %bitcast.21), channel_id=1, source_target_pairs={{0,1},{1,0},{2,3},{3,2},{4,5},{5,4},{6,7},{7,6},{8,9},{9,8},{10,11... | collective-permute-start | bytes 393224 | tf_op jit(solution)/shard_map/ppermute | solution.py:315
  37.9 4.2 %collective-permute-done.2.q3.g3 = bf16[144,384]{1,0:T(8,128)(2,1)S(1)} collective-permute-done((bf16[144,384]{1,0:T(8,128)(2,1)S(1)}, bf16[144,384]{1,0:T(8,128)(2,1)S(1)}, u32[]{:S(2)}, u32[]{:S(2)}) %collective-permute-start.2) | collective-permute-done | bytes 110624 | tf_op jit(solution)/shard_map/ppermute | solution.py:315
  42.1 3.1 %shard_map.112 = (f32[4,8,128]{2,1,0:T(8,128)S(1)}, bf16[3584,384]{1,0:T(8,128)(2,1)S(1)}, f32[4,8,384]{2,1,0:T(8,128)S(1)}, f32[4,8,384]{2,1,0:T(8,128)S(1)}, b...) custom-call(s32[1]{0:T(128)} %bitcast.did, s32[1,2048]{1,0:T(1,128)S(1)} %get-tuple-element.40.seg, ...), custom_call_target="tpu_custom_call" | custom-call | tf_op jit(solution)/shard_map/pallas_call | solution.py:369
  45.2 0.7 collective-permute-start.12
  46.8 2.3 %shard_map.113 = (bf16[3584,384]{1,0:T(8,128)(2,1)S(1)}, f32[4,128,384]{2,1,0:T(8,128)S(1)}, bf16[4,128,384]{2,1,0:T(8,128)(2,1)S(1)}) custom-call(s32[1]{0:T(128)} %bitcast.did, f32[2,1536]{1,0:T(2,128)S(1)} %get-tuple-element.41.w, bf16[3584,384]{1,0:T(8,128)(2,1)S(1)} %get-tuple-element.46.p, f32[4,8,384]{2,1,0:T(8,128)S(1)} %get-tuple-element.47.delta, ...), custom_call_target="tpu_custom_call" | custom-call | tf_op jit(solution)/shard_map/pallas_call | solution.py:383
  49.1 0.9 %collective-permute-done.11.l2 = f32[4,8,128]{2,1,0:T(8,128)S(1)} collective-permute-done((f32[4,8,128]{2,1,0:T(8,128)S(1)}, f32[4,8,128]{2,1,0:T(8,128)S(1)}, u32[]{:S(2)}, u32[]{:S(2)}) %collective-permute-start.11) | collective-permute-done | bytes 16416 | tf_op jit(solution)/shard_map/ppermute | solution.py:315
  50.3 1.0 %shard_map.114 = (bf16[4,4,2,32,256]{4,3,2,1,0:T(8,128)(2,1)S(1)}, f32[4,8,384]{2,1,0:T(8,128)S(1)}, bf16[4,128,384]{2,1,0:T(8,128)(2,1)S(1)}, bf16[4,128,384]{2,1,0:T(8,128)(2,1)S(1)}, f32[8,128]{1,0:T(8,128)S(1)}) custom-call(s32[1]{0:T(128)} %bitcast.did, f32[2,1536]{1,0:T(2,128)S(1)} %get-tuple-element.41.w, f32[4,8,128]{2,1,0:T(8,128)S(1)} %get-tuple-element.51.l0, ...), custom_call_target="tpu_custom_call" | custom-call | tf_op jit(solution)/shard_map/pallas_call | solution.py:393
  51.3 3.8 %collective-permute-start.13 = (bf16[4,4,2,32,256]{4,3,2,1,0:T(8,128)(2,1)S(1)}, bf16[4,4,2,32,256]{4,3,2,1,0:T(8,128)(2,1)S(1)}, u32[]{:S(2)}, u32[]{:S(2)}) collective-permute-start(bf16[4,4,2,32,256]{4,3,2,1,0:T(8,128)(2,1)S(1)} %get-tuple-element.60), channel_id=1, source_target_pairs={{0,1},{1,0},{2,3},{3,2},{4,5},{5,4},{6,7},{7,6},{8,9},{9,8},{10,11... | collective-permute-start | bytes 1572872 | tf_op jit(solution)/shard_map/ppermute | solution.py:315
  55.1 1.7 %shard_map.115 = (bf16[4,4,2,32,256]{4,3,2,1,0:T(8,128)(2,1)S(1)}, f32[8,128]{1,0:T(8,128)S(1)}, bf16[128,384]{1,0:T(8,128)(2,1)S(1)}, bf16[128,384]{1,0:T(8,128...) custom-call(s32[1]{0:T(128)} %bitcast.did, bf16[3584,384]{1,0:T(8,128)(2,1)S(1)} %get-tuple-element.46.p, ...), custom_call_target="tpu_custom_call" | custom-call | tf_op jit(solution)/shard_map/pallas_call | solution.py:406
  57.1 2.1 %collective-permute-start.14 = (bf16[4,2,32,256]{3,2,1,0:T(8,128)(2,1)S(1)}, bf16[4,2,32,256]{3,2,1,0:T(8,128)(2,1)S(1)}, u32[]{:S(2)}, u32[]{:S(2)}) collective-permute-start(bf16[4,2,32,256]{3,2,1,0:T(8,128)(2,1)S(1)} %get-tuple-element.62), channel_id=1, source_target_pairs={{0,48},{16,0},{32,16},{48,32},{1,49},{17,1},{33,17},{49,33},{2,50}... | collective-permute-start | bytes 393224 | tf_op jit(solution)/shard_map/ppermute | solution.py:315
  59.2 1.2 %collective-permute-start.15 = (bf16[4,2,32,256]{3,2,1,0:T(8,128)(2,1)S(1)}, bf16[4,2,32,256]{3,2,1,0:T(8,128)(2,1)S(1)}, u32[]{:S(2)}, u32[]{:S(2)}) collective-permute-start(bf16[4,2,32,256]{3,2,1,0:T(8,128)(2,1)S(1)} %get-tuple-element.63), channel_id=1, source_target_pairs={{0,32},{16,48},{32,0},{48,16},{1,33},{17,49},{33,1},{49,17},{2,34}... | collective-permute-start | bytes 393224 | tf_op jit(solution)/shard_map/ppermute | solution.py:315
  60.5 0.7 collective-permute-start.17
  61.2 0.8 collective-permute-done.17.hg_far
  62.2 3.2 %collective-permute-done.15.b2 = bf16[4,2,32,256]{3,2,1,0:T(8,128)(2,1)S(1)} collective-permute-done((bf16[4,2,32,256]{3,2,1,0:T(8,128)(2,1)S(1)}, bf16[4,2,32,256]{3,2,1,0:T(8,128)(2,1)S(1)}, u32[]{:S(2)}, u32[]{:S(2)}) %collective-permute-start.15) | collective-permute-done | bytes 131104 | tf_op jit(solution)/shard_map/ppermute | solution.py:315
  65.4 3.6 %collective-permute-done.16.b3 = bf16[4,2,32,256]{3,2,1,0:T(8,128)(2,1)S(1)} collective-permute-done((bf16[4,2,32,256]{3,2,1,0:T(8,128)(2,1)S(1)}, bf16[4,2,32,256]{3,2,1,0:T(8,128)(2,1)S(1)}, u32[]{:S(2)}, u32[]{:S(2)}) %collective-permute-start.16) | collective-permute-done | bytes 131104 | tf_op jit(solution)/shard_map/ppermute | solution.py:315
  69.0 0.8 shard_map.117
  69.7 4.2 %all-to-all-start.1 = ((bf16[32,8,384]{2,1,0:T(8,128)(2,1)}), bf16[32,8,384]{2,1,0:T(8,128)(2,1)S(1)}, u32[]{:S(2)}, u32[]{:S(2)}) async-start(bf16[32,8,384]{2,1,0:T(8,128)(2,1)} %bitcast.9), calls=%async_computation.1 | async-start | bytes 393216 | tf_op jit(solution)/shard_map/all_to_all | solution.py:416
  74.0 2.6 %collective-permute-start.18 = (bf16[128,384]{1,0:T(8,128)(2,1)S(1)}, bf16[128,384]{1,0:T(8,128)(2,1)S(1)}, u32[]{:S(2)}, u32[]{:S(2)}) collective-permute-start(bf16[128,384]{1,0:T(8,128)(2,1)S(1)} %get-tuple-element.67), channel_id=1, source_target_pairs={{0,12},{4,0},{8,4},{12,8},{1,13},{5,1},{9,5},{13,9},{2,14},{6,2},{... | collective-permute-start | bytes 294920 | tf_op jit(solution)/shard_map/ppermute | solution.py:315
  76.5 0.5 collective-permute-start.19
  77.1 0.6 collective-permute-start.20
  77.7 2.0 %collective-permute-done.18.d1 = bf16[128,384]{1,0:T(8,128)(2,1)S(1)} collective-permute-done((bf16[128,384]{1,0:T(8,128)(2,1)S(1)}, bf16[128,384]{1,0:T(8,128)(2,1)S(1)}, u32[]{:S(2)}, u32[]{:S(2)}) %collective-permute-start.18) | collective-permute-done | bytes 98336 | tf_op jit(solution)/shard_map/ppermute | solution.py:315
  79.7 2.7 %collective-permute-done.19.d2 = bf16[128,384]{1,0:T(8,128)(2,1)S(1)} collective-permute-done((bf16[128,384]{1,0:T(8,128)(2,1)S(1)}, bf16[128,384]{1,0:T(8,128)(2,1)S(1)}, u32[]{:S(2)}, u32[]{:S(2)}) %collective-permute-start.19) | collective-permute-done | bytes 98336 | tf_op jit(solution)/shard_map/ppermute | solution.py:315
  82.4 3.8 %collective-permute-done.20.d3 = bf16[128,384]{1,0:T(8,128)(2,1)S(1)} collective-permute-done((bf16[128,384]{1,0:T(8,128)(2,1)S(1)}, bf16[128,384]{1,0:T(8,128)(2,1)S(1)}, u32[]{:S(2)}, u32[]{:S(2)}) %collective-permute-start.20) | collective-permute-done | bytes 98336 | tf_op jit(solution)/shard_map/ppermute | solution.py:315
  86.2 1.0 %shard_map.118 = (f32[128,1536]{1,0:T(8,128)}, f32[8,512]{1,0:T(8,128)}, f32[8,512]{1,0:T(8,128)}, f32[2,1536]{1,0:T(2,128)}, f32[1]{0:T(128)}) custom-call(s32[1]{0:T(128)} %bitcast.did, bf16[4,2,4,8,384]{4,3,2,1,0:T(8,128)(2,1)S(1)} %bitcast.16, bf16[128,384]{1,0:T(8,128)(2,1)S(1)} %get-tuple-element.66.d0, ...), custom_call_target="tpu_custom_call" | custom-call | tf_op jit(solution)/shard_map/pallas_call | solution.py:420
  (22 shorter events, 2.5 us)
Async XLA Ops:
  22.4 14.9 %collective-permute-start.5 = (bf16[4,2,32,256]{3,2,1,0:T(8,128)(2,1)S(1)}, bf16[4,2,32,256]{3,2,1,0:T(8,128)(2,1)S(1)}, u32[]{:S(2)}, u32[]{:S(2)}) collective-permute-start(bf16[4,2,32,256]{3,2,1,0:T(8,128)(2,1)S(1)} %bitcast.18), channel_id=1, source_target_pairs={{0,48},{16,0},{32,16},{48,32},{1,49},{17,1},{33,17},{49,33},{2,50}... | collective-permute-start | bytes 393224 | tf_op jit(solution)/shard_map/ppermute | solution.py:315
  24.8 12.5 %collective-permute-start.4 = (bf16[4,2,32,256]{3,2,1,0:T(8,128)(2,1)S(1)}, bf16[4,2,32,256]{3,2,1,0:T(8,128)(2,1)S(1)}, u32[]{:S(2)}, u32[]{:S(2)}) collective-permute-start(bf16[4,2,32,256]{3,2,1,0:T(8,128)(2,1)S(1)} %bitcast.19), channel_id=1, source_target_pairs={{0,32},{16,48},{32,0},{48,16},{1,33},{17,49},{33,1},{49,17},{2,34}... | collective-permute-start | bytes 393224 | tf_op jit(solution)/shard_map/ppermute | solution.py:315
  25.4 12.4 %collective-permute-start.3 = (bf16[4,2,32,256]{3,2,1,0:T(8,128)(2,1)S(1)}, bf16[4,2,32,256]{3,2,1,0:T(8,128)(2,1)S(1)}, u32[]{:S(2)}, u32[]{:S(2)}) collective-permute-start(bf16[4,2,32,256]{3,2,1,0:T(8,128)(2,1)S(1)} %bitcast.20), channel_id=1, source_target_pairs={{0,16},{16,32},{32,48},{48,0},{1,17},{17,33},{33,49},{49,1},{2,18}... | collective-permute-start | bytes 393224 | tf_op jit(solution)/shard_map/ppermute | solution.py:315
  27.1 6.4 %collective-permute-start = (bf16[144,384]{1,0:T(8,128)(2,1)S(1)}, bf16[144,384]{1,0:T(8,128)(2,1)S(1)}, u32[]{:S(2)}, u32[]{:S(2)}) collective-permute-start(bf16[144,384]{1,0:T(8,128)(2,1)S(1)} %get-tuple-element.43), channel_id=1, source_target_pairs={{0,4},{4,8},{8,12},{12,0},{1,5},{5,9},{9,13},{13,1},{2,6},{6,10},{... | collective-permute-start | bytes 331784 | tf_op jit(solution)/shard_map/ppermute | solution.py:315
  27.5 10.3 %collective-permute-start.1 = (bf16[144,384]{1,0:T(8,128)(2,1)S(1)}, bf16[144,384]{1,0:T(8,128)(2,1)S(1)}, u32[]{:S(2)}, u32[]{:S(2)}) collective-permute-start(bf16[144,384]{1,0:T(8,128)(2,1)S(1)} %get-tuple-element.44), channel_id=1, source_target_pairs={{0,8},{4,12},{8,0},{12,4},{1,9},{5,13},{9,1},{13,5},{2,10},{6,14},... | collective-permute-start | bytes 331784 | tf_op jit(solution)/shard_map/ppermute | solution.py:315
  33.5 8.6 %collective-permute-start.6 = (bf16[4,2,32,256]{3,2,1,0:T(8,128)(2,1)S(1)}, bf16[4,2,32,256]{3,2,1,0:T(8,128)(2,1)S(1)}, u32[]{:S(2)}, u32[]{:S(2)}) collective-permute-start(bf16[4,2,32,256]{3,2,1,0:T(8,128)(2,1)S(1)} %bitcast.21), channel_id=1, source_target_pairs={{0,1},{1,0},{2,3},{3,2},{4,5},{5,4},{6,7},{7,6},{8,9},{9,8},{10,11... | collective-permute-start | bytes 393224 | tf_op jit(solution)/shard_map/ppermute | solution.py:315
  37.3 4.8 %collective-permute-start.9 = (bf16[4,2,32,256]{3,2,1,0:T(8,128)(2,1)S(1)}, bf16[4,2,32,256]{3,2,1,0:T(8,128)(2,1)S(1)}, u32[]{:S(2)}, u32[]{:S(2)}) collective-permute-start(bf16[4,2,32,256]{3,2,1,0:T(8,128)(2,1)S(1)} %collective-permute-done.5.rest_3_), channel_id=1, source_target_pairs={{0,1},{1,0},{2,3},{3,2},{4,5},{5,4},{6,7},{7,6},{8,9},{9,8},{10,11... | collective-permute-start | bytes 393224 | tf_op jit(solution)/shard_map/ppermute | solution.py:315
  37.3 4.8 %collective-permute-start.8 = (bf16[4,2,32,256]{3,2,1,0:T(8,128)(2,1)S(1)}, bf16[4,2,32,256]{3,2,1,0:T(8,128)(2,1)S(1)}, u32[]{:S(2)}, u32[]{:S(2)}) collective-permute-start(bf16[4,2,32,256]{3,2,1,0:T(8,128)(2,1)S(1)} %collective-permute-done.4.rest_2_), channel_id=1, source_target_pairs={{0,1},{1,0},{2,3},{3,2},{4,5},{5,4},{6,7},{7,6},{8,9},{9,8},{10,11... | collective-permute-start | bytes 393224 | tf_op jit(solution)/shard_map/ppermute | solution.py:315
  37.8 4.3 %collective-permute-start.7 = (bf16[4,2,32,256]{3,2,1,0:T(8,128)(2,1)S(1)}, bf16[4,2,32,256]{3,2,1,0:T(8,128)(2,1)S(1)}, u32[]{:S(2)}, u32[]{:S(2)}) collective-permute-start(bf16[4,2,32,256]{3,2,1,0:T(8,128)(2,1)S(1)} %collective-permute-done.3.rest_1_), channel_id=1, source_target_pairs={{0,1},{1,0},{2,3},{3,2},{4,5},{5,4},{6,7},{7,6},{8,9},{9,8},{10,11... | collective-permute-start | bytes 393224 | tf_op jit(solution)/shard_map/ppermute | solution.py:315
  37.9 4.2 %collective-permute-start.2 = (bf16[144,384]{1,0:T(8,128)(2,1)S(1)}, bf16[144,384]{1,0:T(8,128)(2,1)S(1)}, u32[]{:S(2)}, u32[]{:S(2)}) collective-permute-start(bf16[144,384]{1,0:T(8,128)(2,1)S(1)} %get-tuple-element.45), channel_id=1, source_target_pairs={{0,12},{4,0},{8,4},{12,8},{1,13},{5,1},{9,5},{13,9},{2,14},{6,2},{... | collective-permute-start | bytes 331784 | tf_op jit(solution)/shard_map/ppermute | solution.py:315
  45.2 3.9 %collective-permute-start.12 = (f32[4,8,128]{2,1,0:T(8,128)S(1)}, f32[4,8,128]{2,1,0:T(8,128)S(1)}, u32[]{:S(2)}, u32[]{:S(2)}) collective-permute-start(f32[4,8,128]{2,1,0:T(8,128)S(1)} %get-tuple-element.51.l0), channel_id=1, source_target_pairs={{0,12},{4,0},{8,4},{12,8},{1,13},{5,1},{9,5},{13,9},{2,14},{6,2},{... | collective-permute-start | bytes 49160 | tf_op jit(solution)/shard_map/ppermute | solution.py:315
  45.9 4.1 %collective-permute-start.11 = (f32[4,8,128]{2,1,0:T(8,128)S(1)}, f32[4,8,128]{2,1,0:T(8,128)S(1)}, u32[]{:S(2)}, u32[]{:S(2)}) collective-permute-start(f32[4,8,128]{2,1,0:T(8,128)S(1)} %get-tuple-element.51.l0), channel_id=1, source_target_pairs={{0,8},{4,12},{8,0},{12,4},{1,9},{5,13},{9,1},{13,5},{2,10},{6,14},... | collective-permute-start | bytes 49160 | tf_op jit(solution)/shard_map/ppermute | solution.py:315
  46.4 3.9 %collective-permute-start.10 = (f32[4,8,128]{2,1,0:T(8,128)S(1)}, f32[4,8,128]{2,1,0:T(8,128)S(1)}, u32[]{:S(2)}, u32[]{:S(2)}) collective-permute-start(f32[4,8,128]{2,1,0:T(8,128)S(1)} %get-tuple-element.51.l0), channel_id=1, source_target_pairs={{0,4},{4,8},{8,12},{12,0},{1,5},{5,9},{9,13},{13,1},{2,6},{6,10},{... | collective-permute-start | bytes 49160 | tf_op jit(solution)/shard_map/ppermute | solution.py:315
  51.3 5.6 %collective-permute-start.13 = (bf16[4,4,2,32,256]{4,3,2,1,0:T(8,128)(2,1)S(1)}, bf16[4,4,2,32,256]{4,3,2,1,0:T(8,128)(2,1)S(1)}, u32[]{:S(2)}, u32[]{:S(2)}) collective-permute-start(bf16[4,4,2,32,256]{4,3,2,1,0:T(8,128)(2,1)S(1)} %get-tuple-element.60), channel_id=1, source_target_pairs={{0,1},{1,0},{2,3},{3,2},{4,5},{5,4},{6,7},{7,6},{8,9},{9,8},{10,11... | collective-permute-start | bytes 1572872 | tf_op jit(solution)/shard_map/ppermute | solution.py:315
  57.1 5.1 %collective-permute-start.14 = (bf16[4,2,32,256]{3,2,1,0:T(8,128)(2,1)S(1)}, bf16[4,2,32,256]{3,2,1,0:T(8,128)(2,1)S(1)}, u32[]{:S(2)}, u32[]{:S(2)}) collective-permute-start(bf16[4,2,32,256]{3,2,1,0:T(8,128)(2,1)S(1)} %get-tuple-element.62), channel_id=1, source_target_pairs={{0,48},{16,0},{32,16},{48,32},{1,49},{17,1},{33,17},{49,33},{2,50}... | collective-permute-start | bytes 393224 | tf_op jit(solution)/shard_map/ppermute | solution.py:315
  59.2 6.1 %collective-permute-start.15 = (bf16[4,2,32,256]{3,2,1,0:T(8,128)(2,1)S(1)}, bf16[4,2,32,256]{3,2,1,0:T(8,128)(2,1)S(1)}, u32[]{:S(2)}, u32[]{:S(2)}) collective-permute-start(bf16[4,2,32,256]{3,2,1,0:T(8,128)(2,1)S(1)} %get-tuple-element.63), channel_id=1, source_target_pairs={{0,32},{16,48},{32,0},{48,16},{1,33},{17,49},{33,1},{49,17},{2,34}... | collective-permute-start | bytes 393224 | tf_op jit(solution)/shard_map/ppermute | solution.py:315
  60.5 8.5 %collective-permute-start.16 = (bf16[4,2,32,256]{3,2,1,0:T(8,128)(2,1)S(1)}, bf16[4,2,32,256]{3,2,1,0:T(8,128)(2,1)S(1)}, u32[]{:S(2)}, u32[]{:S(2)}) collective-permute-start(bf16[4,2,32,256]{3,2,1,0:T(8,128)(2,1)S(1)} %get-tuple-element.64), channel_id=1, source_target_pairs={{0,16},{16,32},{32,48},{48,0},{1,17},{17,33},{33,49},{49,1},{2,18}... | collective-permute-start | bytes 393224 | tf_op jit(solution)/shard_map/ppermute | solution.py:315
  60.5 1.5 %collective-permute-start.17 = (f32[8,128]{1,0:T(8,128)S(1)}, f32[8,128]{1,0:T(8,128)S(1)}, u32[]{:S(2)}, u32[]{:S(2)}) collective-permute-start(f32[8,128]{1,0:T(8,128)S(1)} %get-tuple-element.65.hg), channel_id=1, source_target_pairs={{0,1},{1,0},{2,3},{3,2},{4,5},{5,4},{6,7},{7,6},{8,9},{9,8},{10,11... | collective-permute-start | bytes 12296 | tf_op jit(solution)/shard_map/ppermute | solution.py:315
  69.7 16.5 %all-to-all-start.1 = ((bf16[32,8,384]{2,1,0:T(8,128)(2,1)}), bf16[32,8,384]{2,1,0:T(8,128)(2,1)S(1)}, u32[]{:S(2)}, u32[]{:S(2)}) async-start(bf16[32,8,384]{2,1,0:T(8,128)(2,1)} %bitcast.9), calls=%async_computation.1 | async-start | bytes 393216 | tf_op jit(solution)/shard_map/all_to_all | solution.py:416
  74.0 5.7 %collective-permute-start.18 = (bf16[128,384]{1,0:T(8,128)(2,1)S(1)}, bf16[128,384]{1,0:T(8,128)(2,1)S(1)}, u32[]{:S(2)}, u32[]{:S(2)}) collective-permute-start(bf16[128,384]{1,0:T(8,128)(2,1)S(1)} %get-tuple-element.67), channel_id=1, source_target_pairs={{0,12},{4,0},{8,4},{12,8},{1,13},{5,1},{9,5},{13,9},{2,14},{6,2},{... | collective-permute-start | bytes 294920 | tf_op jit(solution)/shard_map/ppermute | solution.py:315
  76.5 5.9 %collective-permute-start.19 = (bf16[128,384]{1,0:T(8,128)(2,1)S(1)}, bf16[128,384]{1,0:T(8,128)(2,1)S(1)}, u32[]{:S(2)}, u32[]{:S(2)}) collective-permute-start(bf16[128,384]{1,0:T(8,128)(2,1)S(1)} %get-tuple-element.68), channel_id=1, source_target_pairs={{0,8},{4,12},{8,0},{12,4},{1,9},{5,13},{9,1},{13,5},{2,10},{6,14},... | collective-permute-start | bytes 294920 | tf_op jit(solution)/shard_map/ppermute | solution.py:315
  77.1 9.1 %collective-permute-start.20 = (bf16[128,384]{1,0:T(8,128)(2,1)S(1)}, bf16[128,384]{1,0:T(8,128)(2,1)S(1)}, u32[]{:S(2)}, u32[]{:S(2)}) collective-permute-start(bf16[128,384]{1,0:T(8,128)(2,1)S(1)} %get-tuple-element.69), channel_id=1, source_target_pairs={{0,4},{4,8},{8,12},{12,0},{1,5},{5,9},{9,13},{13,1},{2,6},{6,10},{... | collective-permute-start | bytes 294920 | tf_op jit(solution)/shard_map/ppermute | solution.py:315

commit v2 on v1

--- a/solution.py
+++ b/solution.py
@@ -16,6 +16,7 @@
 NEG = -1.0e30
 F32 = jnp.float32
 BF16 = jnp.bfloat16
+HIGH = lax.Precision.HIGHEST
 CHUNKS = ((0,), (0, 1), (0, 1, 2), (3,))
 P_AT = (0, 1, 3, 6)
 YZ_AXES = ("y", "zh", "zl")
@@ -163,7 +164,7 @@
         plog[(y - ys + 4) % 4] = jnp.broadcast_to(lg, (8, BLOCK))
 
 
-def middle_kernel(did, w, p, delta, q, kv, g_out, dq_out, qt_out, kt, u):
+def middle_kernel(did, w, p, delta, q, kv, g_out, dq_out, qt_out, pv_out, kt, vt, u):
     _, _, y, _, _ = coords(did)
     eye = jnp.where(
         lax.broadcasted_iota(jnp.int32, (BLOCK, BLOCK), 0) == lax.broadcasted_iota(jnp.int32, (BLOCK, BLOCK), 1), 1.0, 0.0
@@ -174,12 +175,17 @@
     for ch in range(4):
         rows = slice(ch * CHUNK, (ch + 1) * CHUNK)
         kt[:, rows] = times_t(eye, kv[rows, :HEAD_WIDTH]).astype(BF16)
+        vt[:, rows] = times_t(eye, kv[rows, HEAD_WIDTH:]).astype(BF16)
         u[rows, :] = times_t(kv[rows, HEAD_WIDTH:], high) + times_t(kv[rows, HEAD_WIDTH:], low)
     for ys in range(4):
         qt_out[ys] = times_t(eye, q[ys]).astype(BF16)
         dqt = jnp.zeros((HEAD_WIDTH, WIDE), F32)
+        pv = jnp.zeros((HEAD_WIDTH, WIDE), F32)
         for i, ch in enumerate(CHUNKS[ys]):
             at_p = (P_AT[ys] + i) * CHUNK
+            pv = pv + jnp.dot(
+                vt[:, ch * CHUNK : (ch + 1) * CHUNK], p[at_p : at_p + CHUNK, :], preferred_element_type=F32
+            )
             for b in range(CHUNK // BLOCK):
                 row = ch * CHUNK + b * BLOCK
                 at = slice(at_p + b * BLOCK, at_p + (b + 1) * BLOCK)
@@ -191,6 +197,7 @@
                 kt[:, ch * CHUNK : (ch + 1) * CHUNK], g_out[at_p : at_p + CHUNK, :], preferred_element_type=F32
             )
         dq_out[ys] = dqt
+        pv_out[ys] = pv
 
 
 def key_terms(out, half, p, g, qf, at16):
@@ -206,10 +213,10 @@
         for z in range(2):
             for kx in range(4):
                 row = z * BLOCK + kx * 32
-                out[kx, ch, z] = both[row : row + 32]
-
-
-def far_kernel(did, w, l0, l1, l2, l3, g0, g1, g2, g3, p, g, inv, qt, out, f_out, qf, at16, loss_out, lgs, labs):
+                out[kx * 8 + ch * 2 + z] = both[row : row + 32]
+
+
+def far_kernel(did, w, l0, l1, l2, l3, g0, g1, g2, g3, p, g, inv, qt, pv, out, f_out, qf, at16, hg_out, lgs, labs):
     _, _, y, _, _ = coords(did)
     for k, ref in enumerate((l0, l1, l2, l3)):
         src = (y - k + 4) % 4
@@ -219,7 +226,10 @@
     for k, ref in enumerate((g0, g1, g2, g3)):
         labs[(y - k + 4) % 4] = ref[BLOCK:, :256].astype(F32)[8:16, :]
     wt = jnp.concatenate([jnp.broadcast_to(head_diff(w, y, h), (BLOCK, HEAD_WIDTH)).T for h in range(GROUP)], axis=1)
+    head_of = lax.broadcasted_iota(jnp.int32, (8, WIDE), 1) // BLOCK
+    head_at = lax.broadcasted_iota(jnp.int32, (8, WIDE), 0)
     loss = jnp.zeros((1, BLOCK), F32)
+    hg = jnp.zeros((8, HEAD_WIDTH), F32)
     for ys in range(4):
         z = (lgs[0, ys] + lgs[1, ys] + lgs[2, ys] + lgs[3, ys])[0:1, :]
         one = labs[ys, 0:1, :BLOCK] > 0.5
@@ -233,25 +243,21 @@
         f_out[ys] = jnp.broadcast_to(f, (8, WIDE))
         at16[ys] = (wt * f).astype(BF16)
         qf[ys] = (qt[ys].astype(F32) * (f * SCALE)).astype(BF16)
-    loss_out[...] = jnp.broadcast_to(loss, (8, BLOCK))
+        hg = hg + lax.dot_general(
+            jnp.where(head_of == head_at, f, 0.0), pv[ys], NT, precision=HIGH, preferred_element_type=F32
+        )
+    row8 = lax.broadcasted_iota(jnp.int32, (8, BLOCK), 0)
+    high, low = halves(jnp.where(row8 == GROUP, loss, hg))
+    hg_out[...] = high + low
+    tail = jnp.concatenate([high, low], axis=1)
+    out[32] = jnp.concatenate([tail] * 4, axis=0).astype(BF16)
     key_terms(out, 1, p, g, qf, at16)
 
 
-def own_kernel(did, p, g, qf, at16, f, loss, kv, dqt, out, hg_out, d0, d1, d2, d3, dqb, ct):
+def own_kernel(did, p, g, qf, at16, f, dqt, out, d0, d1, d2, d3, dqb):
     _, _, y, _, _ = coords(did)
     key_terms(out, 0, p, g, qf, at16)
-    head_of = lax.broadcasted_iota(jnp.int32, (8, WIDE), 1) // BLOCK
-    head_at = lax.broadcasted_iota(jnp.int32, (8, WIDE), 0)
-    seen = set()
     for ys in range(4):
-        fm = on_both(jnp.where(head_of == head_at, f[ys, 0:1, :], 0.0))
-        for i, ch in enumerate(CHUNKS[ys]):
-            at = (P_AT[ys] + i) * CHUNK
-            rows = slice(ch * CHUNK, (ch + 1) * CHUNK)
-            cs = times_t(fm, p[at : at + CHUNK, :])
-            cs = cs[:8] + cs[8:]
-            ct[:, rows] = ct[:, rows] + cs if ch in seen else cs
-            seen.add(ch)
         dqs = dqt[ys] * (f[ys, 0:1, :] * SCALE)
         slot = (y - ys + 4) % 4
         for h in range(GROUP):
@@ -259,23 +265,24 @@
             dqb[slot, :, cols] = dqs[:, cols].T.astype(BF16)
     for k, ref in enumerate((d0, d1, d2, d3)):
         ref[...] = dqb[k]
-    hg = jnp.dot(on_both(ct[...]), kv[:, HEAD_WIDTH:], preferred_element_type=F32)
-    row8 = lax.broadcasted_iota(jnp.int32, (8, BLOCK), 0)
-    hg_out[...] = jnp.where(row8 == GROUP, loss[...], hg[:8] + hg[8:])
-
-
-def core_kernel(own, far, b0, b1, b2, b3):
+
+
+def core_kernel(own, far, hg, b0, b1, b2, b3, hg_out):
     for kx, out in enumerate((b0, b1, b2, b3)):
 
         def add(ys, carry, kx=kx, out=out):
-            out[ys] = (own[kx, ys].astype(F32) + far[kx, ys].astype(F32)).astype(BF16)
+            for z in range(2):
+                at = kx * 8 + ys * 2 + z
+                out[ys, z] = (own[at].astype(F32) + far[at].astype(F32)).astype(BF16)
             return carry
 
         lax.fori_loop(0, 4, add, 0)
-
-
-def x_kernel(b0, b1, b2, b3, hg, hg_far, out):
-    high, low = halves(hg[...] + hg_far[...])
+    v = far[32].astype(F32)[:8]
+    hg_out[...] = hg[...] + (v[:, :BLOCK] + v[:, BLOCK:])
+
+
+def x_kernel(b0, b1, b2, b3, hg, out):
+    high, low = halves(hg[...])
     tail = jnp.concatenate([high[:4], low[:4]], axis=0).astype(BF16)
     tail = jnp.broadcast_to(tail[None, None], (2, 4, 8, BLOCK))
 
@@ -288,8 +295,15 @@
     lax.fori_loop(0, 4, add, 0)
 
 
-def finish_kernel(did, pieces, d0, d1, d2, d3, qg, gk, gv, hg, loss):
-    zl, _, y, _, _ = coords(did)
+def rows_kernel(did, d0, d1, d2, d3, qg):
+    _, _, y, _, _ = coords(did)
+    for k, d in enumerate((d0, d1, d2, d3)):
+        wide = pl.ds(pl.multiple_of(((y + k) % 4) * WIDE, HEAD_WIDTH), WIDE)
+        qg[:, wide] = d[...].astype(F32)
+
+
+def finish_kernel(did, pieces, gk, gv, hg, loss):
+    zl, _, _, _, _ = coords(did)
     for g in range(4):
         v = jnp.zeros((8, 256), F32)
         for k in range(2):
@@ -306,9 +320,6 @@
             hg[1:2, cols] = -v[h : h + 1]
         if g == 0:
             loss[0] = jnp.sum(v[GROUP : GROUP + 1]) * (1.0 / TOKENS)
-    for k, d in enumerate((d0, d1, d2, d3)):
-        wide = pl.ds(pl.multiple_of(((y + k) % 4) * WIDE, HEAD_WIDTH), WIDE)
-        qg[:, wide] = d[...].astype(F32)
 
 
 def shift(v, axis, size, k):
@@ -338,7 +349,7 @@
     did = lax.axis_index(("zl", "x", "y", "zh", "c")).astype(jnp.int32).reshape(1)
     (copies,) = call(
         keys_kernel,
-        [like((4, 8, 8, 256), BF16)],
+        [pltpu.VMEM((4, 8, 8, 256), BF16)],
         [HBM] * 2,
         scratch=[pltpu.VMEM((8, 512), BF16), pltpu.VMEM((8, 512), BF16), pltpu.SemaphoreType.DMA((2,))],
     )(in_hbm(keys), in_hbm(values))
@@ -380,55 +391,56 @@
         scratch=[pltpu.VMEM((3 * CHUNK, WIDE), F32), pltpu.VMEM((16, TOKENS), BF16)],
     )(did, seg, w, *packs, *over_x, *over_c)
     logs = [plog] + [shift(plog, "y", 4, k) for k in range(1, 4)]
-    g, dqt, qt = call(
+    g, dqt, qt, pv = call(
         middle_kernel,
         [
             like((7 * CHUNK, WIDE), BF16),
             like((4, HEAD_WIDTH, WIDE), F32),
             like((4, HEAD_WIDTH, WIDE), BF16),
+            like((4, HEAD_WIDTH, WIDE), F32),
         ],
         [SMEM] + [VMEM] * 5,
-        scratch=[pltpu.VMEM((HEAD_WIDTH, TOKENS), BF16), pltpu.VMEM((TOKENS, BLOCK), F32)],
+        scratch=[
+            pltpu.VMEM((HEAD_WIDTH, TOKENS), BF16),
+            pltpu.VMEM((HEAD_WIDTH, TOKENS), BF16),
+            pltpu.VMEM((TOKENS, BLOCK), F32),
+        ],
     )(did, w, p, delta, q, kv)
-    far_d, f, qf, at16, loss_rows = call(
+    far_d, f, qf, at16, hg = call(
         far_kernel,
         [
-            like((4, 4, 2, 32, 256), BF16),
+            like((33, 32, 256), BF16),
             like((4, 8, WIDE), F32),
             like((4, HEAD_WIDTH, WIDE), BF16),
             like((4, HEAD_WIDTH, WIDE), BF16),
             like((8, BLOCK), F32),
         ],
-        [SMEM] + [VMEM] * 13,
+        [SMEM] + [VMEM] * 14,
         scratch=[pltpu.VMEM((4, 4, 8, BLOCK), F32), pltpu.VMEM((4, 8, 256), F32)],
-    )(did, w, *logs, *packs, p, g, inv, qt)
+    )(did, w, *logs, *packs, p, g, inv, qt, pv)
     far = shift(far_d, "c", 2, 1)
-    own_d, hg, *dq = call(
+    own_d, *dq = call(
         own_kernel,
-        [like((4, 4, 2, 32, 256), BF16), like((8, BLOCK), F32)] + [like((BLOCK, WIDE), BF16)] * 4,
-        [SMEM] + [VMEM] * 8,
-        scratch=[pltpu.VMEM((4, BLOCK, WIDE), BF16), pltpu.VMEM((8, TOKENS), F32)],
-    )(did, p, g, qf, at16, f, loss_rows, kv, dqt)
-    by_x = call(core_kernel, [like((4, 2, 32, 256), BF16)] * 4, [VMEM] * 2)(own_d, far)
+        [like((32, 32, 256), BF16)] + [like((BLOCK, WIDE), BF16)] * 4,
+        [SMEM] + [VMEM] * 6,
+        scratch=[pltpu.VMEM((4, BLOCK, WIDE), BF16)],
+    )(did, p, g, qf, at16, f, dqt)
+    *by_x, hg = call(core_kernel, [like((4, 2, 32, 256), BF16)] * 4 + [like((8, BLOCK), F32)], [VMEM] * 3)(
+        own_d, far, hg
+    )
     got = [by_x[0]] + [shift(by_x[k], "x", 4, -k) for k in range(1, 4)]
-    hg_far = shift(hg, "c", 2, 1)
-    (by_z,) = call(x_kernel, [like((4, 2, 4, 8, WIDE), BF16)], [VMEM] * 6)(*got, hg, hg_far)
+    (by_z,) = call(x_kernel, [pltpu.VMEM((4, 2, 4, 8, WIDE), BF16)], [VMEM] * 5)(*got, hg)
     pieces = lax.all_to_all(by_z.reshape(32, 8, WIDE), YZ_AXES, 0, 0, tiled=True).reshape(4, 2, 4, 8, WIDE)
     back = [dq[0]]
     for k in range(1, 4):
         back.append(shift(dq[k], "y", 4, -k))
-    query_gradient, grad_keys, grad_values, head_t, loss = call(
+    (query_gradient,) = call(rows_kernel, [like((BLOCK, 4 * WIDE), F32)], [SMEM] + [VMEM] * 4)(did, *back)
+    grad_keys, grad_values, head_t, loss = call(
         finish_kernel,
-        [
-            like((BLOCK, 4 * WIDE), F32),
-            like((8, 512), F32),
-            like((8, 512), F32),
-            like((2, 4 * WIDE), F32),
-            like((1,), F32),
-        ],
-        [SMEM] + [VMEM] * 5,
-        [VMEM] * 4 + [SMEM],
-    )(did, pieces, *back)
+        [like((8, 512), F32), like((8, 512), F32), like((2, 4 * WIDE), F32), like((1,), F32)],
+        [SMEM, VMEM],
+        [VMEM] * 3 + [SMEM],
+    )(did, pieces)
     return loss, query_gradient[None], grad_keys, grad_values, head_t.T[None]
 
 

time: 87.7 us -> 86.9 us (level)
  waiting for transfers between devices: 25.9 us -> 24.4 us
    ppermute x21 -> x20, waiting for transfers between devices: 25.9 us -> 24.4 us  [shift(): return lax.ppermute(v, axis, [(i, (i + k) % size) for i in range(size)])]
    ppermute x21 -> x20, starting transfers between devices: 23.3 us -> 23.9 us  [shift(): return lax.ppermute(v, axis, [(i, (i + k) % size) for i in range(size)])]
    pallas_call x6 -> x7, Pallas kernels: 5.42 us -> 5.92 us  [the longest x1 1.73 us: per_device(): call(far_kernel, [like((33, 32, 256), BF16), like((4, 8, WIDE), F32), lik...]
  transfers between devices with their start and end apart: 22 -> 21, of which waited for: 11 -> 9; matrix products, arithmetic and copies ran while one was open for 0% -> 0% of each run, Pallas kernels for 6% -> 6%
where the time goes in v2:
time: 86.9 us; the launch traced here: 86.6 us
  starting transfers between devices  27.8 us (32%)
  waiting for transfers between devices  24.4 us (28%)
  blocking collectives  21 us (24%)
  Pallas kernels  12.5 us (14%)
  between operations  0.93 us (1%)
    ppermute x20, waiting for transfers between devices, shift(): return lax.ppermute(v, axis, [(i, (i + k) % size) for i in range(size)])  24.4 us
    ppermute x20, starting transfers between devices, shift(): return lax.ppermute(v, axis, [(i, (i + k) % size) for i in range(size)])  23.9 us
    all_to_all x1, blocking collectives, per_device(): lax.all_to_all(copies.reshape(32, 8, 256), YZ_AXES, 0, 0, tiled=True)  21 us
    all_to_all x1, starting transfers between devices, per_device(): lax.all_to_all(by_z.reshape(32, 8, WIDE), YZ_AXES, 0, 0, tiled=True)  3.87 us
    pallas_call x1, Pallas kernels, per_device(): call(forward_kernel, [like((4, 8, BLOCK), F32), like((7 * CHUNK, WIDE), B...  3.06 us
    pallas_call x1, Pallas kernels, per_device(): call(middle_kernel, [like((7 * CHUNK, WIDE), BF16), like((4, HEAD_WIDTH,...  2.36 us
  transfers between devices with their start and end apart: 21, of which 9 were waited for; matrix products, arithmetic and copies ran while one was open for 0% of the time, Pallas kernels for 6%

profile of v2, /device:TPU:1, one launch (start us, length us, event | category | flops | bytes accessed | tf_op | source)
XLA Modules:
  0.0 86.6 jit_solution(7988428105246812693)
XLA Ops:
  0.6 0.7 shard_map.111
  1.4 21.0 %all_to_all.10 = bf16[32,8,256]{2,1,0:T(8,128)(2,1)S(1)} all-to-all(bf16[32,8,256]{2,1,0:T(8,128)(2,1)S(1)} %bitcast.17), channel_id=1, replica_groups=mesh['zl'=4,'x'=4,'y'=4,'zh'=2,'c'=2] {'y','zh','zl'}, dimensions={0} | all-to-all | bytes 262144 | tf_op jit(solution)/shard_map/all_to_all | solution.py:356
  22.4 1.2 %collective-permute-start.3 = (bf16[4,2,32,256]{3,2,1,0:T(8,128)(2,1)S(1)}, bf16[4,2,32,256]{3,2,1,0:T(8,128)(2,1)S(1)}, u32[]{:S(2)}, u32[]{:S(2)}) collective-permute-start(bf16[4,2,32,256]{3,2,1,0:T(8,128)(2,1)S(1)} %bitcast.18), channel_id=1, source_target_pairs={{0,16},{16,32},{32,48},{48,0},{1,17},{17,33},{33,49},{49,1},{2,18}... | collective-permute-start | bytes 393224 | tf_op jit(solution)/shard_map/ppermute | solution.py:326
  23.6 2.5 %collective-permute-start.4 = (bf16[4,2,32,256]{3,2,1,0:T(8,128)(2,1)S(1)}, bf16[4,2,32,256]{3,2,1,0:T(8,128)(2,1)S(1)}, u32[]{:S(2)}, u32[]{:S(2)}) collective-permute-start(bf16[4,2,32,256]{3,2,1,0:T(8,128)(2,1)S(1)} %bitcast.19), channel_id=1, source_target_pairs={{0,32},{16,48},{32,0},{48,16},{1,33},{17,49},{33,1},{49,17},{2,34}... | collective-permute-start | bytes 393224 | tf_op jit(solution)/shard_map/ppermute | solution.py:326
  26.0 1.2 %collective-permute-start.5 = (bf16[4,2,32,256]{3,2,1,0:T(8,128)(2,1)S(1)}, bf16[4,2,32,256]{3,2,1,0:T(8,128)(2,1)S(1)}, u32[]{:S(2)}, u32[]{:S(2)}) collective-permute-start(bf16[4,2,32,256]{3,2,1,0:T(8,128)(2,1)S(1)} %bitcast.20), channel_id=1, source_target_pairs={{0,48},{16,0},{32,16},{48,32},{1,49},{17,1},{33,17},{49,33},{2,50}... | collective-permute-start | bytes 393224 | tf_op jit(solution)/shard_map/ppermute | solution.py:326
  27.2 1.2 %shard_map.110 = (bf16[144,384]{1,0:T(8,128)(2,1)S(1)}, bf16[144,384]{1,0:T(8,128)(2,1)S(1)}, bf16[144,384]{1,0:T(8,128)(2,1)S(1)}, bf16[144,384]{1,0:T(8,128)(2...) custom-call(s32[1]{0:T(128)} %bitcast.did, s32[1,128]{1,0:T(1,128)} %bitcast.27, s32[1,128]{1,0:T(1,128)} %bitcast.28, ...), custom_call_target="tpu_custom_call" | custom-call | tf_op jit(solution)/shard_map/pallas_call | solution.py:357
  28.8 1.7 %collective-permute-start.1 = (bf16[144,384]{1,0:T(8,128)(2,1)S(1)}, bf16[144,384]{1,0:T(8,128)(2,1)S(1)}, u32[]{:S(2)}, u32[]{:S(2)}) collective-permute-start(bf16[144,384]{1,0:T(8,128)(2,1)S(1)} %get-tuple-element.44), channel_id=1, source_target_pairs={{0,8},{4,12},{8,0},{12,4},{1,9},{5,13},{9,1},{13,5},{2,10},{6,14},... | collective-permute-start | bytes 331784 | tf_op jit(solution)/shard_map/ppermute | solution.py:326
  30.5 3.9 %collective-permute-done.q1.g1 = bf16[144,384]{1,0:T(8,128)(2,1)S(1)} collective-permute-done((bf16[144,384]{1,0:T(8,128)(2,1)S(1)}, bf16[144,384]{1,0:T(8,128)(2,1)S(1)}, u32[]{:S(2)}, u32[]{:S(2)}) %collective-permute-start) | collective-permute-done | bytes 110624 | tf_op jit(solution)/shard_map/ppermute | solution.py:326
  34.4 4.1 %collective-permute-start.6 = (bf16[4,2,32,256]{3,2,1,0:T(8,128)(2,1)S(1)}, bf16[4,2,32,256]{3,2,1,0:T(8,128)(2,1)S(1)}, u32[]{:S(2)}, u32[]{:S(2)}) collective-permute-start(bf16[4,2,32,256]{3,2,1,0:T(8,128)(2,1)S(1)} %bitcast.21), channel_id=1, source_target_pairs={{0,1},{1,0},{2,3},{3,2},{4,5},{5,4},{6,7},{7,6},{8,9},{9,8},{10,11... | collective-permute-start | bytes 393224 | tf_op jit(solution)/shard_map/ppermute | solution.py:326
  38.5 0.5 collective-permute-start.8
  39.1 4.2 %collective-permute-done.2.q3.g3 = bf16[144,384]{1,0:T(8,128)(2,1)S(1)} collective-permute-done((bf16[144,384]{1,0:T(8,128)(2,1)S(1)}, bf16[144,384]{1,0:T(8,128)(2,1)S(1)}, u32[]{:S(2)}, u32[]{:S(2)}) %collective-permute-start.2) | collective-permute-done | bytes 110624 | tf_op jit(solution)/shard_map/ppermute | solution.py:326
  43.3 3.1 %shard_map.112 = (f32[4,8,128]{2,1,0:T(8,128)S(1)}, bf16[3584,384]{1,0:T(8,128)(2,1)S(1)}, f32[4,8,384]{2,1,0:T(8,128)S(1)}, f32[4,8,384]{2,1,0:T(8,128)S(1)}, b...) custom-call(s32[1]{0:T(128)} %bitcast.did, s32[1,2048]{1,0:T(1,128)S(1)} %get-tuple-element.40.seg, ...), custom_call_target="tpu_custom_call" | custom-call | tf_op jit(solution)/shard_map/pallas_call | solution.py:380
  46.5 1.8 %collective-permute-start.11 = (f32[4,8,128]{2,1,0:T(8,128)S(1)}, f32[4,8,128]{2,1,0:T(8,128)S(1)}, u32[]{:S(2)}, u32[]{:S(2)}) collective-permute-start(f32[4,8,128]{2,1,0:T(8,128)S(1)} %get-tuple-element.51.l0), channel_id=1, source_target_pairs={{0,8},{4,12},{8,0},{12,4},{1,9},{5,13},{9,1},{13,5},{2,10},{6,14},... | collective-permute-start | bytes 49160 | tf_op jit(solution)/shard_map/ppermute | solution.py:326
  48.3 0.9 %collective-permute-start.12 = (f32[4,8,128]{2,1,0:T(8,128)S(1)}, f32[4,8,128]{2,1,0:T(8,128)S(1)}, u32[]{:S(2)}, u32[]{:S(2)}) collective-permute-start(f32[4,8,128]{2,1,0:T(8,128)S(1)} %get-tuple-element.51.l0), channel_id=1, source_target_pairs={{0,12},{4,0},{8,4},{12,8},{1,13},{5,1},{9,5},{13,9},{2,14},{6,2},{... | collective-permute-start | bytes 49160 | tf_op jit(solution)/shard_map/ppermute | solution.py:326
  49.1 2.4 %shard_map.113 = (bf16[3584,384]{1,0:T(8,128)(2,1)S(1)}, f32[4,128,384]{2,1,0:T(8,128)S(1)}, bf16[4,128,384]{2,1,0:T(8,128)(2,1)S(1)}, f32[4,128,384]{2,1,0:T(8,128)S(1)}) custom-call(s32[1]{0:T(128)} %bitcast.did, f32[2,1536]{1,0:T(2,128)S(1)} %get-tuple-element.41.w, bf16[3584,384]{1,0:T(8,128)(2,1)S(1)} %get-tuple-element.46.p, ...), custom_call_target="tpu_custom_call" | custom-call | tf_op jit(solution)/shard_map/pallas_call | solution.py:394
  51.5 1.7 %shard_map.114 = (bf16[33,32,256]{2,1,0:T(8,128)(2,1)S(1)}, f32[4,8,384]{2,1,0:T(8,128)S(1)}, bf16[4,128,384]{2,1,0:T(8,128)(2,1)S(1)}, bf16[4,128,384]{2,1,0:T(8,128)(2,1)S(1)}, f32[8,128]{1,0:T(8,128)S(1)}) custom-call(s32[1]{0:T(128)} %bitcast.did, f32[2,1536]{1,0:T(2,128)S(1)} %get-tuple-element.41.w, f32[4,8,128]{2,1,0:T(8,128)S(1)} %get-tuple-element.51.l0, ...), custom_call_target="tpu_custom_call" | custom-call | tf_op jit(solution)/shard_map/pallas_call | solution.py:409
  53.3 3.7 %collective-permute-start.13 = (bf16[33,32,256]{2,1,0:T(8,128)(2,1)S(1)}, bf16[33,32,256]{2,1,0:T(8,128)(2,1)S(1)}, u32[]{:S(2)}, u32[]{:S(2)}) collective-permute-start(bf16[33,32,256]{2,1,0:T(8,128)(2,1)S(1)} %get-tuple-element.60), channel_id=1, source_target_pairs={{0,1},{1,0},{2,3},{3,2},{4,5},{5,4},{6,7},{7,6},{8,9},{9,8},{10,11... | collective-permute-start | bytes 1622024 | tf_op jit(solution)/shard_map/ppermute | solution.py:326
  57.0 0.9 %shard_map.115 = (bf16[32,32,256]{2,1,0:T(8,128)(2,1)S(1)}, bf16[128,384]{1,0:T(8,128)(2,1)S(1)}, bf16[128,384]{1,0:T(8,128)(2,1)S(1)}, bf16[128,384]{1,0:T(8,128)(2,1)S(1)}, bf16[128,384]{1,0:T(8,128)(2,1)S(1)}) custom-call(s32[1]{0:T(128)} %bitcast.did, bf16[3584,384]{1,0:T(8,128)(2,1)S(1)} %get-tuple-element.46.p, ...), custom_call_target="tpu_custom_call" | custom-call | tf_op jit(solution)/shard_map/pallas_call | solution.py:422
  57.9 0.7 collective-permute-done.13.far
  58.8 2.1 %collective-permute-start.15 = (bf16[4,2,32,256]{3,2,1,0:T(8,128)(2,1)S(1)}, bf16[4,2,32,256]{3,2,1,0:T(8,128)(2,1)S(1)}, u32[]{:S(2)}, u32[]{:S(2)}) collective-permute-start(bf16[4,2,32,256]{3,2,1,0:T(8,128)(2,1)S(1)} %get-tuple-element.64), channel_id=1, source_target_pairs={{0,32},{16,48},{32,0},{48,16},{1,33},{17,49},{33,1},{49,17},{2,34}... | collective-permute-start | bytes 393224 | tf_op jit(solution)/shard_map/ppermute | solution.py:326
  60.9 2.6 %collective-permute-done.14.b1 = bf16[4,2,32,256]{3,2,1,0:T(8,128)(2,1)S(1)} collective-permute-done((bf16[4,2,32,256]{3,2,1,0:T(8,128)(2,1)S(1)}, bf16[4,2,32,256]{3,2,1,0:T(8,128)(2,1)S(1)}, u32[]{:S(2)}, u32[]{:S(2)}) %collective-permute-start.14) | collective-permute-done | bytes 131104 | tf_op jit(solution)/shard_map/ppermute | solution.py:326
  63.5 1.6 %collective-permute-done.15.b2 = bf16[4,2,32,256]{3,2,1,0:T(8,128)(2,1)S(1)} collective-permute-done((bf16[4,2,32,256]{3,2,1,0:T(8,128)(2,1)S(1)}, bf16[4,2,32,256]{3,2,1,0:T(8,128)(2,1)S(1)}, u32[]{:S(2)}, u32[]{:S(2)}) %collective-permute-start.15) | collective-permute-done | bytes 131104 | tf_op jit(solution)/shard_map/ppermute | solution.py:326
  65.1 3.1 %collective-permute-done.16.b3 = bf16[4,2,32,256]{3,2,1,0:T(8,128)(2,1)S(1)} collective-permute-done((bf16[4,2,32,256]{3,2,1,0:T(8,128)(2,1)S(1)}, bf16[4,2,32,256]{3,2,1,0:T(8,128)(2,1)S(1)}, u32[]{:S(2)}, u32[]{:S(2)}) %collective-permute-start.16) | collective-permute-done | bytes 131104 | tf_op jit(solution)/shard_map/ppermute | solution.py:326
  68.2 0.8 shard_map.117
  69.0 3.9 %all-to-all-start.1 = ((bf16[32,8,384]{2,1,0:T(8,128)(2,1)}), bf16[32,8,384]{2,1,0:T(8,128)(2,1)S(1)}, u32[]{:S(2)}, u32[]{:S(2)}) async-start(bf16[32,8,384]{2,1,0:T(8,128)(2,1)} %bitcast.9), calls=%async_computation.1 | async-start | bytes 393216 | tf_op jit(solution)/shard_map/all_to_all | solution.py:433
  72.8 2.6 %collective-permute-start.17 = (bf16[128,384]{1,0:T(8,128)(2,1)S(1)}, bf16[128,384]{1,0:T(8,128)(2,1)S(1)}, u32[]{:S(2)}, u32[]{:S(2)}) collective-permute-start(bf16[128,384]{1,0:T(8,128)(2,1)S(1)} %get-tuple-element.69), channel_id=1, source_target_pairs={{0,12},{4,0},{8,4},{12,8},{1,13},{5,1},{9,5},{13,9},{2,14},{6,2},{... | collective-permute-start | bytes 294920 | tf_op jit(solution)/shard_map/ppermute | solution.py:326
  75.9 0.6 collective-permute-start.19
  76.5 1.7 %collective-permute-done.17.d1 = bf16[128,384]{1,0:T(8,128)(2,1)S(1)} collective-permute-done((bf16[128,384]{1,0:T(8,128)(2,1)S(1)}, bf16[128,384]{1,0:T(8,128)(2,1)S(1)}, u32[]{:S(2)}, u32[]{:S(2)}) %collective-permute-start.17) | collective-permute-done | bytes 98336 | tf_op jit(solution)/shard_map/ppermute | solution.py:326
  78.2 3.1 %collective-permute-done.18.d2 = bf16[128,384]{1,0:T(8,128)(2,1)S(1)} collective-permute-done((bf16[128,384]{1,0:T(8,128)(2,1)S(1)}, bf16[128,384]{1,0:T(8,128)(2,1)S(1)}, u32[]{:S(2)}, u32[]{:S(2)}) %collective-permute-start.18) | collective-permute-done | bytes 98336 | tf_op jit(solution)/shard_map/ppermute | solution.py:326
  81.3 3.6 %collective-permute-done.19.d3 = bf16[128,384]{1,0:T(8,128)(2,1)S(1)} collective-permute-done((bf16[128,384]{1,0:T(8,128)(2,1)S(1)}, bf16[128,384]{1,0:T(8,128)(2,1)S(1)}, u32[]{:S(2)}, u32[]{:S(2)}) %collective-permute-start.19) | collective-permute-done | bytes 98336 | tf_op jit(solution)/shard_map/ppermute | solution.py:326
  84.8 0.9 %shard_map.119 = f32[128,1536]{1,0:T(8,128)} custom-call(s32[1]{0:T(128)} %bitcast.did, bf16[128,384]{1,0:T(8,128)(2,1)S(1)} %get-tuple-element.68.d0, bf16[128,384]{1,0:T(8,128)(2,1)S(1)} %collective-permute-done.17.d1, bf16[128,384]{1,0:T(8,128)(2,1)S(1)} %collective-permute-done.18.d2, bf16[128,384]{1,0:T(8,128)(2,1)S(1)} %collective-permute-done.19.d3), custom_call_target="tpu_custom_call" | custom-call | tf_op jit(solution)/shard_map/pallas_call | solution.py:437
  85.8 0.6 shard_map.118
  (21 shorter events, 1.4 us)
Async XLA Ops:
  22.4 16.1 %collective-permute-start.3 = (bf16[4,2,32,256]{3,2,1,0:T(8,128)(2,1)S(1)}, bf16[4,2,32,256]{3,2,1,0:T(8,128)(2,1)S(1)}, u32[]{:S(2)}, u32[]{:S(2)}) collective-permute-start(bf16[4,2,32,256]{3,2,1,0:T(8,128)(2,1)S(1)} %bitcast.18), channel_id=1, source_target_pairs={{0,16},{16,32},{32,48},{48,0},{1,17},{17,33},{33,49},{49,1},{2,18}... | collective-permute-start | bytes 393224 | tf_op jit(solution)/shard_map/ppermute | solution.py:326
  23.6 14.9 %collective-permute-start.4 = (bf16[4,2,32,256]{3,2,1,0:T(8,128)(2,1)S(1)}, bf16[4,2,32,256]{3,2,1,0:T(8,128)(2,1)S(1)}, u32[]{:S(2)}, u32[]{:S(2)}) collective-permute-start(bf16[4,2,32,256]{3,2,1,0:T(8,128)(2,1)S(1)} %bitcast.19), channel_id=1, source_target_pairs={{0,32},{16,48},{32,0},{48,16},{1,33},{17,49},{33,1},{49,17},{2,34}... | collective-permute-start | bytes 393224 | tf_op jit(solution)/shard_map/ppermute | solution.py:326
  26.0 13.0 %collective-permute-start.5 = (bf16[4,2,32,256]{3,2,1,0:T(8,128)(2,1)S(1)}, bf16[4,2,32,256]{3,2,1,0:T(8,128)(2,1)S(1)}, u32[]{:S(2)}, u32[]{:S(2)}) collective-permute-start(bf16[4,2,32,256]{3,2,1,0:T(8,128)(2,1)S(1)} %bitcast.20), channel_id=1, source_target_pairs={{0,48},{16,0},{32,16},{48,32},{1,49},{17,1},{33,17},{49,33},{2,50}... | collective-permute-start | bytes 393224 | tf_op jit(solution)/shard_map/ppermute | solution.py:326
  28.4 6.1 %collective-permute-start = (bf16[144,384]{1,0:T(8,128)(2,1)S(1)}, bf16[144,384]{1,0:T(8,128)(2,1)S(1)}, u32[]{:S(2)}, u32[]{:S(2)}) collective-permute-start(bf16[144,384]{1,0:T(8,128)(2,1)S(1)} %get-tuple-element.43), channel_id=1, source_target_pairs={{0,4},{4,8},{8,12},{12,0},{1,5},{5,9},{9,13},{13,1},{2,6},{6,10},{... | collective-permute-start | bytes 331784 | tf_op jit(solution)/shard_map/ppermute | solution.py:326
  28.8 10.3 %collective-permute-start.1 = (bf16[144,384]{1,0:T(8,128)(2,1)S(1)}, bf16[144,384]{1,0:T(8,128)(2,1)S(1)}, u32[]{:S(2)}, u32[]{:S(2)}) collective-permute-start(bf16[144,384]{1,0:T(8,128)(2,1)S(1)} %get-tuple-element.44), channel_id=1, source_target_pairs={{0,8},{4,12},{8,0},{12,4},{1,9},{5,13},{9,1},{13,5},{2,10},{6,14},... | collective-permute-start | bytes 331784 | tf_op jit(solution)/shard_map/ppermute | solution.py:326
  34.4 8.9 %collective-permute-start.6 = (bf16[4,2,32,256]{3,2,1,0:T(8,128)(2,1)S(1)}, bf16[4,2,32,256]{3,2,1,0:T(8,128)(2,1)S(1)}, u32[]{:S(2)}, u32[]{:S(2)}) collective-permute-start(bf16[4,2,32,256]{3,2,1,0:T(8,128)(2,1)S(1)} %bitcast.21), channel_id=1, source_target_pairs={{0,1},{1,0},{2,3},{3,2},{4,5},{5,4},{6,7},{7,6},{8,9},{9,8},{10,11... | collective-permute-start | bytes 393224 | tf_op jit(solution)/shard_map/ppermute | solution.py:326
  38.5 4.8 %collective-permute-start.7 = (bf16[4,2,32,256]{3,2,1,0:T(8,128)(2,1)S(1)}, bf16[4,2,32,256]{3,2,1,0:T(8,128)(2,1)S(1)}, u32[]{:S(2)}, u32[]{:S(2)}) collective-permute-start(bf16[4,2,32,256]{3,2,1,0:T(8,128)(2,1)S(1)} %collective-permute-done.3.rest_1_), channel_id=1, source_target_pairs={{0,1},{1,0},{2,3},{3,2},{4,5},{5,4},{6,7},{7,6},{8,9},{9,8},{10,11... | collective-permute-start | bytes 393224 | tf_op jit(solution)/shard_map/ppermute | solution.py:326
  38.5 4.8 %collective-permute-start.8 = (bf16[4,2,32,256]{3,2,1,0:T(8,128)(2,1)S(1)}, bf16[4,2,32,256]{3,2,1,0:T(8,128)(2,1)S(1)}, u32[]{:S(2)}, u32[]{:S(2)}) collective-permute-start(bf16[4,2,32,256]{3,2,1,0:T(8,128)(2,1)S(1)} %collective-permute-done.4.rest_2_), channel_id=1, source_target_pairs={{0,1},{1,0},{2,3},{3,2},{4,5},{5,4},{6,7},{7,6},{8,9},{9,8},{10,11... | collective-permute-start | bytes 393224 | tf_op jit(solution)/shard_map/ppermute | solution.py:326
  39.0 4.3 %collective-permute-start.9 = (bf16[4,2,32,256]{3,2,1,0:T(8,128)(2,1)S(1)}, bf16[4,2,32,256]{3,2,1,0:T(8,128)(2,1)S(1)}, u32[]{:S(2)}, u32[]{:S(2)}) collective-permute-start(bf16[4,2,32,256]{3,2,1,0:T(8,128)(2,1)S(1)} %collective-permute-done.5.rest_3_), channel_id=1, source_target_pairs={{0,1},{1,0},{2,3},{3,2},{4,5},{5,4},{6,7},{7,6},{8,9},{9,8},{10,11... | collective-permute-start | bytes 393224 | tf_op jit(solution)/shard_map/ppermute | solution.py:326
  39.1 4.2 %collective-permute-start.2 = (bf16[144,384]{1,0:T(8,128)(2,1)S(1)}, bf16[144,384]{1,0:T(8,128)(2,1)S(1)}, u32[]{:S(2)}, u32[]{:S(2)}) collective-permute-start(bf16[144,384]{1,0:T(8,128)(2,1)S(1)} %get-tuple-element.45), channel_id=1, source_target_pairs={{0,12},{4,0},{8,4},{12,8},{1,13},{5,1},{9,5},{13,9},{2,14},{6,2},{... | collective-permute-start | bytes 331784 | tf_op jit(solution)/shard_map/ppermute | solution.py:326
  46.4 5.1 %collective-permute-start.10 = (f32[4,8,128]{2,1,0:T(8,128)S(1)}, f32[4,8,128]{2,1,0:T(8,128)S(1)}, u32[]{:S(2)}, u32[]{:S(2)}) collective-permute-start(f32[4,8,128]{2,1,0:T(8,128)S(1)} %get-tuple-element.51.l0), channel_id=1, source_target_pairs={{0,4},{4,8},{8,12},{12,0},{1,5},{5,9},{9,13},{13,1},{2,6},{6,10},{... | collective-permute-start | bytes 49160 | tf_op jit(solution)/shard_map/ppermute | solution.py:326
  46.5 5.0 %collective-permute-start.11 = (f32[4,8,128]{2,1,0:T(8,128)S(1)}, f32[4,8,128]{2,1,0:T(8,128)S(1)}, u32[]{:S(2)}, u32[]{:S(2)}) collective-permute-start(f32[4,8,128]{2,1,0:T(8,128)S(1)} %get-tuple-element.51.l0), channel_id=1, source_target_pairs={{0,8},{4,12},{8,0},{12,4},{1,9},{5,13},{9,1},{13,5},{2,10},{6,14},... | collective-permute-start | bytes 49160 | tf_op jit(solution)/shard_map/ppermute | solution.py:326
  48.3 3.3 %collective-permute-start.12 = (f32[4,8,128]{2,1,0:T(8,128)S(1)}, f32[4,8,128]{2,1,0:T(8,128)S(1)}, u32[]{:S(2)}, u32[]{:S(2)}) collective-permute-start(f32[4,8,128]{2,1,0:T(8,128)S(1)} %get-tuple-element.51.l0), channel_id=1, source_target_pairs={{0,12},{4,0},{8,4},{12,8},{1,13},{5,1},{9,5},{13,9},{2,14},{6,2},{... | collective-permute-start | bytes 49160 | tf_op jit(solution)/shard_map/ppermute | solution.py:326
  53.3 5.2 %collective-permute-start.13 = (bf16[33,32,256]{2,1,0:T(8,128)(2,1)S(1)}, bf16[33,32,256]{2,1,0:T(8,128)(2,1)S(1)}, u32[]{:S(2)}, u32[]{:S(2)}) collective-permute-start(bf16[33,32,256]{2,1,0:T(8,128)(2,1)S(1)} %get-tuple-element.60), channel_id=1, source_target_pairs={{0,1},{1,0},{2,3},{3,2},{4,5},{5,4},{6,7},{7,6},{8,9},{9,8},{10,11... | collective-permute-start | bytes 1622024 | tf_op jit(solution)/shard_map/ppermute | solution.py:326
  58.7 4.8 %collective-permute-start.14 = (bf16[4,2,32,256]{3,2,1,0:T(8,128)(2,1)S(1)}, bf16[4,2,32,256]{3,2,1,0:T(8,128)(2,1)S(1)}, u32[]{:S(2)}, u32[]{:S(2)}) collective-permute-start(bf16[4,2,32,256]{3,2,1,0:T(8,128)(2,1)S(1)} %get-tuple-element.63), channel_id=1, source_target_pairs={{0,48},{16,0},{32,16},{48,32},{1,49},{17,1},{33,17},{49,33},{2,50}... | collective-permute-start | bytes 393224 | tf_op jit(solution)/shard_map/ppermute | solution.py:326
  58.8 6.3 %collective-permute-start.15 = (bf16[4,2,32,256]{3,2,1,0:T(8,128)(2,1)S(1)}, bf16[4,2,32,256]{3,2,1,0:T(8,128)(2,1)S(1)}, u32[]{:S(2)}, u32[]{:S(2)}) collective-permute-start(bf16[4,2,32,256]{3,2,1,0:T(8,128)(2,1)S(1)} %get-tuple-element.64), channel_id=1, source_target_pairs={{0,32},{16,48},{32,0},{48,16},{1,33},{17,49},{33,1},{49,17},{2,34}... | collective-permute-start | bytes 393224 | tf_op jit(solution)/shard_map/ppermute | solution.py:326
  60.9 7.3 %collective-permute-start.16 = (bf16[4,2,32,256]{3,2,1,0:T(8,128)(2,1)S(1)}, bf16[4,2,32,256]{3,2,1,0:T(8,128)(2,1)S(1)}, u32[]{:S(2)}, u32[]{:S(2)}) collective-permute-start(bf16[4,2,32,256]{3,2,1,0:T(8,128)(2,1)S(1)} %get-tuple-element.65), channel_id=1, source_target_pairs={{0,16},{16,32},{32,48},{48,0},{1,17},{17,33},{33,49},{49,1},{2,18}... | collective-permute-start | bytes 393224 | tf_op jit(solution)/shard_map/ppermute | solution.py:326
  69.0 16.8 %all-to-all-start.1 = ((bf16[32,8,384]{2,1,0:T(8,128)(2,1)}), bf16[32,8,384]{2,1,0:T(8,128)(2,1)S(1)}, u32[]{:S(2)}, u32[]{:S(2)}) async-start(bf16[32,8,384]{2,1,0:T(8,128)(2,1)} %bitcast.9), calls=%async_computation.1 | async-start | bytes 393216 | tf_op jit(solution)/shard_map/all_to_all | solution.py:433
  72.8 5.3 %collective-permute-start.17 = (bf16[128,384]{1,0:T(8,128)(2,1)S(1)}, bf16[128,384]{1,0:T(8,128)(2,1)S(1)}, u32[]{:S(2)}, u32[]{:S(2)}) collective-permute-start(bf16[128,384]{1,0:T(8,128)(2,1)S(1)} %get-tuple-element.69), channel_id=1, source_target_pairs={{0,12},{4,0},{8,4},{12,8},{1,13},{5,1},{9,5},{13,9},{2,14},{6,2},{... | collective-permute-start | bytes 294920 | tf_op jit(solution)/shard_map/ppermute | solution.py:326
  75.4 5.9 %collective-permute-start.18 = (bf16[128,384]{1,0:T(8,128)(2,1)S(1)}, bf16[128,384]{1,0:T(8,128)(2,1)S(1)}, u32[]{:S(2)}, u32[]{:S(2)}) collective-permute-start(bf16[128,384]{1,0:T(8,128)(2,1)S(1)} %get-tuple-element.70), channel_id=1, source_target_pairs={{0,8},{4,12},{8,0},{12,4},{1,9},{5,13},{9,1},{13,5},{2,10},{6,14},... | collective-permute-start | bytes 294920 | tf_op jit(solution)/shard_map/ppermute | solution.py:326
  75.9 9.0 %collective-permute-start.19 = (bf16[128,384]{1,0:T(8,128)(2,1)S(1)}, bf16[128,384]{1,0:T(8,128)(2,1)S(1)}, u32[]{:S(2)}, u32[]{:S(2)}) collective-permute-start(bf16[128,384]{1,0:T(8,128)(2,1)S(1)} %get-tuple-element.71), channel_id=1, source_target_pairs={{0,4},{4,8},{8,12},{12,0},{1,5},{5,9},{9,13},{13,1},{2,6},{6,10},{... | collective-permute-start | bytes 294920 | tf_op jit(solution)/shard_map/ppermute | solution.py:326

commit v3 on v1

--- a/solution.py
+++ b/solution.py
@@ -31,17 +31,18 @@
     return d // 64, (d // 16) % 4, (d // 4) % 4, (d // 2) % 2, d % 2
 
 
-def keys_kernel(keys, values, kv_out, kb, vb, sems):
-    copies = [pltpu.make_async_copy(keys, kb, sems.at[0]), pltpu.make_async_copy(values, vb, sems.at[1])]
+def keys_kernel(keys, values, kv_out, sems):
+    copies = []
+    for g in range(4):
+        cols = pl.ds(g * HEAD_WIDTH, HEAD_WIDTH)
+        for z in range(8):
+            for part, src in enumerate((keys, values)):
+                to = kv_out.at[g, z, :, pl.ds(part * HEAD_WIDTH, HEAD_WIDTH)]
+                copies.append(pltpu.make_async_copy(src.at[:, cols], to, sems.at[len(copies)]))
     for copy in copies:
         copy.start()
     for copy in copies:
         copy.wait()
-    for g in range(4):
-        cols = slice(g * HEAD_WIDTH, (g + 1) * HEAD_WIDTH)
-        both = jnp.concatenate([kb[:, cols], vb[:, cols]], axis=1)
-        for z in range(8):
-            kv_out[g, z] = both
 
 
 def queries_kernel(did, labels, mask, queries, w, seg, q0, q1, q2, q3, w_out, seg_out, lb, mb, sems):
@@ -117,6 +118,7 @@
         part = times_t(diffs16, kv_out[rows, HEAD_WIDTH:])
         high, low = halves(part[:8] + part[8:])
         u_rows[:, rows] = jnp.concatenate([high + ones, low], axis=0).astype(BF16)
+    plog[...] = jnp.zeros_like(plog)
     j = zh * 2 + c
     r = lax.broadcasted_iota(jnp.int32, (BLOCK, BLOCK), 0)
     from_x = jnp.bitwise_and(x + 4 - jnp.right_shift(r, 5), 3)
@@ -160,7 +162,7 @@
         inv_out[ys] = jnp.broadcast_to(inv, (8, WIDE))
         delta_out[ys] = jnp.broadcast_to(delta, (8, WIDE))
         lg = delta[:, :BLOCK] + delta[:, BLOCK : 2 * BLOCK] + delta[:, 2 * BLOCK :]
-        plog[(y - ys + 4) % 4] = jnp.broadcast_to(lg, (8, BLOCK))
+        plog[pl.ds((y - ys + 4) % 4, 1), :] = lg
 
 
 def middle_kernel(did, w, p, delta, q, kv, g_out, dq_out, qt_out, kt, u):
@@ -215,7 +217,7 @@
         src = (y - k + 4) % 4
         for m in range(4):
             ys = (y - m + 4) % 4
-            lgs[src, ys] = ref[(m - k) % 4]
+            lgs[src, ys] = jnp.broadcast_to(ref[(m - k) % 4 : (m - k) % 4 + 1, :], (8, BLOCK))
     for k, ref in enumerate((g0, g1, g2, g3)):
         labs[(y - k + 4) % 4] = ref[BLOCK:, :256].astype(F32)[8:16, :]
     wt = jnp.concatenate([jnp.broadcast_to(head_diff(w, y, h), (BLOCK, HEAD_WIDTH)).T for h in range(GROUP)], axis=1)
@@ -288,8 +290,15 @@
     lax.fori_loop(0, 4, add, 0)
 
 
-def finish_kernel(did, pieces, d0, d1, d2, d3, qg, gk, gv, hg, loss):
-    zl, _, y, _, _ = coords(did)
+def rows_kernel(did, d0, d1, d2, d3, qg):
+    _, _, y, _, _ = coords(did)
+    for k, d in enumerate((d0, d1, d2, d3)):
+        wide = pl.ds(pl.multiple_of(((y + k) % 4) * WIDE, HEAD_WIDTH), WIDE)
+        qg[:, wide] = d[...].astype(F32)
+
+
+def finish_kernel(did, pieces, gk, gv, hg, loss):
+    zl, _, _, _, _ = coords(did)
     for g in range(4):
         v = jnp.zeros((8, 256), F32)
         for k in range(2):
@@ -306,9 +315,6 @@
             hg[1:2, cols] = -v[h : h + 1]
         if g == 0:
             loss[0] = jnp.sum(v[GROUP : GROUP + 1]) * (1.0 / TOKENS)
-    for k, d in enumerate((d0, d1, d2, d3)):
-        wide = pl.ds(pl.multiple_of(((y + k) % 4) * WIDE, HEAD_WIDTH), WIDE)
-        qg[:, wide] = d[...].astype(F32)
 
 
 def shift(v, axis, size, k):
@@ -337,10 +343,7 @@
 def per_device(queries, keys, values, head, segments, label_mask, labels):
     did = lax.axis_index(("zl", "x", "y", "zh", "c")).astype(jnp.int32).reshape(1)
     (copies,) = call(
-        keys_kernel,
-        [like((4, 8, 8, 256), BF16)],
-        [HBM] * 2,
-        scratch=[pltpu.VMEM((8, 512), BF16), pltpu.VMEM((8, 512), BF16), pltpu.SemaphoreType.DMA((2,))],
+        keys_kernel, [like((4, 8, 8, 256), BF16)], [HBM] * 2, [HBM], scratch=[pltpu.SemaphoreType.DMA((64,))]
     )(in_hbm(keys), in_hbm(values))
     own = lax.all_to_all(copies.reshape(32, 8, 256), YZ_AXES, 0, 0, tiled=True).reshape(4, 2, 32, 256)
     *packs, w, seg = call(
@@ -369,7 +372,7 @@
     plog, p, inv, delta, q, kv = call(
         forward_kernel,
         [
-            like((4, 8, BLOCK), F32),
+            like((8, BLOCK), F32),
             like((7 * CHUNK, WIDE), BF16),
             like((4, 8, WIDE), F32),
             like((4, 8, WIDE), F32),
@@ -379,7 +382,9 @@
         [SMEM] + [VMEM] * 14,
         scratch=[pltpu.VMEM((3 * CHUNK, WIDE), F32), pltpu.VMEM((16, TOKENS), BF16)],
     )(did, seg, w, *packs, *over_x, *over_c)
-    logs = [plog] + [shift(plog, "y", 4, k) for k in range(1, 4)]
+    logs = [plog]
+    for k in range(1, 4):
+        logs.append(shift(plog, "y", 4, k))
     g, dqt, qt = call(
         middle_kernel,
         [
@@ -410,25 +415,22 @@
         scratch=[pltpu.VMEM((4, BLOCK, WIDE), BF16), pltpu.VMEM((8, TOKENS), F32)],
     )(did, p, g, qf, at16, f, loss_rows, kv, dqt)
     by_x = call(core_kernel, [like((4, 2, 32, 256), BF16)] * 4, [VMEM] * 2)(own_d, far)
-    got = [by_x[0]] + [shift(by_x[k], "x", 4, -k) for k in range(1, 4)]
+    got = [by_x[0]]
+    for k in range(1, 4):
+        got.append(shift(by_x[k], "x", 4, -k))
     hg_far = shift(hg, "c", 2, 1)
     (by_z,) = call(x_kernel, [like((4, 2, 4, 8, WIDE), BF16)], [VMEM] * 6)(*got, hg, hg_far)
     pieces = lax.all_to_all(by_z.reshape(32, 8, WIDE), YZ_AXES, 0, 0, tiled=True).reshape(4, 2, 4, 8, WIDE)
     back = [dq[0]]
     for k in range(1, 4):
         back.append(shift(dq[k], "y", 4, -k))
-    query_gradient, grad_keys, grad_values, head_t, loss = call(
+    (query_gradient,) = call(rows_kernel, [like((BLOCK, 4 * WIDE), F32)], [SMEM] + [VMEM] * 4)(did, *back)
+    grad_keys, grad_values, head_t, loss = call(
         finish_kernel,
-        [
-            like((BLOCK, 4 * WIDE), F32),
-            like((8, 512), F32),
-            like((8, 512), F32),
-            like((2, 4 * WIDE), F32),
-            like((1,), F32),
-        ],
-        [SMEM] + [VMEM] * 5,
-        [VMEM] * 4 + [SMEM],
-    )(did, pieces, *back)
+        [like((8, 512), F32), like((8, 512), F32), like((2, 4 * WIDE), F32), like((1,), F32)],
+        [SMEM, VMEM],
+        [VMEM] * 3 + [SMEM],
+    )(did, pieces)
     return loss, query_gradient[None], grad_keys, grad_values, head_t.T[None]
 
 

time: 87.7 us -> 89 us (1.015)
  Pallas kernels: 12 us -> 13.5 us
    pallas_call x3 -> x4, Pallas kernels: 4.82 us -> 6.33 us  [the longest x1 3.1 us: per_device(): call(forward_kernel, [like((8, BLOCK), F32), like((7 * CHUNK, WIDE), BF16...]
  transfers between devices with their start and end apart: 22 -> 22, of which waited for: 11 -> 11; matrix products, arithmetic and copies ran while one was open for 0% -> 0% of each run, Pallas kernels for 6% -> 7%
where the time goes in v3:
time: 89 us; the launch traced here: 88.7 us
  starting transfers between devices  27.5 us (31%)
  waiting for transfers between devices  25.8 us (29%)
  blocking collectives  21 us (24%)
  Pallas kernels  13.5 us (15%)
  between operations  0.89 us (1%)
    ppermute x21, waiting for transfers between devices, shift(): return lax.ppermute(v, axis, [(i, (i + k) % size) for i in range(size)])  25.8 us
    ppermute x21, starting transfers between devices, shift(): return lax.ppermute(v, axis, [(i, (i + k) % size) for i in range(size)])  23.3 us
    all_to_all x1, blocking collectives, per_device(): lax.all_to_all(copies.reshape(32, 8, 256), YZ_AXES, 0, 0, tiled=True)  21 us
    all_to_all x1, starting transfers between devices, per_device(): lax.all_to_all(by_z.reshape(32, 8, WIDE), YZ_AXES, 0, 0, tiled=True)  4.25 us
    pallas_call x1, Pallas kernels, per_device(): call(forward_kernel, [like((8, BLOCK), F32), like((7 * CHUNK, WIDE), BF16...  3.1 us
    pallas_call x1, Pallas kernels, per_device(): call(middle_kernel, [like((7 * CHUNK, WIDE), BF16), like((4, HEAD_WIDTH,...  2.33 us
  transfers between devices with their start and end apart: 22, of which 11 were waited for; matrix products, arithmetic and copies ran while one was open for 0% of the time, Pallas kernels for 7%

profile of v3, /device:TPU:1, one launch (start us, length us, event | category | flops | bytes accessed | tf_op | source)
XLA Modules:
  0.0 88.7 jit_solution(8283148949622176269)
XLA Ops:
  0.6 1.6 %shard_map.111 = bf16[4,8,8,256]{3,2,1,0:T(8,128)(2,1)S(1)} custom-call(bf16[8,512]{1,0:T(8,128)(2,1)} %keys.1, bf16[8,512]{1,0:T(8,128)(2,1)} %values.1), custom_call_target="tpu_custom_call" | custom-call | tf_op jit(solution)/shard_map/pallas_call | solution.py:345
  2.3 21.0 %all_to_all.10 = bf16[32,8,256]{2,1,0:T(8,128)(2,1)S(1)} all-to-all(bf16[32,8,256]{2,1,0:T(8,128)(2,1)S(1)} %bitcast.17), channel_id=1, replica_groups=mesh['zl'=4,'x'=4,'y'=4,'zh'=2,'c'=2] {'y','zh','zl'}, dimensions={0} | all-to-all | bytes 262144 | tf_op jit(solution)/shard_map/all_to_all | solution.py:348
  23.2 2.5 %collective-permute-start.5 = (bf16[4,2,32,256]{3,2,1,0:T(8,128)(2,1)S(1)}, bf16[4,2,32,256]{3,2,1,0:T(8,128)(2,1)S(1)}, u32[]{:S(2)}, u32[]{:S(2)}) collective-permute-start(bf16[4,2,32,256]{3,2,1,0:T(8,128)(2,1)S(1)} %bitcast.18), channel_id=1, source_target_pairs={{0,48},{16,0},{32,16},{48,32},{1,49},{17,1},{33,17},{49,33},{2,50}... | collective-permute-start | bytes 393224 | tf_op jit(solution)/shard_map/ppermute | solution.py:321
  26.2 0.6 collective-permute-start.3
  26.9 1.2 %shard_map.110 = (bf16[144,384]{1,0:T(8,128)(2,1)S(1)}, bf16[144,384]{1,0:T(8,128)(2,1)S(1)}, bf16[144,384]{1,0:T(8,128)(2,1)S(1)}, bf16[144,384]{1,0:T(8,128)(2...) custom-call(s32[1]{0:T(128)} %bitcast.did, s32[1,128]{1,0:T(1,128)} %bitcast.27, s32[1,128]{1,0:T(1,128)} %bitcast.28, ...), custom_call_target="tpu_custom_call" | custom-call | tf_op jit(solution)/shard_map/pallas_call | solution.py:349
  28.4 1.7 %collective-permute-start.1 = (bf16[144,384]{1,0:T(8,128)(2,1)S(1)}, bf16[144,384]{1,0:T(8,128)(2,1)S(1)}, u32[]{:S(2)}, u32[]{:S(2)}) collective-permute-start(bf16[144,384]{1,0:T(8,128)(2,1)S(1)} %get-tuple-element.43), channel_id=1, source_target_pairs={{0,8},{4,12},{8,0},{12,4},{1,9},{5,13},{9,1},{13,5},{2,10},{6,14},... | collective-permute-start | bytes 331784 | tf_op jit(solution)/shard_map/ppermute | solution.py:321
  30.2 4.2 %collective-permute-done.q1.g1 = bf16[144,384]{1,0:T(8,128)(2,1)S(1)} collective-permute-done((bf16[144,384]{1,0:T(8,128)(2,1)S(1)}, bf16[144,384]{1,0:T(8,128)(2,1)S(1)}, u32[]{:S(2)}, u32[]{:S(2)}) %collective-permute-start) | collective-permute-done | bytes 110624 | tf_op jit(solution)/shard_map/ppermute | solution.py:321
  34.4 3.8 %collective-permute-start.6 = (bf16[4,2,32,256]{3,2,1,0:T(8,128)(2,1)S(1)}, bf16[4,2,32,256]{3,2,1,0:T(8,128)(2,1)S(1)}, u32[]{:S(2)}, u32[]{:S(2)}) collective-permute-start(bf16[4,2,32,256]{3,2,1,0:T(8,128)(2,1)S(1)} %bitcast.21), channel_id=1, source_target_pairs={{0,1},{1,0},{2,3},{3,2},{4,5},{5,4},{6,7},{7,6},{8,9},{9,8},{10,11... | collective-permute-start | bytes 393224 | tf_op jit(solution)/shard_map/ppermute | solution.py:321
  38.8 4.2 %collective-permute-done.2.q3.g3 = bf16[144,384]{1,0:T(8,128)(2,1)S(1)} collective-permute-done((bf16[144,384]{1,0:T(8,128)(2,1)S(1)}, bf16[144,384]{1,0:T(8,128)(2,1)S(1)}, u32[]{:S(2)}, u32[]{:S(2)}) %collective-permute-start.2) | collective-permute-done | bytes 110624 | tf_op jit(solution)/shard_map/ppermute | solution.py:321
  43.0 3.1 %shard_map.112 = (f32[8,128]{1,0:T(8,128)S(1)}, bf16[3584,384]{1,0:T(8,128)(2,1)S(1)}, f32[4,8,384]{2,1,0:T(8,128)S(1)}, f32[4,8,384]{2,1,0:T(8,128)S(1)}, bf16[...) custom-call(s32[1]{0:T(128)} %bitcast.did, s32[1,2048]{1,0:T(1,128)S(1)} %get-tuple-element.39.seg, ...), custom_call_target="tpu_custom_call" | custom-call | tf_op jit(solution)/shard_map/pallas_call | solution.py:372
  46.1 0.7 collective-permute-start.12
  47.7 2.3 %shard_map.113 = (bf16[3584,384]{1,0:T(8,128)(2,1)S(1)}, f32[4,128,384]{2,1,0:T(8,128)S(1)}, bf16[4,128,384]{2,1,0:T(8,128)(2,1)S(1)}) custom-call(s32[1]{0:T(128)} %bitcast.did, f32[2,1536]{1,0:T(2,128)S(1)} %get-tuple-element.40.w, bf16[3584,384]{1,0:T(8,128)(2,1)S(1)} %get-tuple-element.45.p, f32[4,8,384]{2,1,0:T(8,128)S(1)} %get-tuple-element.46.delta, ...), custom_call_target="tpu_custom_call" | custom-call | tf_op jit(solution)/shard_map/pallas_call | solution.py:388
  50.0 0.8 collective-permute-done.11.l2
  51.0 1.0 %shard_map.114 = (bf16[4,4,2,32,256]{4,3,2,1,0:T(8,128)(2,1)S(1)}, f32[4,8,384]{2,1,0:T(8,128)S(1)}, bf16[4,128,384]{2,1,0:T(8,128)(2,1)S(1)}, bf16[4,128,384]{2,1,0:T(8,128)(2,1)S(1)}, f32[8,128]{1,0:T(8,128)S(1)}) custom-call(s32[1]{0:T(128)} %bitcast.did, f32[2,1536]{1,0:T(2,128)S(1)} %get-tuple-element.40.w, f32[8,128]{1,0:T(8,128)S(1)} %get-tuple-element.50.l0, ...), custom_call_target="tpu_custom_call" | custom-call | tf_op jit(solution)/shard_map/pallas_call | solution.py:398
  52.1 3.8 %collective-permute-start.13 = (bf16[4,4,2,32,256]{4,3,2,1,0:T(8,128)(2,1)S(1)}, bf16[4,4,2,32,256]{4,3,2,1,0:T(8,128)(2,1)S(1)}, u32[]{:S(2)}, u32[]{:S(2)}) collective-permute-start(bf16[4,4,2,32,256]{4,3,2,1,0:T(8,128)(2,1)S(1)} %get-tuple-element.59), channel_id=1, source_target_pairs={{0,1},{1,0},{2,3},{3,2},{4,5},{5,4},{6,7},{7,6},{8,9},{9,8},{10,11... | collective-permute-start | bytes 1572872 | tf_op jit(solution)/shard_map/ppermute | solution.py:321
  55.9 1.7 %shard_map.115 = (bf16[4,4,2,32,256]{4,3,2,1,0:T(8,128)(2,1)S(1)}, f32[8,128]{1,0:T(8,128)S(1)}, bf16[128,384]{1,0:T(8,128)(2,1)S(1)}, bf16[128,384]{1,0:T(8,128...) custom-call(s32[1]{0:T(128)} %bitcast.did, bf16[3584,384]{1,0:T(8,128)(2,1)S(1)} %get-tuple-element.45.p, ...), custom_call_target="tpu_custom_call" | custom-call | tf_op jit(solution)/shard_map/pallas_call | solution.py:411
  57.9 2.1 %collective-permute-start.14 = (bf16[4,2,32,256]{3,2,1,0:T(8,128)(2,1)S(1)}, bf16[4,2,32,256]{3,2,1,0:T(8,128)(2,1)S(1)}, u32[]{:S(2)}, u32[]{:S(2)}) collective-permute-start(bf16[4,2,32,256]{3,2,1,0:T(8,128)(2,1)S(1)} %get-tuple-element.61), channel_id=1, source_target_pairs={{0,48},{16,0},{32,16},{48,32},{1,49},{17,1},{33,17},{49,33},{2,50}... | collective-permute-start | bytes 393224 | tf_op jit(solution)/shard_map/ppermute | solution.py:321
  60.0 1.2 %collective-permute-start.15 = (bf16[4,2,32,256]{3,2,1,0:T(8,128)(2,1)S(1)}, bf16[4,2,32,256]{3,2,1,0:T(8,128)(2,1)S(1)}, u32[]{:S(2)}, u32[]{:S(2)}) collective-permute-start(bf16[4,2,32,256]{3,2,1,0:T(8,128)(2,1)S(1)} %get-tuple-element.62), channel_id=1, source_target_pairs={{0,32},{16,48},{32,0},{48,16},{1,33},{17,49},{33,1},{49,17},{2,34}... | collective-permute-start | bytes 393224 | tf_op jit(solution)/shard_map/ppermute | solution.py:321
  61.2 0.7 collective-permute-start.17
  62.0 0.8 collective-permute-done.17.hg_far
  63.0 3.2 %collective-permute-done.15.b2 = bf16[4,2,32,256]{3,2,1,0:T(8,128)(2,1)S(1)} collective-permute-done((bf16[4,2,32,256]{3,2,1,0:T(8,128)(2,1)S(1)}, bf16[4,2,32,256]{3,2,1,0:T(8,128)(2,1)S(1)}, u32[]{:S(2)}, u32[]{:S(2)}) %collective-permute-start.15) | collective-permute-done | bytes 131104 | tf_op jit(solution)/shard_map/ppermute | solution.py:321
  66.1 3.6 %collective-permute-done.16.b3 = bf16[4,2,32,256]{3,2,1,0:T(8,128)(2,1)S(1)} collective-permute-done((bf16[4,2,32,256]{3,2,1,0:T(8,128)(2,1)S(1)}, bf16[4,2,32,256]{3,2,1,0:T(8,128)(2,1)S(1)}, u32[]{:S(2)}, u32[]{:S(2)}) %collective-permute-start.16) | collective-permute-done | bytes 131104 | tf_op jit(solution)/shard_map/ppermute | solution.py:321
  69.7 0.8 shard_map.117
  70.5 4.3 %all-to-all-start.1 = ((bf16[32,8,384]{2,1,0:T(8,128)(2,1)}), bf16[32,8,384]{2,1,0:T(8,128)(2,1)S(1)}, u32[]{:S(2)}, u32[]{:S(2)}) async-start(bf16[32,8,384]{2,1,0:T(8,128)(2,1)} %bitcast.9), calls=%async_computation.1 | async-start | bytes 393216 | tf_op jit(solution)/shard_map/all_to_all | solution.py:423
  74.8 2.6 %collective-permute-start.18 = (bf16[128,384]{1,0:T(8,128)(2,1)S(1)}, bf16[128,384]{1,0:T(8,128)(2,1)S(1)}, u32[]{:S(2)}, u32[]{:S(2)}) collective-permute-start(bf16[128,384]{1,0:T(8,128)(2,1)S(1)} %get-tuple-element.67), channel_id=1, source_target_pairs={{0,12},{4,0},{8,4},{12,8},{1,13},{5,1},{9,5},{13,9},{2,14},{6,2},{... | collective-permute-start | bytes 294920 | tf_op jit(solution)/shard_map/ppermute | solution.py:321
  77.3 0.5 collective-permute-start.19
  77.9 0.6 collective-permute-start.20
  78.4 2.0 %collective-permute-done.18.d1 = bf16[128,384]{1,0:T(8,128)(2,1)S(1)} collective-permute-done((bf16[128,384]{1,0:T(8,128)(2,1)S(1)}, bf16[128,384]{1,0:T(8,128)(2,1)S(1)}, u32[]{:S(2)}, u32[]{:S(2)}) %collective-permute-start.18) | collective-permute-done | bytes 98336 | tf_op jit(solution)/shard_map/ppermute | solution.py:321
  80.5 2.7 %collective-permute-done.19.d2 = bf16[128,384]{1,0:T(8,128)(2,1)S(1)} collective-permute-done((bf16[128,384]{1,0:T(8,128)(2,1)S(1)}, bf16[128,384]{1,0:T(8,128)(2,1)S(1)}, u32[]{:S(2)}, u32[]{:S(2)}) %collective-permute-start.19) | collective-permute-done | bytes 98336 | tf_op jit(solution)/shard_map/ppermute | solution.py:321
  83.2 3.8 %collective-permute-done.20.d3 = bf16[128,384]{1,0:T(8,128)(2,1)S(1)} collective-permute-done((bf16[128,384]{1,0:T(8,128)(2,1)S(1)}, bf16[128,384]{1,0:T(8,128)(2,1)S(1)}, u32[]{:S(2)}, u32[]{:S(2)}) %collective-permute-start.20) | collective-permute-done | bytes 98336 | tf_op jit(solution)/shard_map/ppermute | solution.py:321
  87.0 0.9 %shard_map.119 = f32[128,1536]{1,0:T(8,128)} custom-call(s32[1]{0:T(128)} %bitcast.did, bf16[128,384]{1,0:T(8,128)(2,1)S(1)} %get-tuple-element.66.d0, bf16[128,384]{1,0:T(8,128)(2,1)S(1)} %collective-permute-done.18.d1, bf16[128,384]{1,0:T(8,128)(2,1)S(1)} %collective-permute-done.19.d2, bf16[128,384]{1,0:T(8,128)(2,1)S(1)} %collective-permute-done.20.d3), custom_call_target="tpu_custom_call" | custom-call | tf_op jit(solution)/shard_map/pallas_call | solution.py:427
  87.9 0.6 shard_map.118
  (23 shorter events, 3.1 us)
Async XLA Ops:
  23.2 14.9 %collective-permute-start.5 = (bf16[4,2,32,256]{3,2,1,0:T(8,128)(2,1)S(1)}, bf16[4,2,32,256]{3,2,1,0:T(8,128)(2,1)S(1)}, u32[]{:S(2)}, u32[]{:S(2)}) collective-permute-start(bf16[4,2,32,256]{3,2,1,0:T(8,128)(2,1)S(1)} %bitcast.18), channel_id=1, source_target_pairs={{0,48},{16,0},{32,16},{48,32},{1,49},{17,1},{33,17},{49,33},{2,50}... | collective-permute-start | bytes 393224 | tf_op jit(solution)/shard_map/ppermute | solution.py:321
  25.7 12.5 %collective-permute-start.4 = (bf16[4,2,32,256]{3,2,1,0:T(8,128)(2,1)S(1)}, bf16[4,2,32,256]{3,2,1,0:T(8,128)(2,1)S(1)}, u32[]{:S(2)}, u32[]{:S(2)}) collective-permute-start(bf16[4,2,32,256]{3,2,1,0:T(8,128)(2,1)S(1)} %bitcast.19), channel_id=1, source_target_pairs={{0,32},{16,48},{32,0},{48,16},{1,33},{17,49},{33,1},{49,17},{2,34}... | collective-permute-start | bytes 393224 | tf_op jit(solution)/shard_map/ppermute | solution.py:321
  26.2 12.4 %collective-permute-start.3 = (bf16[4,2,32,256]{3,2,1,0:T(8,128)(2,1)S(1)}, bf16[4,2,32,256]{3,2,1,0:T(8,128)(2,1)S(1)}, u32[]{:S(2)}, u32[]{:S(2)}) collective-permute-start(bf16[4,2,32,256]{3,2,1,0:T(8,128)(2,1)S(1)} %bitcast.20), channel_id=1, source_target_pairs={{0,16},{16,32},{32,48},{48,0},{1,17},{17,33},{33,49},{49,1},{2,18}... | collective-permute-start | bytes 393224 | tf_op jit(solution)/shard_map/ppermute | solution.py:321
  28.0 6.4 %collective-permute-start = (bf16[144,384]{1,0:T(8,128)(2,1)S(1)}, bf16[144,384]{1,0:T(8,128)(2,1)S(1)}, u32[]{:S(2)}, u32[]{:S(2)}) collective-permute-start(bf16[144,384]{1,0:T(8,128)(2,1)S(1)} %get-tuple-element.42), channel_id=1, source_target_pairs={{0,4},{4,8},{8,12},{12,0},{1,5},{5,9},{9,13},{13,1},{2,6},{6,10},{... | collective-permute-start | bytes 331784 | tf_op jit(solution)/shard_map/ppermute | solution.py:321
  28.4 10.3 %collective-permute-start.1 = (bf16[144,384]{1,0:T(8,128)(2,1)S(1)}, bf16[144,384]{1,0:T(8,128)(2,1)S(1)}, u32[]{:S(2)}, u32[]{:S(2)}) collective-permute-start(bf16[144,384]{1,0:T(8,128)(2,1)S(1)} %get-tuple-element.43), channel_id=1, source_target_pairs={{0,8},{4,12},{8,0},{12,4},{1,9},{5,13},{9,1},{13,5},{2,10},{6,14},... | collective-permute-start | bytes 331784 | tf_op jit(solution)/shard_map/ppermute | solution.py:321
  34.4 8.6 %collective-permute-start.6 = (bf16[4,2,32,256]{3,2,1,0:T(8,128)(2,1)S(1)}, bf16[4,2,32,256]{3,2,1,0:T(8,128)(2,1)S(1)}, u32[]{:S(2)}, u32[]{:S(2)}) collective-permute-start(bf16[4,2,32,256]{3,2,1,0:T(8,128)(2,1)S(1)} %bitcast.21), channel_id=1, source_target_pairs={{0,1},{1,0},{2,3},{3,2},{4,5},{5,4},{6,7},{7,6},{8,9},{9,8},{10,11... | collective-permute-start | bytes 393224 | tf_op jit(solution)/shard_map/ppermute | solution.py:321
  38.2 4.8 %collective-permute-start.9 = (bf16[4,2,32,256]{3,2,1,0:T(8,128)(2,1)S(1)}, bf16[4,2,32,256]{3,2,1,0:T(8,128)(2,1)S(1)}, u32[]{:S(2)}, u32[]{:S(2)}) collective-permute-start(bf16[4,2,32,256]{3,2,1,0:T(8,128)(2,1)S(1)} %collective-permute-done.5.rest_3_), channel_id=1, source_target_pairs={{0,1},{1,0},{2,3},{3,2},{4,5},{5,4},{6,7},{7,6},{8,9},{9,8},{10,11... | collective-permute-start | bytes 393224 | tf_op jit(solution)/shard_map/ppermute | solution.py:321
  38.2 4.8 %collective-permute-start.8 = (bf16[4,2,32,256]{3,2,1,0:T(8,128)(2,1)S(1)}, bf16[4,2,32,256]{3,2,1,0:T(8,128)(2,1)S(1)}, u32[]{:S(2)}, u32[]{:S(2)}) collective-permute-start(bf16[4,2,32,256]{3,2,1,0:T(8,128)(2,1)S(1)} %collective-permute-done.4.rest_2_), channel_id=1, source_target_pairs={{0,1},{1,0},{2,3},{3,2},{4,5},{5,4},{6,7},{7,6},{8,9},{9,8},{10,11... | collective-permute-start | bytes 393224 | tf_op jit(solution)/shard_map/ppermute | solution.py:321
  38.7 4.3 %collective-permute-start.7 = (bf16[4,2,32,256]{3,2,1,0:T(8,128)(2,1)S(1)}, bf16[4,2,32,256]{3,2,1,0:T(8,128)(2,1)S(1)}, u32[]{:S(2)}, u32[]{:S(2)}) collective-permute-start(bf16[4,2,32,256]{3,2,1,0:T(8,128)(2,1)S(1)} %collective-permute-done.3.rest_1_), channel_id=1, source_target_pairs={{0,1},{1,0},{2,3},{3,2},{4,5},{5,4},{6,7},{7,6},{8,9},{9,8},{10,11... | collective-permute-start | bytes 393224 | tf_op jit(solution)/shard_map/ppermute | solution.py:321
  38.8 4.2 %collective-permute-start.2 = (bf16[144,384]{1,0:T(8,128)(2,1)S(1)}, bf16[144,384]{1,0:T(8,128)(2,1)S(1)}, u32[]{:S(2)}, u32[]{:S(2)}) collective-permute-start(bf16[144,384]{1,0:T(8,128)(2,1)S(1)} %get-tuple-element.44), channel_id=1, source_target_pairs={{0,12},{4,0},{8,4},{12,8},{1,13},{5,1},{9,5},{13,9},{2,14},{6,2},{... | collective-permute-start | bytes 331784 | tf_op jit(solution)/shard_map/ppermute | solution.py:321
  46.1 3.9 %collective-permute-start.12 = (f32[8,128]{1,0:T(8,128)S(1)}, f32[8,128]{1,0:T(8,128)S(1)}, u32[]{:S(2)}, u32[]{:S(2)}) collective-permute-start(f32[8,128]{1,0:T(8,128)S(1)} %get-tuple-element.50.l0), channel_id=1, source_target_pairs={{0,12},{4,0},{8,4},{12,8},{1,13},{5,1},{9,5},{13,9},{2,14},{6,2},{... | collective-permute-start | bytes 12296 | tf_op jit(solution)/shard_map/ppermute | solution.py:321
  46.8 4.0 %collective-permute-start.11 = (f32[8,128]{1,0:T(8,128)S(1)}, f32[8,128]{1,0:T(8,128)S(1)}, u32[]{:S(2)}, u32[]{:S(2)}) collective-permute-start(f32[8,128]{1,0:T(8,128)S(1)} %get-tuple-element.50.l0), channel_id=1, source_target_pairs={{0,8},{4,12},{8,0},{12,4},{1,9},{5,13},{9,1},{13,5},{2,10},{6,14},... | collective-permute-start | bytes 12296 | tf_op jit(solution)/shard_map/ppermute | solution.py:321
  47.2 3.8 %collective-permute-start.10 = (f32[8,128]{1,0:T(8,128)S(1)}, f32[8,128]{1,0:T(8,128)S(1)}, u32[]{:S(2)}, u32[]{:S(2)}) collective-permute-start(f32[8,128]{1,0:T(8,128)S(1)} %get-tuple-element.50.l0), channel_id=1, source_target_pairs={{0,4},{4,8},{8,12},{12,0},{1,5},{5,9},{9,13},{13,1},{2,6},{6,10},{... | collective-permute-start | bytes 12296 | tf_op jit(solution)/shard_map/ppermute | solution.py:321
  52.1 5.6 %collective-permute-start.13 = (bf16[4,4,2,32,256]{4,3,2,1,0:T(8,128)(2,1)S(1)}, bf16[4,4,2,32,256]{4,3,2,1,0:T(8,128)(2,1)S(1)}, u32[]{:S(2)}, u32[]{:S(2)}) collective-permute-start(bf16[4,4,2,32,256]{4,3,2,1,0:T(8,128)(2,1)S(1)} %get-tuple-element.59), channel_id=1, source_target_pairs={{0,1},{1,0},{2,3},{3,2},{4,5},{5,4},{6,7},{7,6},{8,9},{9,8},{10,11... | collective-permute-start | bytes 1572872 | tf_op jit(solution)/shard_map/ppermute | solution.py:321
  57.9 5.1 %collective-permute-start.14 = (bf16[4,2,32,256]{3,2,1,0:T(8,128)(2,1)S(1)}, bf16[4,2,32,256]{3,2,1,0:T(8,128)(2,1)S(1)}, u32[]{:S(2)}, u32[]{:S(2)}) collective-permute-start(bf16[4,2,32,256]{3,2,1,0:T(8,128)(2,1)S(1)} %get-tuple-element.61), channel_id=1, source_target_pairs={{0,48},{16,0},{32,16},{48,32},{1,49},{17,1},{33,17},{49,33},{2,50}... | collective-permute-start | bytes 393224 | tf_op jit(solution)/shard_map/ppermute | solution.py:321
  60.0 6.1 %collective-permute-start.15 = (bf16[4,2,32,256]{3,2,1,0:T(8,128)(2,1)S(1)}, bf16[4,2,32,256]{3,2,1,0:T(8,128)(2,1)S(1)}, u32[]{:S(2)}, u32[]{:S(2)}) collective-permute-start(bf16[4,2,32,256]{3,2,1,0:T(8,128)(2,1)S(1)} %get-tuple-element.62), channel_id=1, source_target_pairs={{0,32},{16,48},{32,0},{48,16},{1,33},{17,49},{33,1},{49,17},{2,34}... | collective-permute-start | bytes 393224 | tf_op jit(solution)/shard_map/ppermute | solution.py:321
  61.2 8.5 %collective-permute-start.16 = (bf16[4,2,32,256]{3,2,1,0:T(8,128)(2,1)S(1)}, bf16[4,2,32,256]{3,2,1,0:T(8,128)(2,1)S(1)}, u32[]{:S(2)}, u32[]{:S(2)}) collective-permute-start(bf16[4,2,32,256]{3,2,1,0:T(8,128)(2,1)S(1)} %get-tuple-element.63), channel_id=1, source_target_pairs={{0,16},{16,32},{32,48},{48,0},{1,17},{17,33},{33,49},{49,1},{2,18}... | collective-permute-start | bytes 393224 | tf_op jit(solution)/shard_map/ppermute | solution.py:321
  61.2 1.5 %collective-permute-start.17 = (f32[8,128]{1,0:T(8,128)S(1)}, f32[8,128]{1,0:T(8,128)S(1)}, u32[]{:S(2)}, u32[]{:S(2)}) collective-permute-start(f32[8,128]{1,0:T(8,128)S(1)} %get-tuple-element.64.hg), channel_id=1, source_target_pairs={{0,1},{1,0},{2,3},{3,2},{4,5},{5,4},{6,7},{7,6},{8,9},{9,8},{10,11... | collective-permute-start | bytes 12296 | tf_op jit(solution)/shard_map/ppermute | solution.py:321
  70.5 17.4 %all-to-all-start.1 = ((bf16[32,8,384]{2,1,0:T(8,128)(2,1)}), bf16[32,8,384]{2,1,0:T(8,128)(2,1)S(1)}, u32[]{:S(2)}, u32[]{:S(2)}) async-start(bf16[32,8,384]{2,1,0:T(8,128)(2,1)} %bitcast.9), calls=%async_computation.1 | async-start | bytes 393216 | tf_op jit(solution)/shard_map/all_to_all | solution.py:423
  74.8 5.7 %collective-permute-start.18 = (bf16[128,384]{1,0:T(8,128)(2,1)S(1)}, bf16[128,384]{1,0:T(8,128)(2,1)S(1)}, u32[]{:S(2)}, u32[]{:S(2)}) collective-permute-start(bf16[128,384]{1,0:T(8,128)(2,1)S(1)} %get-tuple-element.67), channel_id=1, source_target_pairs={{0,12},{4,0},{8,4},{12,8},{1,13},{5,1},{9,5},{13,9},{2,14},{6,2},{... | collective-permute-start | bytes 294920 | tf_op jit(solution)/shard_map/ppermute | solution.py:321
  77.3 5.9 %collective-permute-start.19 = (bf16[128,384]{1,0:T(8,128)(2,1)S(1)}, bf16[128,384]{1,0:T(8,128)(2,1)S(1)}, u32[]{:S(2)}, u32[]{:S(2)}) collective-permute-start(bf16[128,384]{1,0:T(8,128)(2,1)S(1)} %get-tuple-element.68), channel_id=1, source_target_pairs={{0,8},{4,12},{8,0},{12,4},{1,9},{5,13},{9,1},{13,5},{2,10},{6,14},... | collective-permute-start | bytes 294920 | tf_op jit(solution)/shard_map/ppermute | solution.py:321
  77.9 9.1 %collective-permute-start.20 = (bf16[128,384]{1,0:T(8,128)(2,1)S(1)}, bf16[128,384]{1,0:T(8,128)(2,1)S(1)}, u32[]{:S(2)}, u32[]{:S(2)}) collective-permute-start(bf16[128,384]{1,0:T(8,128)(2,1)S(1)} %get-tuple-element.69), channel_id=1, source_target_pairs={{0,4},{4,8},{8,12},{12,0},{1,5},{5,9},{9,13},{13,1},{2,6},{6,10},{... | collective-permute-start | bytes 294920 | tf_op jit(solution)/shard_map/ppermute | solution.py:321

commit v4 on v3

--- a/solution.py
+++ b/solution.py
@@ -10,6 +10,7 @@
 WIDE = GROUP * HEAD_WIDTH
 BLOCK = 128
 CHUNK = 512
+HALF = 256
 TOKENS = 2048
 SCALE = HEAD_WIDTH ** -0.5
 LOG2E = 1.4426950408889634
@@ -31,18 +32,17 @@
     return d // 64, (d // 16) % 4, (d // 4) % 4, (d // 2) % 2, d % 2
 
 
-def keys_kernel(keys, values, kv_out, sems):
-    copies = []
-    for g in range(4):
-        cols = pl.ds(g * HEAD_WIDTH, HEAD_WIDTH)
-        for z in range(8):
-            for part, src in enumerate((keys, values)):
-                to = kv_out.at[g, z, :, pl.ds(part * HEAD_WIDTH, HEAD_WIDTH)]
-                copies.append(pltpu.make_async_copy(src.at[:, cols], to, sems.at[len(copies)]))
+def keys_kernel(keys, values, kv_out, kb, vb, sems):
+    copies = [pltpu.make_async_copy(keys, kb, sems.at[0]), pltpu.make_async_copy(values, vb, sems.at[1])]
     for copy in copies:
         copy.start()
     for copy in copies:
         copy.wait()
+    for g in range(4):
+        cols = slice(g * HEAD_WIDTH, (g + 1) * HEAD_WIDTH)
+        both = jnp.concatenate([kb[:, cols], vb[:, cols]], axis=1)
+        for z in range(8):
+            kv_out[g, z] = both
 
 
 def queries_kernel(did, labels, mask, queries, w, seg, q0, q1, q2, q3, w_out, seg_out, lb, mb, sems):
@@ -96,33 +96,25 @@
     return lax.dot_general(a, b, NT, preferred_element_type=F32)
 
 
-def forward_kernel(did, seg, w, q0, q1, q2, q3, *rest):
-    kvs = rest[:8]
-    plog, p_out, inv_out, delta_out, q_out, kv_out = rest[8:14]
-    s_buf, u_rows = rest[14:]
-    _, x, y, zh, c = coords(did)
-    for cc in range(2):
-        for kx in range(4):
-            for ys in range(4):
-                for z in range(2):
-                    row = ys * CHUNK + cc * 256 + z * BLOCK + kx * 32
-                    kv_out[row : row + 32, :] = kvs[cc * 4 + kx][ys, z]
-    for k, ref in enumerate((q0, q1, q2, q3)):
-        slot = (y - k + 4) % 4
-        for h in range(GROUP):
-            q_out[slot, h * BLOCK : (h + 1) * BLOCK, :] = ref[:BLOCK, h * HEAD_WIDTH : (h + 1) * HEAD_WIDTH]
+def scores_half(cc, place, q, seg, w, kvs, kv_out, p_out, top_out, sums_out, s_buf, u_rows):
+    _, x, y, zh, c = place
+    for kx in range(4):
+        for ys in range(4):
+            for z in range(2):
+                row = ys * HALF + z * BLOCK + kx * 32
+                kv_out[row : row + 32, :] = kvs[kx][ys, z]
     diffs16 = on_both(stack8([head_diff(w, y, h) for h in range(GROUP)]))
-    ones = stack8([jnp.zeros((1, CHUNK), F32)] * GROUP + [jnp.ones((1, CHUNK), F32)])
-    for ch in range(4):
-        rows = slice(ch * CHUNK, (ch + 1) * CHUNK)
+    ones = stack8([jnp.zeros((1, 2 * HALF), F32)] * GROUP + [jnp.ones((1, 2 * HALF), F32)])
+    for n in range(2):
+        rows = slice(n * 2 * HALF, (n + 1) * 2 * HALF)
         part = times_t(diffs16, kv_out[rows, HEAD_WIDTH:])
         high, low = halves(part[:8] + part[8:])
         u_rows[:, rows] = jnp.concatenate([high + ones, low], axis=0).astype(BF16)
-    plog[...] = jnp.zeros_like(plog)
     j = zh * 2 + c
     r = lax.broadcasted_iota(jnp.int32, (BLOCK, BLOCK), 0)
     from_x = jnp.bitwise_and(x + 4 - jnp.right_shift(r, 5), 3)
     inner = jnp.bitwise_and(jnp.right_shift(r, 3), 3) * 32 + from_x * 8 + jnp.bitwise_and(r, 7)
+    inner = inner + ((c + cc) % 2) * BLOCK
     query_at = lax.broadcasted_iota(jnp.int32, (BLOCK, BLOCK), 1) + j * BLOCK
     last = seg[:, pl.ds(pl.multiple_of(3 * CHUNK + j * BLOCK, BLOCK), BLOCK)]
     start = jnp.zeros((1, BLOCK), F32)
@@ -134,38 +126,67 @@
     for ys in range(4):
         top = jnp.full((1, WIDE), NEG, F32)
         for i, ch in enumerate(CHUNKS[ys]):
-            for b in range(CHUNK // BLOCK):
-                row = ch * CHUNK + b * BLOCK
-                s = times_t(kv_out[row : row + BLOCK, :HEAD_WIDTH], q_out[ys])
+            for z in range(2):
+                row = ch * HALF + z * BLOCK
+                s = times_t(kv_out[row : row + BLOCK, :HEAD_WIDTH], q[ys])
                 if ch == ys:
-                    key_at = inner + ((b % 2) * 256 + ((c + b // 2) % 2) * BLOCK)
+                    key_at = inner + z * 256
                     ok = key_at <= query_at
                     if ys == 3:
                         ok = ok & (key_at >= start)
                     s = jnp.where(jnp.concatenate([ok] * GROUP, axis=1), s, NEG)
                 top = jnp.maximum(top, jnp.max(s, axis=0, keepdims=True))
-                at = i * CHUNK + b * BLOCK
+                at = i * HALF + z * BLOCK
                 s_buf[at : at + BLOCK, :] = s
         sums = jnp.zeros((16, WIDE), F32)
         for i, ch in enumerate(CHUNKS[ys]):
-            at_p = (P_AT[ys] + i) * CHUNK
-            for b in range(CHUNK // BLOCK):
-                at = i * CHUNK + b * BLOCK
+            at_p = (P_AT[ys] + i) * HALF
+            for z in range(2):
+                at = i * HALF + z * BLOCK
                 p = jnp.exp2((s_buf[at : at + BLOCK, :] - top) * (SCALE * LOG2E))
-                p_out[at_p + b * BLOCK : at_p + (b + 1) * BLOCK, :] = p.astype(BF16)
+                p_out[at_p + z * BLOCK : at_p + (z + 1) * BLOCK, :] = p.astype(BF16)
             sums = sums + jnp.dot(
-                u_rows[:, ch * CHUNK : (ch + 1) * CHUNK], p_out[at_p : at_p + CHUNK, :], preferred_element_type=F32
+                u_rows[:, ch * HALF : (ch + 1) * HALF], p_out[at_p : at_p + HALF, :], preferred_element_type=F32
             )
-        inv = 1.0 / sums[GROUP : GROUP + 1, :]
-        both = (sums[:8] + sums[8:]) * inv
-        delta = jnp.concatenate([both[h : h + 1, h * BLOCK : (h + 1) * BLOCK] for h in range(GROUP)], axis=1)
+        top_out[ys] = jnp.broadcast_to(top, (8, WIDE))
+        sums_out[ys] = sums
+
+
+def near_kernel(did, seg, w, q0, q1, q2, q3, k0, k1, k2, k3, q_out, kv_out, p_out, top_out, sums_out, s_buf, u_rows):
+    place = coords(did)
+    y = place[2]
+    for k, ref in enumerate((q0, q1, q2, q3)):
+        slot = (y - k + 4) % 4
+        for h in range(GROUP):
+            q_out[slot, h * BLOCK : (h + 1) * BLOCK, :] = ref[:BLOCK, h * HEAD_WIDTH : (h + 1) * HEAD_WIDTH]
+    scores_half(0, place, q_out, seg, w, (k0, k1, k2, k3), kv_out, p_out, top_out, sums_out, s_buf, u_rows)
+
+
+def rest_kernel(
+    did, seg, w, q, top0, sums0, k0, k1, k2, k3, plog, inv_out, delta_out, alpha_out, kv_out, p_out, top, sums, s_buf, u_rows
+):
+    place = coords(did)
+    y = place[2]
+    scores_half(1, place, q, seg, w, (k0, k1, k2, k3), kv_out, p_out, top, sums, s_buf, u_rows)
+    plog[...] = jnp.zeros_like(plog)
+    row8 = lax.broadcasted_iota(jnp.int32, (8, WIDE), 0)
+    for ys in range(4):
+        a, b = top0[ys, 0:1, :], top[ys, 0:1, :]
+        both = jnp.maximum(a, b)
+        a = jnp.exp2((a - both) * (SCALE * LOG2E))
+        b = jnp.exp2((b - both) * (SCALE * LOG2E))
+        total = sums0[ys] * a + sums[ys] * b
+        inv = 1.0 / total[GROUP : GROUP + 1, :]
+        e = (total[:8] + total[8:]) * inv
+        delta = jnp.concatenate([e[h : h + 1, h * BLOCK : (h + 1) * BLOCK] for h in range(GROUP)], axis=1)
         inv_out[ys] = jnp.broadcast_to(inv, (8, WIDE))
         delta_out[ys] = jnp.broadcast_to(delta, (8, WIDE))
+        alpha_out[ys] = jnp.where(row8 == 0, a, b)
         lg = delta[:, :BLOCK] + delta[:, BLOCK : 2 * BLOCK] + delta[:, 2 * BLOCK :]
         plog[pl.ds((y - ys + 4) % 4, 1), :] = lg
 
 
-def middle_kernel(did, w, p, delta, q, kv, g_out, dq_out, qt_out, kt, u):
+def middle_kernel(did, w, p0, p1, delta, alpha, q, kv0, kv1, g0, g1, dq_out, qt_out, kt, u):
     _, _, y, _, _ = coords(did)
     eye = jnp.where(
         lax.broadcasted_iota(jnp.int32, (BLOCK, BLOCK), 0) == lax.broadcasted_iota(jnp.int32, (BLOCK, BLOCK), 1), 1.0, 0.0
@@ -173,37 +194,46 @@
     pad = jnp.zeros((BLOCK - 8, HEAD_WIDTH), F32)
     high, low = halves(jnp.concatenate([stack8([head_diff(w, y, h) for h in range(GROUP)]), pad], axis=0))
     high, low = high.astype(BF16), low.astype(BF16)
+    for half, kv in enumerate((kv0, kv1)):
+        for n in range(2):
+            rows = slice(n * 2 * HALF, (n + 1) * 2 * HALF)
+            kt[half, :, rows] = times_t(eye, kv[rows, :HEAD_WIDTH]).astype(BF16)
+            u[half, rows, :] = times_t(kv[rows, HEAD_WIDTH:], high) + times_t(kv[rows, HEAD_WIDTH:], low)
+    for ys in range(4):
+        qt_out[ys] = times_t(eye, q[ys]).astype(BF16)
+        total = jnp.zeros((HEAD_WIDTH, WIDE), F32)
+        for half, (p, g) in enumerate(((p0, g0), (p1, g1))):
+            dqt = jnp.zeros((HEAD_WIDTH, WIDE), F32)
+            for i, ch in enumerate(CHUNKS[ys]):
+                at_p = (P_AT[ys] + i) * HALF
+                for z in range(2):
+                    row = ch * HALF + z * BLOCK
+                    at = slice(at_p + z * BLOCK, at_p + (z + 1) * BLOCK)
+                    ub = jnp.concatenate(
+                        [jnp.broadcast_to(u[half, row : row + BLOCK, h : h + 1], (BLOCK, BLOCK)) for h in range(GROUP)],
+                        axis=1,
+                    )
+                    g[at, :] = (p[at, :].astype(F32) * (ub - delta[ys, 0:1, :])).astype(BF16)
+                dqt = dqt + jnp.dot(
+                    kt[half, :, ch * HALF : (ch + 1) * HALF], g[at_p : at_p + HALF, :], preferred_element_type=F32
+                )
+            total = total + dqt * alpha[ys, half : half + 1, :]
+        dq_out[ys] = total
+
+
+def key_terms(out, half, p, g, qt, wt, f, alpha, qf, at16):
+    for ys in range(4):
+        fa = f[ys, 0:1, :] * alpha[ys, half : half + 1, :]
+        at16[ys] = (wt[...] * fa).astype(BF16)
+        qf[ys] = (qt[ys].astype(F32) * (fa * SCALE)).astype(BF16)
     for ch in range(4):
-        rows = slice(ch * CHUNK, (ch + 1) * CHUNK)
-        kt[:, rows] = times_t(eye, kv[rows, :HEAD_WIDTH]).astype(BF16)
-        u[rows, :] = times_t(kv[rows, HEAD_WIDTH:], high) + times_t(kv[rows, HEAD_WIDTH:], low)
-    for ys in range(4):
-        qt_out[ys] = times_t(eye, q[ys]).astype(BF16)
-        dqt = jnp.zeros((HEAD_WIDTH, WIDE), F32)
-        for i, ch in enumerate(CHUNKS[ys]):
-            at_p = (P_AT[ys] + i) * CHUNK
-            for b in range(CHUNK // BLOCK):
-                row = ch * CHUNK + b * BLOCK
-                at = slice(at_p + b * BLOCK, at_p + (b + 1) * BLOCK)
-                ub = jnp.concatenate(
-                    [jnp.broadcast_to(u[row : row + BLOCK, h : h + 1], (BLOCK, BLOCK)) for h in range(GROUP)], axis=1
-                )
-                g_out[at, :] = (p[at, :].astype(F32) * (ub - delta[ys, 0:1, :])).astype(BF16)
-            dqt = dqt + jnp.dot(
-                kt[:, ch * CHUNK : (ch + 1) * CHUNK], g_out[at_p : at_p + CHUNK, :], preferred_element_type=F32
-            )
-        dq_out[ys] = dqt
-
-
-def key_terms(out, half, p, g, qf, at16):
-    for ch in range(4):
-        dk = jnp.zeros((256, HEAD_WIDTH), F32)
-        dv = jnp.zeros((256, HEAD_WIDTH), F32)
+        dk = jnp.zeros((HALF, HEAD_WIDTH), F32)
+        dv = jnp.zeros((HALF, HEAD_WIDTH), F32)
         for ys in range(4):
             if ch in CHUNKS[ys]:
-                at = (P_AT[ys] + CHUNKS[ys].index(ch)) * CHUNK + half * 256
-                dk = dk + times_t(g[at : at + 256, :], qf[ys])
-                dv = dv + times_t(p[at : at + 256, :], at16[ys])
+                at = (P_AT[ys] + CHUNKS[ys].index(ch)) * HALF
+                dk = dk + times_t(g[at : at + HALF, :], qf[ys])
+                dv = dv + times_t(p[at : at + HALF, :], at16[ys])
         both = jnp.concatenate([dk, dv], axis=1).astype(BF16)
         for z in range(2):
             for kx in range(4):
@@ -211,7 +241,7 @@
                 out[kx, ch, z] = both[row : row + 32]
 
 
-def far_kernel(did, w, l0, l1, l2, l3, g0, g1, g2, g3, p, g, inv, qt, out, f_out, qf, at16, loss_out, lgs, labs):
+def far_kernel(did, w, l0, l1, l2, l3, g0, g1, g2, g3, p, g, inv, alpha, qt, out, f_out, wt, loss_out, lgs, labs, qf, at16):
     _, _, y, _, _ = coords(did)
     for k, ref in enumerate((l0, l1, l2, l3)):
         src = (y - k + 4) % 4
@@ -220,7 +250,7 @@
             lgs[src, ys] = jnp.broadcast_to(ref[(m - k) % 4 : (m - k) % 4 + 1, :], (8, BLOCK))
     for k, ref in enumerate((g0, g1, g2, g3)):
         labs[(y - k + 4) % 4] = ref[BLOCK:, :256].astype(F32)[8:16, :]
-    wt = jnp.concatenate([jnp.broadcast_to(head_diff(w, y, h), (BLOCK, HEAD_WIDTH)).T for h in range(GROUP)], axis=1)
+    wt[...] = jnp.concatenate([jnp.broadcast_to(head_diff(w, y, h), (BLOCK, HEAD_WIDTH)).T for h in range(GROUP)], axis=1)
     loss = jnp.zeros((1, BLOCK), F32)
     for ys in range(4):
         z = (lgs[0, ys] + lgs[1, ys] + lgs[2, ys] + lgs[3, ys])[0:1, :]
@@ -231,29 +261,33 @@
         loss = loss + mask * (jnp.maximum(a, 0.0) + jnp.log(1.0 + e))
         sig = jnp.where(a >= 0.0, 1.0, e) / (1.0 + e)
         d0 = mask * jnp.where(one, sig, -sig)
-        f = jnp.concatenate([d0] * GROUP, axis=1) * inv[ys, 0:1, :]
-        f_out[ys] = jnp.broadcast_to(f, (8, WIDE))
-        at16[ys] = (wt * f).astype(BF16)
-        qf[ys] = (qt[ys].astype(F32) * (f * SCALE)).astype(BF16)
+        f_out[ys] = jnp.broadcast_to(jnp.concatenate([d0] * GROUP, axis=1) * inv[ys, 0:1, :], (8, WIDE))
     loss_out[...] = jnp.broadcast_to(loss, (8, BLOCK))
-    key_terms(out, 1, p, g, qf, at16)
-
-
-def own_kernel(did, p, g, qf, at16, f, loss, kv, dqt, out, hg_out, d0, d1, d2, d3, dqb, ct):
+    key_terms(out, 1, p, g, qt, wt, f_out, alpha, qf, at16)
+
+
+def own_kernel(
+    did, p0, p1, g, qt, wt, f, alpha, loss, kv0, kv1, dqt, out, hg_out, d0, d1, d2, d3, dqb, ct, qf, at16
+):
     _, _, y, _, _ = coords(did)
-    key_terms(out, 0, p, g, qf, at16)
+    key_terms(out, 0, p0, g, qt, wt, f, alpha, qf, at16)
     head_of = lax.broadcasted_iota(jnp.int32, (8, WIDE), 1) // BLOCK
     head_at = lax.broadcasted_iota(jnp.int32, (8, WIDE), 0)
-    seen = set()
-    for ys in range(4):
-        fm = on_both(jnp.where(head_of == head_at, f[ys, 0:1, :], 0.0))
-        for i, ch in enumerate(CHUNKS[ys]):
-            at = (P_AT[ys] + i) * CHUNK
-            rows = slice(ch * CHUNK, (ch + 1) * CHUNK)
-            cs = times_t(fm, p[at : at + CHUNK, :])
-            cs = cs[:8] + cs[8:]
-            ct[:, rows] = ct[:, rows] + cs if ch in seen else cs
-            seen.add(ch)
+    hg = jnp.zeros((16, HEAD_WIDTH), F32)
+    for half, (p, kv) in enumerate(((p0, kv0), (p1, kv1))):
+        seen = set()
+        for ys in range(4):
+            fa = f[ys, 0:1, :] * alpha[ys, half : half + 1, :]
+            fm = on_both(jnp.where(head_of == head_at, fa, 0.0))
+            for i, ch in enumerate(CHUNKS[ys]):
+                at = (P_AT[ys] + i) * HALF
+                rows = slice(ch * HALF, (ch + 1) * HALF)
+                cs = times_t(fm, p[at : at + HALF, :])
+                cs = cs[:8] + cs[8:]
+                ct[:, rows] = ct[:, rows] + cs if ch in seen else cs
+                seen.add(ch)
+        hg = hg + jnp.dot(on_both(ct[...]), kv[:, HEAD_WIDTH:], preferred_element_type=F32)
+    for ys in range(4):
         dqs = dqt[ys] * (f[ys, 0:1, :] * SCALE)
         slot = (y - ys + 4) % 4
         for h in range(GROUP):
@@ -261,7 +295,6 @@
             dqb[slot, :, cols] = dqs[:, cols].T.astype(BF16)
     for k, ref in enumerate((d0, d1, d2, d3)):
         ref[...] = dqb[k]
-    hg = jnp.dot(on_both(ct[...]), kv[:, HEAD_WIDTH:], preferred_element_type=F32)
     row8 = lax.broadcasted_iota(jnp.int32, (8, BLOCK), 0)
     hg_out[...] = jnp.where(row8 == GROUP, loss[...], hg[:8] + hg[8:])
 
@@ -343,7 +376,10 @@
 def per_device(queries, keys, values, head, segments, label_mask, labels):
     did = lax.axis_index(("zl", "x", "y", "zh", "c")).astype(jnp.int32).reshape(1)
     (copies,) = call(
-        keys_kernel, [like((4, 8, 8, 256), BF16)], [HBM] * 2, [HBM], scratch=[pltpu.SemaphoreType.DMA((64,))]
+        keys_kernel,
+        [like((4, 8, 8, 256), BF16)],
+        [HBM] * 2,
+        scratch=[pltpu.VMEM((8, 512), BF16), pltpu.VMEM((8, 512), BF16), pltpu.SemaphoreType.DMA((2,))],
     )(in_hbm(keys), in_hbm(values))
     own = lax.all_to_all(copies.reshape(32, 8, 256), YZ_AXES, 0, 0, tiled=True).reshape(4, 2, 32, 256)
     *packs, w, seg = call(
@@ -369,51 +405,46 @@
     over_c = [shift(a, "c", 2, 1) for a in over_x]
     for k in range(1, 4):
         packs[k] = shift(packs[k], "y", 4, k)
-    plog, p, inv, delta, q, kv = call(
-        forward_kernel,
-        [
-            like((8, BLOCK), F32),
-            like((7 * CHUNK, WIDE), BF16),
-            like((4, 8, WIDE), F32),
-            like((4, 8, WIDE), F32),
-            like((4, WIDE, HEAD_WIDTH), BF16),
-            like((TOKENS, 256), BF16),
-        ],
-        [SMEM] + [VMEM] * 14,
-        scratch=[pltpu.VMEM((3 * CHUNK, WIDE), F32), pltpu.VMEM((16, TOKENS), BF16)],
-    )(did, seg, w, *packs, *over_x, *over_c)
+    half_p = like((7 * HALF, WIDE), BF16)
+    half_kv = like((4 * HALF, 256), BF16)
+    row_set = like((4, 8, WIDE), F32)
+    wide_set = like((4, HEAD_WIDTH, WIDE), BF16)
+    half_scratch = [pltpu.VMEM((3 * HALF, WIDE), F32), pltpu.VMEM((16, 4 * HALF), BF16)]
+    q, kv0, p0, top0, sums0 = call(
+        near_kernel,
+        [like((4, WIDE, HEAD_WIDTH), BF16), half_kv, half_p, row_set, like((4, 16, WIDE), F32)],
+        [SMEM] + [VMEM] * 10,
+        scratch=half_scratch,
+    )(did, seg, w, *packs, *over_x)
+    plog, inv, delta, alpha, kv1, p1 = call(
+        rest_kernel,
+        [like((8, BLOCK), F32), row_set, row_set, row_set, half_kv, half_p],
+        [SMEM] + [VMEM] * 9,
+        scratch=[pltpu.VMEM((4, 8, WIDE), F32), pltpu.VMEM((4, 16, WIDE), F32)] + half_scratch,
+    )(did, seg, w, q, top0, sums0, *over_c)
     logs = [plog]
     for k in range(1, 4):
         logs.append(shift(plog, "y", 4, k))
-    g, dqt, qt = call(
+    g0, g1, dqt, qt = call(
         middle_kernel,
-        [
-            like((7 * CHUNK, WIDE), BF16),
-            like((4, HEAD_WIDTH, WIDE), F32),
-            like((4, HEAD_WIDTH, WIDE), BF16),
-        ],
-        [SMEM] + [VMEM] * 5,
-        scratch=[pltpu.VMEM((HEAD_WIDTH, TOKENS), BF16), pltpu.VMEM((TOKENS, BLOCK), F32)],
-    )(did, w, p, delta, q, kv)
-    far_d, f, qf, at16, loss_rows = call(
+        [half_p, half_p, like((4, HEAD_WIDTH, WIDE), F32), wide_set],
+        [SMEM] + [VMEM] * 8,
+        scratch=[pltpu.VMEM((2, HEAD_WIDTH, 4 * HALF), BF16), pltpu.VMEM((2, 4 * HALF, BLOCK), F32)],
+    )(did, w, p0, p1, delta, alpha, q, kv0, kv1)
+    factor_scratch = [pltpu.VMEM((4, HEAD_WIDTH, WIDE), BF16), pltpu.VMEM((4, HEAD_WIDTH, WIDE), BF16)]
+    far_d, f, wt, loss_rows = call(
         far_kernel,
-        [
-            like((4, 4, 2, 32, 256), BF16),
-            like((4, 8, WIDE), F32),
-            like((4, HEAD_WIDTH, WIDE), BF16),
-            like((4, HEAD_WIDTH, WIDE), BF16),
-            like((8, BLOCK), F32),
-        ],
-        [SMEM] + [VMEM] * 13,
-        scratch=[pltpu.VMEM((4, 4, 8, BLOCK), F32), pltpu.VMEM((4, 8, 256), F32)],
-    )(did, w, *logs, *packs, p, g, inv, qt)
+        [like((4, 4, 2, 32, 256), BF16), row_set, like((HEAD_WIDTH, WIDE), F32), like((8, BLOCK), F32)],
+        [SMEM] + [VMEM] * 14,
+        scratch=[pltpu.VMEM((4, 4, 8, BLOCK), F32), pltpu.VMEM((4, 8, 256), F32)] + factor_scratch,
+    )(did, w, *logs, *packs, p1, g1, inv, alpha, qt)
     far = shift(far_d, "c", 2, 1)
     own_d, hg, *dq = call(
         own_kernel,
         [like((4, 4, 2, 32, 256), BF16), like((8, BLOCK), F32)] + [like((BLOCK, WIDE), BF16)] * 4,
-        [SMEM] + [VMEM] * 8,
-        scratch=[pltpu.VMEM((4, BLOCK, WIDE), BF16), pltpu.VMEM((8, TOKENS), F32)],
-    )(did, p, g, qf, at16, f, loss_rows, kv, dqt)
+        [SMEM] + [VMEM] * 11,
+        scratch=[pltpu.VMEM((4, BLOCK, WIDE), BF16), pltpu.VMEM((8, 4 * HALF), F32)] + factor_scratch,
+    )(did, p0, p1, g0, qt, wt, f, alpha, loss_rows, kv0, kv1, dqt)
     by_x = call(core_kernel, [like((4, 2, 32, 256), BF16)] * 4, [VMEM] * 2)(own_d, far)
     got = [by_x[0]]
     for k in range(1, 4):

time: 89 us -> 88.9 us (level)
    pallas_call x4 -> x5, Pallas kernels: 8.06 us -> 7.81 us  [the longest x1 2.3 us: per_device(): call(middle_kernel, [half_p, half_p, like((4, HEAD_WIDTH, WIDE), F32), wi...]
  transfers between devices with their start and end apart: 22 -> 22, of which waited for: 11 -> 11; matrix products, arithmetic and copies ran while one was open for 0% -> 0% of each run, Pallas kernels for 7% -> 9%
where the time goes in v4:
time: 88.9 us; the launch traced here: 88.5 us
  starting transfers between devices  27.5 us (31%)
  waiting for transfers between devices  25.9 us (29%)
  blocking collectives  21 us (24%)
  Pallas kernels  13.3 us (15%)
  between operations  0.9 us (1%)
    ppermute x21, waiting for transfers between devices, shift(): return lax.ppermute(v, axis, [(i, (i + k) % size) for i in range(size)])  25.9 us
    ppermute x21, starting transfers between devices, shift(): return lax.ppermute(v, axis, [(i, (i + k) % size) for i in range(size)])  23.3 us
    all_to_all x1, blocking collectives, per_device(): lax.all_to_all(copies.reshape(32, 8, 256), YZ_AXES, 0, 0, tiled=True)  21 us
    all_to_all x1, starting transfers between devices, per_device(): lax.all_to_all(by_z.reshape(32, 8, WIDE), YZ_AXES, 0, 0, tiled=True)  4.23 us
    pallas_call x1, Pallas kernels, per_device(): call(middle_kernel, [half_p, half_p, like((4, HEAD_WIDTH, WIDE), F32), wi...  2.3 us
    pallas_call x1, Pallas kernels, per_device(): call(near_kernel, [like((4, WIDE, HEAD_WIDTH), BF16), half_kv, half_p, ro...  1.91 us
    pallas_call x1, Pallas kernels, per_device(): call(rest_kernel, [like((8, BLOCK), F32), row_set, row_set, row_set, half...  1.87 us
  transfers between devices with their start and end apart: 22, of which 11 were waited for; matrix products, arithmetic and copies ran while one was open for 0% of the time, Pallas kernels for 9%

profile of v4, /device:TPU:1, one launch (start us, length us, event | category | flops | bytes accessed | tf_op | source)
XLA Modules:
  0.0 88.5 jit_solution(13988126863582182299)
XLA Ops:
  0.6 0.7 shard_map.111
  1.4 21.0 %all_to_all.10 = bf16[32,8,256]{2,1,0:T(8,128)(2,1)S(1)} all-to-all(bf16[32,8,256]{2,1,0:T(8,128)(2,1)S(1)} %bitcast.22), channel_id=1, replica_groups=mesh['zl'=4,'x'=4,'y'=4,'zh'=2,'c'=2] {'y','zh','zl'}, dimensions={0} | all-to-all | bytes 262144 | tf_op jit(solution)/shard_map/all_to_all | solution.py:384
  22.4 2.5 %collective-permute-start.5 = (bf16[4,2,32,256]{3,2,1,0:T(8,128)(2,1)S(1)}, bf16[4,2,32,256]{3,2,1,0:T(8,128)(2,1)S(1)}, u32[]{:S(2)}, u32[]{:S(2)}) collective-permute-start(bf16[4,2,32,256]{3,2,1,0:T(8,128)(2,1)S(1)} %bitcast.17), channel_id=1, source_target_pairs={{0,48},{16,0},{32,16},{48,32},{1,49},{17,1},{33,17},{49,33},{2,50}... | collective-permute-start | bytes 393224 | tf_op jit(solution)/shard_map/ppermute | solution.py:354
  25.4 0.6 collective-permute-start.3
  26.0 1.2 %shard_map.110 = (bf16[144,384]{1,0:T(8,128)(2,1)S(1)}, bf16[144,384]{1,0:T(8,128)(2,1)S(1)}, bf16[144,384]{1,0:T(8,128)(2,1)S(1)}, bf16[144,384]{1,0:T(8,128)(2...) custom-call(s32[1]{0:T(128)} %bitcast.did, s32[1,128]{1,0:T(1,128)} %bitcast.27, s32[1,128]{1,0:T(1,128)} %bitcast.28, ...), custom_call_target="tpu_custom_call" | custom-call | tf_op jit(solution)/shard_map/pallas_call | solution.py:385
  27.5 1.7 %collective-permute-start.1 = (bf16[144,384]{1,0:T(8,128)(2,1)S(1)}, bf16[144,384]{1,0:T(8,128)(2,1)S(1)}, u32[]{:S(2)}, u32[]{:S(2)}) collective-permute-start(bf16[144,384]{1,0:T(8,128)(2,1)S(1)} %get-tuple-element.48), channel_id=1, source_target_pairs={{0,8},{4,12},{8,0},{12,4},{1,9},{5,13},{9,1},{13,5},{2,10},{6,14},... | collective-permute-start | bytes 331784 | tf_op jit(solution)/shard_map/ppermute | solution.py:354
  29.3 4.2 %collective-permute-done.q1.g1 = bf16[144,384]{1,0:T(8,128)(2,1)S(1)} collective-permute-done((bf16[144,384]{1,0:T(8,128)(2,1)S(1)}, bf16[144,384]{1,0:T(8,128)(2,1)S(1)}, u32[]{:S(2)}, u32[]{:S(2)}) %collective-permute-start) | collective-permute-done | bytes 110624 | tf_op jit(solution)/shard_map/ppermute | solution.py:354
  33.5 3.8 %collective-permute-start.6 = (bf16[4,2,32,256]{3,2,1,0:T(8,128)(2,1)S(1)}, bf16[4,2,32,256]{3,2,1,0:T(8,128)(2,1)S(1)}, u32[]{:S(2)}, u32[]{:S(2)}) collective-permute-start(bf16[4,2,32,256]{3,2,1,0:T(8,128)(2,1)S(1)} %bitcast.20), channel_id=1, source_target_pairs={{0,1},{1,0},{2,3},{3,2},{4,5},{5,4},{6,7},{7,6},{8,9},{9,8},{10,11... | collective-permute-start | bytes 393224 | tf_op jit(solution)/shard_map/ppermute | solution.py:354
  37.9 4.2 %collective-permute-done.2.q3.g3 = bf16[144,384]{1,0:T(8,128)(2,1)S(1)} collective-permute-done((bf16[144,384]{1,0:T(8,128)(2,1)S(1)}, bf16[144,384]{1,0:T(8,128)(2,1)S(1)}, u32[]{:S(2)}, u32[]{:S(2)}) %collective-permute-start.2) | collective-permute-done | bytes 110624 | tf_op jit(solution)/shard_map/ppermute | solution.py:354
  42.1 1.9 %shard_map.112 = (bf16[4,384,128]{2,1,0:T(8,128)(2,1)S(1)}, bf16[1024,256]{1,0:T(8,128)(2,1)S(1)}, bf16[1792,384]{1,0:T(8,128)(2,1)S(1)}, f32[4,8,384]{2,1,0:T(8,128)S(1)}, f32[4,16,384]{2,1,0:T(8,128)S(1)}) custom-call(s32[1]{0:T(128)} %bitcast.did, s32[1,2048]{1,0:T(1,128)S(1)} %get-tuple-element.44.seg, f32[2,1536]{1,0:T(2,128)S(1)} %get-tuple-element.45.w, ...), custom_call_target="tpu_custom_call" | custom-call | tf_op jit(solution)/shard_map/pallas_call | solution.py:413
  44.0 1.9 %shard_map.113 = (f32[8,128]{1,0:T(8,128)S(1)}, f32[4,8,384]{2,1,0:T(8,128)S(1)}, f32[4,8,384]{2,1,0:T(8,128)S(1)}, f32[4,8,384]{2,1,0:T(8,128)S(1)}, bf16[1024,...) custom-call(s32[1]{0:T(128)} %bitcast.did, s32[1,2048]{1,0:T(1,128)S(1)} %get-tuple-element.44.seg, ...), custom_call_target="tpu_custom_call" | custom-call | tf_op jit(solution)/shard_map/pallas_call | solution.py:419
  45.9 0.7 collective-permute-start.12
  47.5 2.3 %shard_map.114 = (bf16[1792,384]{1,0:T(8,128)(2,1)S(1)}, bf16[1792,384]{1,0:T(8,128)(2,1)S(1)}, f32[4,128,384]{2,1,0:T(8,128)S(1)}, bf16[4,128,384]{2,1,0:T(8,128)(2,1)S(1)}) custom-call(s32[1]{0:T(128)} %bitcast.did, f32[2,1536]{1,0:T(2,128)S(1)} %get-tuple-element.45.w, bf16[1792,384]{1,0:T(8,128)(2,1)S(1)} %get-tuple-element.50.p0, ...), custom_call_target="tpu_custom_call" | custom-call | tf_op jit(solution)/shard_map/pallas_call | solution.py:428
  49.8 0.8 collective-permute-done.11.l2
  50.8 1.0 %shard_map.115 = (bf16[4,4,2,32,256]{4,3,2,1,0:T(8,128)(2,1)S(1)}, f32[4,8,384]{2,1,0:T(8,128)S(1)}, f32[128,384]{1,0:T(8,128)S(1)}, f32[8,128]{1,0:T(8,128)S(1)}) custom-call(s32[1]{0:T(128)} %bitcast.did, f32[2,1536]{1,0:T(2,128)S(1)} %get-tuple-element.45.w, f32[8,128]{1,0:T(8,128)S(1)} %get-tuple-element.61.l0, f32[8,128]{1,0:T(8,128)S(1)} %collective-permute-done.10.l1, ...), custom_call_target="tpu_custom_call" | custom-call | tf_op jit(solution)/shard_map/pallas_call | solution.py:435
  51.8 3.8 %collective-permute-start.13 = (bf16[4,4,2,32,256]{4,3,2,1,0:T(8,128)(2,1)S(1)}, bf16[4,4,2,32,256]{4,3,2,1,0:T(8,128)(2,1)S(1)}, u32[]{:S(2)}, u32[]{:S(2)}) collective-permute-start(bf16[4,4,2,32,256]{4,3,2,1,0:T(8,128)(2,1)S(1)} %get-tuple-element.69), channel_id=1, source_target_pairs={{0,1},{1,0},{2,3},{3,2},{4,5},{5,4},{6,7},{7,6},{8,9},{9,8},{10,11... | collective-permute-start | bytes 1572872 | tf_op jit(solution)/shard_map/ppermute | solution.py:354
  55.7 1.8 %shard_map.116 = (bf16[4,4,2,32,256]{4,3,2,1,0:T(8,128)(2,1)S(1)}, f32[8,128]{1,0:T(8,128)S(1)}, bf16[128,384]{1,0:T(8,128)(2,1)S(1)}, bf16[128,384]{1,0:T(8,128...) custom-call(s32[1]{0:T(128)} %bitcast.did, bf16[1792,384]{1,0:T(8,128)(2,1)S(1)} %get-tuple-element.50.p0, ...), custom_call_target="tpu_custom_call" | custom-call | tf_op jit(solution)/shard_map/pallas_call | solution.py:442
  57.6 2.2 %collective-permute-start.14 = (bf16[4,2,32,256]{3,2,1,0:T(8,128)(2,1)S(1)}, bf16[4,2,32,256]{3,2,1,0:T(8,128)(2,1)S(1)}, u32[]{:S(2)}, u32[]{:S(2)}) collective-permute-start(bf16[4,2,32,256]{3,2,1,0:T(8,128)(2,1)S(1)} %get-tuple-element.71), channel_id=1, source_target_pairs={{0,48},{16,0},{32,16},{48,32},{1,49},{17,1},{33,17},{49,33},{2,50}... | collective-permute-start | bytes 393224 | tf_op jit(solution)/shard_map/ppermute | solution.py:354
  59.8 1.2 %collective-permute-start.15 = (bf16[4,2,32,256]{3,2,1,0:T(8,128)(2,1)S(1)}, bf16[4,2,32,256]{3,2,1,0:T(8,128)(2,1)S(1)}, u32[]{:S(2)}, u32[]{:S(2)}) collective-permute-start(bf16[4,2,32,256]{3,2,1,0:T(8,128)(2,1)S(1)} %get-tuple-element.72), channel_id=1, source_target_pairs={{0,32},{16,48},{32,0},{48,16},{1,33},{17,49},{33,1},{49,17},{2,34}... | collective-permute-start | bytes 393224 | tf_op jit(solution)/shard_map/ppermute | solution.py:354
  61.1 0.7 collective-permute-start.17
  61.7 0.8 collective-permute-done.17.hg_far
  62.8 3.2 %collective-permute-done.15.b2 = bf16[4,2,32,256]{3,2,1,0:T(8,128)(2,1)S(1)} collective-permute-done((bf16[4,2,32,256]{3,2,1,0:T(8,128)(2,1)S(1)}, bf16[4,2,32,256]{3,2,1,0:T(8,128)(2,1)S(1)}, u32[]{:S(2)}, u32[]{:S(2)}) %collective-permute-start.15) | collective-permute-done | bytes 131104 | tf_op jit(solution)/shard_map/ppermute | solution.py:354
  66.0 3.6 %collective-permute-done.16.b3 = bf16[4,2,32,256]{3,2,1,0:T(8,128)(2,1)S(1)} collective-permute-done((bf16[4,2,32,256]{3,2,1,0:T(8,128)(2,1)S(1)}, bf16[4,2,32,256]{3,2,1,0:T(8,128)(2,1)S(1)}, u32[]{:S(2)}, u32[]{:S(2)}) %collective-permute-start.16) | collective-permute-done | bytes 131104 | tf_op jit(solution)/shard_map/ppermute | solution.py:354
  69.5 0.8 shard_map.118
  70.3 4.2 %all-to-all-start.1 = ((bf16[32,8,384]{2,1,0:T(8,128)(2,1)}), bf16[32,8,384]{2,1,0:T(8,128)(2,1)S(1)}, u32[]{:S(2)}, u32[]{:S(2)}) async-start(bf16[32,8,384]{2,1,0:T(8,128)(2,1)} %bitcast.9), calls=%async_computation.1 | async-start | bytes 393216 | tf_op jit(solution)/shard_map/all_to_all | solution.py:454
  74.5 2.6 %collective-permute-start.18 = (bf16[128,384]{1,0:T(8,128)(2,1)S(1)}, bf16[128,384]{1,0:T(8,128)(2,1)S(1)}, u32[]{:S(2)}, u32[]{:S(2)}) collective-permute-start(bf16[128,384]{1,0:T(8,128)(2,1)S(1)} %get-tuple-element.77), channel_id=1, source_target_pairs={{0,12},{4,0},{8,4},{12,8},{1,13},{5,1},{9,5},{13,9},{2,14},{6,2},{... | collective-permute-start | bytes 294920 | tf_op jit(solution)/shard_map/ppermute | solution.py:354
  77.6 0.6 collective-permute-start.20
  78.2 2.0 %collective-permute-done.18.d1 = bf16[128,384]{1,0:T(8,128)(2,1)S(1)} collective-permute-done((bf16[128,384]{1,0:T(8,128)(2,1)S(1)}, bf16[128,384]{1,0:T(8,128)(2,1)S(1)}, u32[]{:S(2)}, u32[]{:S(2)}) %collective-permute-start.18) | collective-permute-done | bytes 98336 | tf_op jit(solution)/shard_map/ppermute | solution.py:354
  80.3 2.7 %collective-permute-done.19.d2 = bf16[128,384]{1,0:T(8,128)(2,1)S(1)} collective-permute-done((bf16[128,384]{1,0:T(8,128)(2,1)S(1)}, bf16[128,384]{1,0:T(8,128)(2,1)S(1)}, u32[]{:S(2)}, u32[]{:S(2)}) %collective-permute-start.19) | collective-permute-done | bytes 98336 | tf_op jit(solution)/shard_map/ppermute | solution.py:354
  83.0 3.8 %collective-permute-done.20.d3 = bf16[128,384]{1,0:T(8,128)(2,1)S(1)} collective-permute-done((bf16[128,384]{1,0:T(8,128)(2,1)S(1)}, bf16[128,384]{1,0:T(8,128)(2,1)S(1)}, u32[]{:S(2)}, u32[]{:S(2)}) %collective-permute-start.20) | collective-permute-done | bytes 98336 | tf_op jit(solution)/shard_map/ppermute | solution.py:354
  86.8 0.9 %shard_map.120 = f32[128,1536]{1,0:T(8,128)} custom-call(s32[1]{0:T(128)} %bitcast.did, bf16[128,384]{1,0:T(8,128)(2,1)S(1)} %get-tuple-element.76.d0, bf16[128,384]{1,0:T(8,128)(2,1)S(1)} %collective-permute-done.18.d1, bf16[128,384]{1,0:T(8,128)(2,1)S(1)} %collective-permute-done.19.d2, bf16[128,384]{1,0:T(8,128)(2,1)S(1)} %collective-permute-done.20.d3), custom_call_target="tpu_custom_call" | custom-call | tf_op jit(solution)/shard_map/pallas_call | solution.py:458
  87.7 0.6 shard_map.119
  (24 shorter events, 3.7 us)
Async XLA Ops:
  22.4 14.9 %collective-permute-start.5 = (bf16[4,2,32,256]{3,2,1,0:T(8,128)(2,1)S(1)}, bf16[4,2,32,256]{3,2,1,0:T(8,128)(2,1)S(1)}, u32[]{:S(2)}, u32[]{:S(2)}) collective-permute-start(bf16[4,2,32,256]{3,2,1,0:T(8,128)(2,1)S(1)} %bitcast.17), channel_id=1, source_target_pairs={{0,48},{16,0},{32,16},{48,32},{1,49},{17,1},{33,17},{49,33},{2,50}... | collective-permute-start | bytes 393224 | tf_op jit(solution)/shard_map/ppermute | solution.py:354
  24.8 12.5 %collective-permute-start.4 = (bf16[4,2,32,256]{3,2,1,0:T(8,128)(2,1)S(1)}, bf16[4,2,32,256]{3,2,1,0:T(8,128)(2,1)S(1)}, u32[]{:S(2)}, u32[]{:S(2)}) collective-permute-start(bf16[4,2,32,256]{3,2,1,0:T(8,128)(2,1)S(1)} %bitcast.18), channel_id=1, source_target_pairs={{0,32},{16,48},{32,0},{48,16},{1,33},{17,49},{33,1},{49,17},{2,34}... | collective-permute-start | bytes 393224 | tf_op jit(solution)/shard_map/ppermute | solution.py:354
  25.4 12.4 %collective-permute-start.3 = (bf16[4,2,32,256]{3,2,1,0:T(8,128)(2,1)S(1)}, bf16[4,2,32,256]{3,2,1,0:T(8,128)(2,1)S(1)}, u32[]{:S(2)}, u32[]{:S(2)}) collective-permute-start(bf16[4,2,32,256]{3,2,1,0:T(8,128)(2,1)S(1)} %bitcast.19), channel_id=1, source_target_pairs={{0,16},{16,32},{32,48},{48,0},{1,17},{17,33},{33,49},{49,1},{2,18}... | collective-permute-start | bytes 393224 | tf_op jit(solution)/shard_map/ppermute | solution.py:354
  27.1 6.4 %collective-permute-start = (bf16[144,384]{1,0:T(8,128)(2,1)S(1)}, bf16[144,384]{1,0:T(8,128)(2,1)S(1)}, u32[]{:S(2)}, u32[]{:S(2)}) collective-permute-start(bf16[144,384]{1,0:T(8,128)(2,1)S(1)} %get-tuple-element.47), channel_id=1, source_target_pairs={{0,4},{4,8},{8,12},{12,0},{1,5},{5,9},{9,13},{13,1},{2,6},{6,10},{... | collective-permute-start | bytes 331784 | tf_op jit(solution)/shard_map/ppermute | solution.py:354
  27.5 10.3 %collective-permute-start.1 = (bf16[144,384]{1,0:T(8,128)(2,1)S(1)}, bf16[144,384]{1,0:T(8,128)(2,1)S(1)}, u32[]{:S(2)}, u32[]{:S(2)}) collective-permute-start(bf16[144,384]{1,0:T(8,128)(2,1)S(1)} %get-tuple-element.48), channel_id=1, source_target_pairs={{0,8},{4,12},{8,0},{12,4},{1,9},{5,13},{9,1},{13,5},{2,10},{6,14},... | collective-permute-start | bytes 331784 | tf_op jit(solution)/shard_map/ppermute | solution.py:354
  33.5 10.5 %collective-permute-start.6 = (bf16[4,2,32,256]{3,2,1,0:T(8,128)(2,1)S(1)}, bf16[4,2,32,256]{3,2,1,0:T(8,128)(2,1)S(1)}, u32[]{:S(2)}, u32[]{:S(2)}) collective-permute-start(bf16[4,2,32,256]{3,2,1,0:T(8,128)(2,1)S(1)} %bitcast.20), channel_id=1, source_target_pairs={{0,1},{1,0},{2,3},{3,2},{4,5},{5,4},{6,7},{7,6},{8,9},{9,8},{10,11... | collective-permute-start | bytes 393224 | tf_op jit(solution)/shard_map/ppermute | solution.py:354
  37.3 6.7 %collective-permute-start.9 = (bf16[4,2,32,256]{3,2,1,0:T(8,128)(2,1)S(1)}, bf16[4,2,32,256]{3,2,1,0:T(8,128)(2,1)S(1)}, u32[]{:S(2)}, u32[]{:S(2)}) collective-permute-start(bf16[4,2,32,256]{3,2,1,0:T(8,128)(2,1)S(1)} %collective-permute-done.5.k3), channel_id=1, source_target_pairs={{0,1},{1,0},{2,3},{3,2},{4,5},{5,4},{6,7},{7,6},{8,9},{9,8},{10,11... | collective-permute-start | bytes 393224 | tf_op jit(solution)/shard_map/ppermute | solution.py:354
  37.3 6.7 %collective-permute-start.8 = (bf16[4,2,32,256]{3,2,1,0:T(8,128)(2,1)S(1)}, bf16[4,2,32,256]{3,2,1,0:T(8,128)(2,1)S(1)}, u32[]{:S(2)}, u32[]{:S(2)}) collective-permute-start(bf16[4,2,32,256]{3,2,1,0:T(8,128)(2,1)S(1)} %collective-permute-done.4.k2), channel_id=1, source_target_pairs={{0,1},{1,0},{2,3},{3,2},{4,5},{5,4},{6,7},{7,6},{8,9},{9,8},{10,11... | collective-permute-start | bytes 393224 | tf_op jit(solution)/shard_map/ppermute | solution.py:354
  37.8 6.2 %collective-permute-start.7 = (bf16[4,2,32,256]{3,2,1,0:T(8,128)(2,1)S(1)}, bf16[4,2,32,256]{3,2,1,0:T(8,128)(2,1)S(1)}, u32[]{:S(2)}, u32[]{:S(2)}) collective-permute-start(bf16[4,2,32,256]{3,2,1,0:T(8,128)(2,1)S(1)} %collective-permute-done.3.k1), channel_id=1, source_target_pairs={{0,1},{1,0},{2,3},{3,2},{4,5},{5,4},{6,7},{7,6},{8,9},{9,8},{10,11... | collective-permute-start | bytes 393224 | tf_op jit(solution)/shard_map/ppermute | solution.py:354
  37.9 4.2 %collective-permute-start.2 = (bf16[144,384]{1,0:T(8,128)(2,1)S(1)}, bf16[144,384]{1,0:T(8,128)(2,1)S(1)}, u32[]{:S(2)}, u32[]{:S(2)}) collective-permute-start(bf16[144,384]{1,0:T(8,128)(2,1)S(1)} %get-tuple-element.49), channel_id=1, source_target_pairs={{0,12},{4,0},{8,4},{12,8},{1,13},{5,1},{9,5},{13,9},{2,14},{6,2},{... | collective-permute-start | bytes 331784 | tf_op jit(solution)/shard_map/ppermute | solution.py:354
  45.9 3.9 %collective-permute-start.12 = (f32[8,128]{1,0:T(8,128)S(1)}, f32[8,128]{1,0:T(8,128)S(1)}, u32[]{:S(2)}, u32[]{:S(2)}) collective-permute-start(f32[8,128]{1,0:T(8,128)S(1)} %get-tuple-element.61.l0), channel_id=1, source_target_pairs={{0,12},{4,0},{8,4},{12,8},{1,13},{5,1},{9,5},{13,9},{2,14},{6,2},{... | collective-permute-start | bytes 12296 | tf_op jit(solution)/shard_map/ppermute | solution.py:354
  46.6 4.0 %collective-permute-start.11 = (f32[8,128]{1,0:T(8,128)S(1)}, f32[8,128]{1,0:T(8,128)S(1)}, u32[]{:S(2)}, u32[]{:S(2)}) collective-permute-start(f32[8,128]{1,0:T(8,128)S(1)} %get-tuple-element.61.l0), channel_id=1, source_target_pairs={{0,8},{4,12},{8,0},{12,4},{1,9},{5,13},{9,1},{13,5},{2,10},{6,14},... | collective-permute-start | bytes 12296 | tf_op jit(solution)/shard_map/ppermute | solution.py:354
  47.0 3.8 %collective-permute-start.10 = (f32[8,128]{1,0:T(8,128)S(1)}, f32[8,128]{1,0:T(8,128)S(1)}, u32[]{:S(2)}, u32[]{:S(2)}) collective-permute-start(f32[8,128]{1,0:T(8,128)S(1)} %get-tuple-element.61.l0), channel_id=1, source_target_pairs={{0,4},{4,8},{8,12},{12,0},{1,5},{5,9},{9,13},{13,1},{2,6},{6,10},{... | collective-permute-start | bytes 12296 | tf_op jit(solution)/shard_map/ppermute | solution.py:354
  51.8 5.6 %collective-permute-start.13 = (bf16[4,4,2,32,256]{4,3,2,1,0:T(8,128)(2,1)S(1)}, bf16[4,4,2,32,256]{4,3,2,1,0:T(8,128)(2,1)S(1)}, u32[]{:S(2)}, u32[]{:S(2)}) collective-permute-start(bf16[4,4,2,32,256]{4,3,2,1,0:T(8,128)(2,1)S(1)} %get-tuple-element.69), channel_id=1, source_target_pairs={{0,1},{1,0},{2,3},{3,2},{4,5},{5,4},{6,7},{7,6},{8,9},{9,8},{10,11... | collective-permute-start | bytes 1572872 | tf_op jit(solution)/shard_map/ppermute | solution.py:354
  57.6 5.2 %collective-permute-start.14 = (bf16[4,2,32,256]{3,2,1,0:T(8,128)(2,1)S(1)}, bf16[4,2,32,256]{3,2,1,0:T(8,128)(2,1)S(1)}, u32[]{:S(2)}, u32[]{:S(2)}) collective-permute-start(bf16[4,2,32,256]{3,2,1,0:T(8,128)(2,1)S(1)} %get-tuple-element.71), channel_id=1, source_target_pairs={{0,48},{16,0},{32,16},{48,32},{1,49},{17,1},{33,17},{49,33},{2,50}... | collective-permute-start | bytes 393224 | tf_op jit(solution)/shard_map/ppermute | solution.py:354
  59.8 6.1 %collective-permute-start.15 = (bf16[4,2,32,256]{3,2,1,0:T(8,128)(2,1)S(1)}, bf16[4,2,32,256]{3,2,1,0:T(8,128)(2,1)S(1)}, u32[]{:S(2)}, u32[]{:S(2)}) collective-permute-start(bf16[4,2,32,256]{3,2,1,0:T(8,128)(2,1)S(1)} %get-tuple-element.72), channel_id=1, source_target_pairs={{0,32},{16,48},{32,0},{48,16},{1,33},{17,49},{33,1},{49,17},{2,34}... | collective-permute-start | bytes 393224 | tf_op jit(solution)/shard_map/ppermute | solution.py:354
  61.0 8.5 %collective-permute-start.16 = (bf16[4,2,32,256]{3,2,1,0:T(8,128)(2,1)S(1)}, bf16[4,2,32,256]{3,2,1,0:T(8,128)(2,1)S(1)}, u32[]{:S(2)}, u32[]{:S(2)}) collective-permute-start(bf16[4,2,32,256]{3,2,1,0:T(8,128)(2,1)S(1)} %get-tuple-element.73), channel_id=1, source_target_pairs={{0,16},{16,32},{32,48},{48,0},{1,17},{17,33},{33,49},{49,1},{2,18}... | collective-permute-start | bytes 393224 | tf_op jit(solution)/shard_map/ppermute | solution.py:354
  61.1 1.5 %collective-permute-start.17 = (f32[8,128]{1,0:T(8,128)S(1)}, f32[8,128]{1,0:T(8,128)S(1)}, u32[]{:S(2)}, u32[]{:S(2)}) collective-permute-start(f32[8,128]{1,0:T(8,128)S(1)} %get-tuple-element.74.hg), channel_id=1, source_target_pairs={{0,1},{1,0},{2,3},{3,2},{4,5},{5,4},{6,7},{7,6},{8,9},{9,8},{10,11... | collective-permute-start | bytes 12296 | tf_op jit(solution)/shard_map/ppermute | solution.py:354
  70.3 17.4 %all-to-all-start.1 = ((bf16[32,8,384]{2,1,0:T(8,128)(2,1)}), bf16[32,8,384]{2,1,0:T(8,128)(2,1)S(1)}, u32[]{:S(2)}, u32[]{:S(2)}) async-start(bf16[32,8,384]{2,1,0:T(8,128)(2,1)} %bitcast.9), calls=%async_computation.1 | async-start | bytes 393216 | tf_op jit(solution)/shard_map/all_to_all | solution.py:454
  74.5 5.7 %collective-permute-start.18 = (bf16[128,384]{1,0:T(8,128)(2,1)S(1)}, bf16[128,384]{1,0:T(8,128)(2,1)S(1)}, u32[]{:S(2)}, u32[]{:S(2)}) collective-permute-start(bf16[128,384]{1,0:T(8,128)(2,1)S(1)} %get-tuple-element.77), channel_id=1, source_target_pairs={{0,12},{4,0},{8,4},{12,8},{1,13},{5,1},{9,5},{13,9},{2,14},{6,2},{... | collective-permute-start | bytes 294920 | tf_op jit(solution)/shard_map/ppermute | solution.py:354
  77.1 5.9 %collective-permute-start.19 = (bf16[128,384]{1,0:T(8,128)(2,1)S(1)}, bf16[128,384]{1,0:T(8,128)(2,1)S(1)}, u32[]{:S(2)}, u32[]{:S(2)}) collective-permute-start(bf16[128,384]{1,0:T(8,128)(2,1)S(1)} %get-tuple-element.78), channel_id=1, source_target_pairs={{0,8},{4,12},{8,0},{12,4},{1,9},{5,13},{9,1},{13,5},{2,10},{6,14},... | collective-permute-start | bytes 294920 | tf_op jit(solution)/shard_map/ppermute | solution.py:354
  77.6 9.1 %collective-permute-start.20 = (bf16[128,384]{1,0:T(8,128)(2,1)S(1)}, bf16[128,384]{1,0:T(8,128)(2,1)S(1)}, u32[]{:S(2)}, u32[]{:S(2)}) collective-permute-start(bf16[128,384]{1,0:T(8,128)(2,1)S(1)} %get-tuple-element.79), channel_id=1, source_target_pairs={{0,4},{4,8},{8,12},{12,0},{1,5},{5,9},{9,13},{13,1},{2,6},{6,10},{... | collective-permute-start | bytes 294920 | tf_op jit(solution)/shard_map/ppermute | solution.py:354

commit v5 on v4

--- a/solution.py
+++ b/solution.py
@@ -96,13 +96,33 @@
     return lax.dot_general(a, b, NT, preferred_element_type=F32)
 
 
-def scores_half(cc, place, q, seg, w, kvs, kv_out, p_out, top_out, sums_out, s_buf, u_rows):
-    _, x, y, zh, c = place
-    for kx in range(4):
+def place_kernel(k0, k1, k2, k3, kv_out):
+    for kx, ref in enumerate((k0, k1, k2, k3)):
         for ys in range(4):
             for z in range(2):
                 row = ys * HALF + z * BLOCK + kx * 32
-                kv_out[row : row + 32, :] = kvs[kx][ys, z]
+                kv_out[row : row + 32, :] = ref[ys, z]
+
+
+def eye_of():
+    return jnp.where(
+        lax.broadcasted_iota(jnp.int32, (BLOCK, BLOCK), 0) == lax.broadcasted_iota(jnp.int32, (BLOCK, BLOCK), 1), 1.0, 0.0
+    ).astype(BF16)
+
+
+def columns_half(w, y, kv, kt, u):
+    eye = eye_of()
+    pad = jnp.zeros((BLOCK - 8, HEAD_WIDTH), F32)
+    high, low = halves(jnp.concatenate([stack8([head_diff(w, y, h) for h in range(GROUP)]), pad], axis=0))
+    high, low = high.astype(BF16), low.astype(BF16)
+    for n in range(2):
+        rows = slice(n * 2 * HALF, (n + 1) * 2 * HALF)
+        kt[:, rows] = times_t(eye, kv[rows, :HEAD_WIDTH]).astype(BF16)
+        u[rows, :] = times_t(kv[rows, HEAD_WIDTH:], high) + times_t(kv[rows, HEAD_WIDTH:], low)
+
+
+def scores_half(cc, place, q, seg, w, kv_out, p_out, top_out, sums_out, s_buf, u_rows):
+    _, x, y, zh, c = place
     diffs16 = on_both(stack8([head_diff(w, y, h) for h in range(GROUP)]))
     ones = stack8([jnp.zeros((1, 2 * HALF), F32)] * GROUP + [jnp.ones((1, 2 * HALF), F32)])
     for n in range(2):
@@ -152,22 +172,25 @@
         sums_out[ys] = sums
 
 
-def near_kernel(did, seg, w, q0, q1, q2, q3, k0, k1, k2, k3, q_out, kv_out, p_out, top_out, sums_out, s_buf, u_rows):
+def near_kernel(did, seg, w, q0, q1, q2, q3, kv, q_out, qt_out, kt, u, p_out, top_out, sums_out, s_buf, u_rows):
     place = coords(did)
     y = place[2]
     for k, ref in enumerate((q0, q1, q2, q3)):
         slot = (y - k + 4) % 4
         for h in range(GROUP):
             q_out[slot, h * BLOCK : (h + 1) * BLOCK, :] = ref[:BLOCK, h * HEAD_WIDTH : (h + 1) * HEAD_WIDTH]
-    scores_half(0, place, q_out, seg, w, (k0, k1, k2, k3), kv_out, p_out, top_out, sums_out, s_buf, u_rows)
+    scores_half(0, place, q_out, seg, w, kv, p_out, top_out, sums_out, s_buf, u_rows)
+    for ys in range(4):
+        qt_out[ys] = times_t(eye_of(), q_out[ys]).astype(BF16)
+    columns_half(w, y, kv, kt, u)
 
 
 def rest_kernel(
-    did, seg, w, q, top0, sums0, k0, k1, k2, k3, plog, inv_out, delta_out, alpha_out, kv_out, p_out, top, sums, s_buf, u_rows
+    did, seg, w, q, top0, sums0, kv, plog, inv_out, delta_out, alpha_out, p_out, top, sums, s_buf, u_rows
 ):
     place = coords(did)
     y = place[2]
-    scores_half(1, place, q, seg, w, (k0, k1, k2, k3), kv_out, p_out, top, sums, s_buf, u_rows)
+    scores_half(1, place, q, seg, w, kv, p_out, top, sums, s_buf, u_rows)
     plog[...] = jnp.zeros_like(plog)
     row8 = lax.broadcasted_iota(jnp.int32, (8, WIDE), 0)
     for ys in range(4):
@@ -186,23 +209,12 @@
         plog[pl.ds((y - ys + 4) % 4, 1), :] = lg
 
 
-def middle_kernel(did, w, p0, p1, delta, alpha, q, kv0, kv1, g0, g1, dq_out, qt_out, kt, u):
+def middle_kernel(did, w, p0, p1, delta, alpha, kv1, kt0, u0, g0, g1, dq_out, kt1, u1):
     _, _, y, _, _ = coords(did)
-    eye = jnp.where(
-        lax.broadcasted_iota(jnp.int32, (BLOCK, BLOCK), 0) == lax.broadcasted_iota(jnp.int32, (BLOCK, BLOCK), 1), 1.0, 0.0
-    ).astype(BF16)
-    pad = jnp.zeros((BLOCK - 8, HEAD_WIDTH), F32)
-    high, low = halves(jnp.concatenate([stack8([head_diff(w, y, h) for h in range(GROUP)]), pad], axis=0))
-    high, low = high.astype(BF16), low.astype(BF16)
-    for half, kv in enumerate((kv0, kv1)):
-        for n in range(2):
-            rows = slice(n * 2 * HALF, (n + 1) * 2 * HALF)
-            kt[half, :, rows] = times_t(eye, kv[rows, :HEAD_WIDTH]).astype(BF16)
-            u[half, rows, :] = times_t(kv[rows, HEAD_WIDTH:], high) + times_t(kv[rows, HEAD_WIDTH:], low)
-    for ys in range(4):
-        qt_out[ys] = times_t(eye, q[ys]).astype(BF16)
+    columns_half(w, y, kv1, kt1, u1)
+    for ys in range(4):
         total = jnp.zeros((HEAD_WIDTH, WIDE), F32)
-        for half, (p, g) in enumerate(((p0, g0), (p1, g1))):
+        for half, (p, g, kt, u) in enumerate(((p0, g0, kt0, u0), (p1, g1, kt1, u1))):
             dqt = jnp.zeros((HEAD_WIDTH, WIDE), F32)
             for i, ch in enumerate(CHUNKS[ys]):
                 at_p = (P_AT[ys] + i) * HALF
@@ -210,12 +222,12 @@
                     row = ch * HALF + z * BLOCK
                     at = slice(at_p + z * BLOCK, at_p + (z + 1) * BLOCK)
                     ub = jnp.concatenate(
-                        [jnp.broadcast_to(u[half, row : row + BLOCK, h : h + 1], (BLOCK, BLOCK)) for h in range(GROUP)],
+                        [jnp.broadcast_to(u[row : row + BLOCK, h : h + 1], (BLOCK, BLOCK)) for h in range(GROUP)],
                         axis=1,
                     )
                     g[at, :] = (p[at, :].astype(F32) * (ub - delta[ys, 0:1, :])).astype(BF16)
                 dqt = dqt + jnp.dot(
-                    kt[half, :, ch * HALF : (ch + 1) * HALF], g[at_p : at_p + HALF, :], preferred_element_type=F32
+                    kt[:, ch * HALF : (ch + 1) * HALF], g[at_p : at_p + HALF, :], preferred_element_type=F32
                 )
             total = total + dqt * alpha[ys, half : half + 1, :]
         dq_out[ys] = total
@@ -402,35 +414,44 @@
     over_x = [own]
     for k in range(1, 4):
         over_x.append(shift(own, "x", 4, k))
-    over_c = [shift(a, "c", 2, 1) for a in over_x]
+    half_kv = like((4 * HALF, 256), BF16)
+    (kv0,) = call(place_kernel, [half_kv], [VMEM] * 4)(*over_x)
+    kv1 = shift(kv0, "c", 2, 1)
     for k in range(1, 4):
         packs[k] = shift(packs[k], "y", 4, k)
     half_p = like((7 * HALF, WIDE), BF16)
-    half_kv = like((4 * HALF, 256), BF16)
     row_set = like((4, 8, WIDE), F32)
     wide_set = like((4, HEAD_WIDTH, WIDE), BF16)
     half_scratch = [pltpu.VMEM((3 * HALF, WIDE), F32), pltpu.VMEM((16, 4 * HALF), BF16)]
-    q, kv0, p0, top0, sums0 = call(
+    q, qt, kt0, u0, p0, top0, sums0 = call(
         near_kernel,
-        [like((4, WIDE, HEAD_WIDTH), BF16), half_kv, half_p, row_set, like((4, 16, WIDE), F32)],
-        [SMEM] + [VMEM] * 10,
+        [
+            like((4, WIDE, HEAD_WIDTH), BF16),
+            wide_set,
+            like((HEAD_WIDTH, 4 * HALF), BF16),
+            like((4 * HALF, BLOCK), F32),
+            half_p,
+            row_set,
+            like((4, 16, WIDE), F32),
+        ],
+        [SMEM] + [VMEM] * 7,
         scratch=half_scratch,
-    )(did, seg, w, *packs, *over_x)
-    plog, inv, delta, alpha, kv1, p1 = call(
+    )(did, seg, w, *packs, kv0)
+    plog, inv, delta, alpha, p1 = call(
         rest_kernel,
-        [like((8, BLOCK), F32), row_set, row_set, row_set, half_kv, half_p],
-        [SMEM] + [VMEM] * 9,
+        [like((8, BLOCK), F32), row_set, row_set, row_set, half_p],
+        [SMEM] + [VMEM] * 6,
         scratch=[pltpu.VMEM((4, 8, WIDE), F32), pltpu.VMEM((4, 16, WIDE), F32)] + half_scratch,
-    )(did, seg, w, q, top0, sums0, *over_c)
+    )(did, seg, w, q, top0, sums0, kv1)
     logs = [plog]
     for k in range(1, 4):
         logs.append(shift(plog, "y", 4, k))
-    g0, g1, dqt, qt = call(
+    g0, g1, dqt = call(
         middle_kernel,
-        [half_p, half_p, like((4, HEAD_WIDTH, WIDE), F32), wide_set],
+        [half_p, half_p, like((4, HEAD_WIDTH, WIDE), F32)],
         [SMEM] + [VMEM] * 8,
-        scratch=[pltpu.VMEM((2, HEAD_WIDTH, 4 * HALF), BF16), pltpu.VMEM((2, 4 * HALF, BLOCK), F32)],
-    )(did, w, p0, p1, delta, alpha, q, kv0, kv1)
+        scratch=[pltpu.VMEM((HEAD_WIDTH, 4 * HALF), BF16), pltpu.VMEM((4 * HALF, BLOCK), F32)],
+    )(did, w, p0, p1, delta, alpha, kv1, kt0, u0)
     factor_scratch = [pltpu.VMEM((4, HEAD_WIDTH, WIDE), BF16), pltpu.VMEM((4, HEAD_WIDTH, WIDE), BF16)]
     far_d, f, wt, loss_rows = call(
         far_kernel,

time: 88.9 us -> 90.9 us (1.022)
  starting transfers between devices: 27.5 us -> 29.4 us
    ppermute x21 -> x18, starting transfers between devices: 23.3 us -> 25.5 us  [shift(): return lax.ppermute(v, axis, [(i, (i + k) % size) for i in range(size)])]
    pallas_call x2 -> x3, Pallas kernels: 4.2 us -> 4.46 us  [the longest x1 2.28 us: per_device(): call(near_kernel, [like((4, WIDE, HEAD_WIDTH), BF16), wide_set, like((HEA...]
    ppermute x21 -> x18, waiting for transfers between devices: 25.9 us -> 25.8 us  [shift(): return lax.ppermute(v, axis, [(i, (i + k) % size) for i in range(size)])]
  transfers between devices with their start and end apart: 22 -> 19, of which waited for: 11 -> 13; matrix products, arithmetic and copies ran while one was open for 0% -> 0% of each run, Pallas kernels for 9% -> 9%
where the time goes in v5:
time: 90.9 us; the launch traced here: 90.6 us
  starting transfers between devices  29.4 us (32%)
  waiting for transfers between devices  25.8 us (28%)
  blocking collectives  21 us (23%)
  Pallas kernels  13.5 us (15%)
    ppermute x18, waiting for transfers between devices, shift(): return lax.ppermute(v, axis, [(i, (i + k) % size) for i in range(size)])  25.8 us
    ppermute x18, starting transfers between devices, shift(): return lax.ppermute(v, axis, [(i, (i + k) % size) for i in range(size)])  25.5 us
    all_to_all x1, blocking collectives, per_device(): lax.all_to_all(copies.reshape(32, 8, 256), YZ_AXES, 0, 0, tiled=True)  21 us
    all_to_all x1, starting transfers between devices, per_device(): lax.all_to_all(by_z.reshape(32, 8, WIDE), YZ_AXES, 0, 0, tiled=True)  3.86 us
    pallas_call x1, Pallas kernels, per_device(): call(near_kernel, [like((4, WIDE, HEAD_WIDTH), BF16), wide_set, like((HEA...  2.28 us
    pallas_call x1, Pallas kernels, per_device(): call(middle_kernel, [half_p, half_p, like((4, HEAD_WIDTH, WIDE), F32)], [...  2.14 us
    pallas_call x1, Pallas kernels, per_device(): call(rest_kernel, [like((8, BLOCK), F32), row_set, row_set, row_set, half...  1.85 us
  transfers between devices with their start and end apart: 19, of which 13 were waited for; matrix products, arithmetic and copies ran while one was open for 0% of the time, Pallas kernels for 9%

profile of v5, /device:TPU:1, one launch (start us, length us, event | category | flops | bytes accessed | tf_op | source)
XLA Modules:
  0.0 90.6 jit_solution(5211329102904923265)
XLA Ops:
  0.6 0.7 shard_map.111
  1.4 21.0 %all_to_all.10 = bf16[32,8,256]{2,1,0:T(8,128)(2,1)S(1)} all-to-all(bf16[32,8,256]{2,1,0:T(8,128)(2,1)S(1)} %bitcast.17), channel_id=1, replica_groups=mesh['zl'=4,'x'=4,'y'=4,'zh'=2,'c'=2] {'y','zh','zl'}, dimensions={0} | all-to-all | bytes 262144 | tf_op jit(solution)/shard_map/all_to_all | solution.py:396
  22.4 1.2 %collective-permute-start.3 = (bf16[4,2,32,256]{3,2,1,0:T(8,128)(2,1)S(1)}, bf16[4,2,32,256]{3,2,1,0:T(8,128)(2,1)S(1)}, u32[]{:S(2)}, u32[]{:S(2)}) collective-permute-start(bf16[4,2,32,256]{3,2,1,0:T(8,128)(2,1)S(1)} %bitcast.18), channel_id=1, source_target_pairs={{0,16},{16,32},{32,48},{48,0},{1,17},{17,33},{33,49},{49,1},{2,18}... | collective-permute-start | bytes 393224 | tf_op jit(solution)/shard_map/ppermute | solution.py:366
  23.6 2.5 %collective-permute-start.4 = (bf16[4,2,32,256]{3,2,1,0:T(8,128)(2,1)S(1)}, bf16[4,2,32,256]{3,2,1,0:T(8,128)(2,1)S(1)}, u32[]{:S(2)}, u32[]{:S(2)}) collective-permute-start(bf16[4,2,32,256]{3,2,1,0:T(8,128)(2,1)S(1)} %bitcast.19), channel_id=1, source_target_pairs={{0,32},{16,48},{32,0},{48,16},{1,33},{17,49},{33,1},{49,17},{2,34}... | collective-permute-start | bytes 393224 | tf_op jit(solution)/shard_map/ppermute | solution.py:366
  26.0 1.2 %collective-permute-start.5 = (bf16[4,2,32,256]{3,2,1,0:T(8,128)(2,1)S(1)}, bf16[4,2,32,256]{3,2,1,0:T(8,128)(2,1)S(1)}, u32[]{:S(2)}, u32[]{:S(2)}) collective-permute-start(bf16[4,2,32,256]{3,2,1,0:T(8,128)(2,1)S(1)} %bitcast.20), channel_id=1, source_target_pairs={{0,48},{16,0},{32,16},{48,32},{1,49},{17,1},{33,17},{49,33},{2,50}... | collective-permute-start | bytes 393224 | tf_op jit(solution)/shard_map/ppermute | solution.py:366
  27.4 2.7 %collective-permute-done.4.k2 = bf16[4,2,32,256]{3,2,1,0:T(8,128)(2,1)S(1)} collective-permute-done((bf16[4,2,32,256]{3,2,1,0:T(8,128)(2,1)S(1)}, bf16[4,2,32,256]{3,2,1,0:T(8,128)(2,1)S(1)}, u32[]{:S(2)}, u32[]{:S(2)}) %collective-permute-start.4) | collective-permute-done | bytes 131104 | tf_op jit(solution)/shard_map/ppermute | solution.py:366
  30.6 3.1 %collective-permute-start.6 = (bf16[1024,256]{1,0:T(8,128)(2,1)S(1)}, bf16[1024,256]{1,0:T(8,128)(2,1)S(1)}, u32[]{:S(2)}, u32[]{:S(2)}) collective-permute-start(bf16[1024,256]{1,0:T(8,128)(2,1)S(1)} %shard_map.112.kv.kv0), channel_id=1, source_target_pairs={{0,1},{1,0},{2,3},{3,2},{4,5},{5,4},{6,7},{7,6},{8,9},{9,8},{10,11... | collective-permute-start | bytes 1572872 | tf_op jit(solution)/shard_map/ppermute | solution.py:366
  33.7 1.2 %shard_map.110 = (bf16[144,384]{1,0:T(8,128)(2,1)S(1)}, bf16[144,384]{1,0:T(8,128)(2,1)S(1)}, bf16[144,384]{1,0:T(8,128)(2,1)S(1)}, bf16[144,384]{1,0:T(8,128)(2...) custom-call(s32[1]{0:T(128)} %bitcast.did, s32[1,128]{1,0:T(1,128)} %bitcast.26, s32[1,128]{1,0:T(1,128)} %bitcast.27, ...), custom_call_target="tpu_custom_call" | custom-call | tf_op jit(solution)/shard_map/pallas_call | solution.py:397
  35.3 1.7 %collective-permute-start.1 = (bf16[144,384]{1,0:T(8,128)(2,1)S(1)}, bf16[144,384]{1,0:T(8,128)(2,1)S(1)}, u32[]{:S(2)}, u32[]{:S(2)}) collective-permute-start(bf16[144,384]{1,0:T(8,128)(2,1)S(1)} %get-tuple-element.48), channel_id=1, source_target_pairs={{0,8},{4,12},{8,0},{12,4},{1,9},{5,13},{9,1},{13,5},{2,10},{6,14},... | collective-permute-start | bytes 331784 | tf_op jit(solution)/shard_map/ppermute | solution.py:366
  37.1 1.2 %collective-permute-start.2 = (bf16[144,384]{1,0:T(8,128)(2,1)S(1)}, bf16[144,384]{1,0:T(8,128)(2,1)S(1)}, u32[]{:S(2)}, u32[]{:S(2)}) collective-permute-start(bf16[144,384]{1,0:T(8,128)(2,1)S(1)} %get-tuple-element.49), channel_id=1, source_target_pairs={{0,12},{4,0},{8,4},{12,8},{1,13},{5,1},{9,5},{13,9},{2,14},{6,2},{... | collective-permute-start | bytes 331784 | tf_op jit(solution)/shard_map/ppermute | solution.py:366
  38.2 4.9 %collective-permute-done.q1.g1 = bf16[144,384]{1,0:T(8,128)(2,1)S(1)} collective-permute-done((bf16[144,384]{1,0:T(8,128)(2,1)S(1)}, bf16[144,384]{1,0:T(8,128)(2,1)S(1)}, u32[]{:S(2)}, u32[]{:S(2)}) %collective-permute-start) | collective-permute-done | bytes 110624 | tf_op jit(solution)/shard_map/ppermute | solution.py:366
  43.5 2.3 %shard_map.113 = (bf16[4,384,128]{2,1,0:T(8,128)(2,1)S(1)}, bf16[4,128,384]{2,1,0:T(8,128)(2,1)S(1)}, bf16[128,1024]{1,0:T(8,128)(2,1)S(1)}, f32[1024,128]{1,0:T...) custom-call(s32[1]{0:T(128)} %bitcast.did, ...), custom_call_target="tpu_custom_call" | custom-call | tf_op jit(solution)/shard_map/pallas_call | solution.py:426
  45.8 1.9 %shard_map.114 = (f32[8,128]{1,0:T(8,128)S(1)}, f32[4,8,384]{2,1,0:T(8,128)S(1)}, f32[4,8,384]{2,1,0:T(8,128)S(1)}, f32[4,8,384]{2,1,0:T(8,128)S(1)}, bf16[1792,384]{1,0:T(8,128)(2,1)S(1)}) custom-call(s32[1]{0:T(128)} %bitcast.did, s32[1,2048]{1,0:T(1,128)S(1)} %get-tuple-element.44.seg, f32[2,1536]{1,0:T(2,128)S(1)} %get-tuple-element.45.w, ...), custom_call_target="tpu_custom_call" | custom-call | tf_op jit(solution)/shard_map/pallas_call | solution.py:440
  47.6 1.2 %collective-permute-start.7 = (f32[8,128]{1,0:T(8,128)S(1)}, f32[8,128]{1,0:T(8,128)S(1)}, u32[]{:S(2)}, u32[]{:S(2)}) collective-permute-start(f32[8,128]{1,0:T(8,128)S(1)} %get-tuple-element.61.l0), channel_id=1, source_target_pairs={{0,4},{4,8},{8,12},{12,0},{1,5},{5,9},{9,13},{13,1},{2,6},{6,10},{... | collective-permute-start | bytes 12296 | tf_op jit(solution)/shard_map/ppermute | solution.py:366
  48.9 3.1 %collective-permute-start.8 = (f32[8,128]{1,0:T(8,128)S(1)}, f32[8,128]{1,0:T(8,128)S(1)}, u32[]{:S(2)}, u32[]{:S(2)}) collective-permute-start(f32[8,128]{1,0:T(8,128)S(1)} %get-tuple-element.61.l0), channel_id=1, source_target_pairs={{0,8},{4,12},{8,0},{12,4},{1,9},{5,13},{9,1},{13,5},{2,10},{6,14},... | collective-permute-start | bytes 12296 | tf_op jit(solution)/shard_map/ppermute | solution.py:366
  52.0 2.1 %shard_map.115 = (bf16[1792,384]{1,0:T(8,128)(2,1)S(1)}, bf16[1792,384]{1,0:T(8,128)(2,1)S(1)}, f32[4,128,384]{2,1,0:T(8,128)S(1)}) custom-call(s32[1]{0:T(128)} %bitcast.did, f32[2,1536]{1,0:T(2,128)S(1)} %get-tuple-element.45.w, bf16[1792,384]{1,0:T(8,128)(2,1)S(1)} %get-tuple-element.50.p0, bf16[1792,384]{1,0:T(8,128)(2,1)S(1)} %get-tuple-element.54.p1.p, ...), custom_call_target="tpu_custom_call" | custom-call | tf_op jit(solution)/shard_map/pallas_call | solution.py:449
  54.4 1.0 %shard_map.116 = (bf16[4,4,2,32,256]{4,3,2,1,0:T(8,128)(2,1)S(1)}, f32[4,8,384]{2,1,0:T(8,128)S(1)}, f32[128,384]{1,0:T(8,128)S(1)}, f32[8,128]{1,0:T(8,128)S(1)}) custom-call(s32[1]{0:T(128)} %bitcast.did, f32[2,1536]{1,0:T(2,128)S(1)} %get-tuple-element.45.w, f32[8,128]{1,0:T(8,128)S(1)} %get-tuple-element.61.l0, f32[8,128]{1,0:T(8,128)S(1)} %collective-permute-done.7.l1, ...), custom_call_target="tpu_custom_call" | custom-call | tf_op jit(solution)/shard_map/pallas_call | solution.py:456
  55.4 2.3 %collective-permute-start.10 = (bf16[4,4,2,32,256]{4,3,2,1,0:T(8,128)(2,1)S(1)}, bf16[4,4,2,32,256]{4,3,2,1,0:T(8,128)(2,1)S(1)}, u32[]{:S(2)}, u32[]{:S(2)}) collective-permute-start(bf16[4,4,2,32,256]{4,3,2,1,0:T(8,128)(2,1)S(1)} %get-tuple-element.69), channel_id=1, source_target_pairs={{0,1},{1,0},{2,3},{3,2},{4,5},{5,4},{6,7},{7,6},{8,9},{9,8},{10,11... | collective-permute-start | bytes 1572872 | tf_op jit(solution)/shard_map/ppermute | solution.py:366
  57.7 1.8 %shard_map.117 = (bf16[4,4,2,32,256]{4,3,2,1,0:T(8,128)(2,1)S(1)}, f32[8,128]{1,0:T(8,128)S(1)}, bf16[128,384]{1,0:T(8,128)(2,1)S(1)}, bf16[128,384]{1,0:T(8,128...) custom-call(s32[1]{0:T(128)} %bitcast.did, bf16[1792,384]{1,0:T(8,128)(2,1)S(1)} %get-tuple-element.50.p0, ...), custom_call_target="tpu_custom_call" | custom-call | tf_op jit(solution)/shard_map/pallas_call | solution.py:463
  59.7 2.5 %collective-permute-start.11 = (bf16[4,2,32,256]{3,2,1,0:T(8,128)(2,1)S(1)}, bf16[4,2,32,256]{3,2,1,0:T(8,128)(2,1)S(1)}, u32[]{:S(2)}, u32[]{:S(2)}) collective-permute-start(bf16[4,2,32,256]{3,2,1,0:T(8,128)(2,1)S(1)} %get-tuple-element.71), channel_id=1, source_target_pairs={{0,48},{16,0},{32,16},{48,32},{1,49},{17,1},{33,17},{49,33},{2,50}... | collective-permute-start | bytes 393224 | tf_op jit(solution)/shard_map/ppermute | solution.py:366
  62.8 0.9 collective-permute-start.14
  63.7 0.8 collective-permute-done.14.hg_far
  64.5 3.0 %collective-permute-done.11.b1 = bf16[4,2,32,256]{3,2,1,0:T(8,128)(2,1)S(1)} collective-permute-done((bf16[4,2,32,256]{3,2,1,0:T(8,128)(2,1)S(1)}, bf16[4,2,32,256]{3,2,1,0:T(8,128)(2,1)S(1)}, u32[]{:S(2)}, u32[]{:S(2)}) %collective-permute-start.11) | collective-permute-done | bytes 131104 | tf_op jit(solution)/shard_map/ppermute | solution.py:366
  67.5 0.8 collective-permute-done.12.b2
  68.3 3.5 %collective-permute-done.13.b3 = bf16[4,2,32,256]{3,2,1,0:T(8,128)(2,1)S(1)} collective-permute-done((bf16[4,2,32,256]{3,2,1,0:T(8,128)(2,1)S(1)}, bf16[4,2,32,256]{3,2,1,0:T(8,128)(2,1)S(1)}, u32[]{:S(2)}, u32[]{:S(2)}) %collective-permute-start.13) | collective-permute-done | bytes 131104 | tf_op jit(solution)/shard_map/ppermute | solution.py:366
  71.9 0.8 shard_map.119
  72.6 3.9 %all-to-all-start.1 = ((bf16[32,8,384]{2,1,0:T(8,128)(2,1)}), bf16[32,8,384]{2,1,0:T(8,128)(2,1)S(1)}, u32[]{:S(2)}, u32[]{:S(2)}) async-start(bf16[32,8,384]{2,1,0:T(8,128)(2,1)} %bitcast.9), calls=%async_computation.1 | async-start | bytes 393216 | tf_op jit(solution)/shard_map/all_to_all | solution.py:475
  76.5 2.6 %collective-permute-start.15 = (bf16[128,384]{1,0:T(8,128)(2,1)S(1)}, bf16[128,384]{1,0:T(8,128)(2,1)S(1)}, u32[]{:S(2)}, u32[]{:S(2)}) collective-permute-start(bf16[128,384]{1,0:T(8,128)(2,1)S(1)} %get-tuple-element.77), channel_id=1, source_target_pairs={{0,12},{4,0},{8,4},{12,8},{1,13},{5,1},{9,5},{13,9},{2,14},{6,2},{... | collective-permute-start | bytes 294920 | tf_op jit(solution)/shard_map/ppermute | solution.py:366
  80.2 2.2 %collective-permute-done.15.d1 = bf16[128,384]{1,0:T(8,128)(2,1)S(1)} collective-permute-done((bf16[128,384]{1,0:T(8,128)(2,1)S(1)}, bf16[128,384]{1,0:T(8,128)(2,1)S(1)}, u32[]{:S(2)}, u32[]{:S(2)}) %collective-permute-start.15) | collective-permute-done | bytes 98336 | tf_op jit(solution)/shard_map/ppermute | solution.py:366
  82.3 2.7 %collective-permute-done.16.d2 = bf16[128,384]{1,0:T(8,128)(2,1)S(1)} collective-permute-done((bf16[128,384]{1,0:T(8,128)(2,1)S(1)}, bf16[128,384]{1,0:T(8,128)(2,1)S(1)}, u32[]{:S(2)}, u32[]{:S(2)}) %collective-permute-start.16) | collective-permute-done | bytes 98336 | tf_op jit(solution)/shard_map/ppermute | solution.py:366
  85.0 3.8 %collective-permute-done.17.d3 = bf16[128,384]{1,0:T(8,128)(2,1)S(1)} collective-permute-done((bf16[128,384]{1,0:T(8,128)(2,1)S(1)}, bf16[128,384]{1,0:T(8,128)(2,1)S(1)}, u32[]{:S(2)}, u32[]{:S(2)}) %collective-permute-start.17) | collective-permute-done | bytes 98336 | tf_op jit(solution)/shard_map/ppermute | solution.py:366
  88.8 0.9 %shard_map.121 = f32[128,1536]{1,0:T(8,128)} custom-call(s32[1]{0:T(128)} %bitcast.did, bf16[128,384]{1,0:T(8,128)(2,1)S(1)} %get-tuple-element.76.d0, bf16[128,384]{1,0:T(8,128)(2,1)S(1)} %collective-permute-done.15.d1, bf16[128,384]{1,0:T(8,128)(2,1)S(1)} %collective-permute-done.16.d2, bf16[128,384]{1,0:T(8,128)(2,1)S(1)} %collective-permute-done.17.d3), custom_call_target="tpu_custom_call" | custom-call | tf_op jit(solution)/shard_map/pallas_call | solution.py:479
  (19 shorter events, 4.4 us)
Async XLA Ops:
  22.4 5.0 %collective-permute-start.3 = (bf16[4,2,32,256]{3,2,1,0:T(8,128)(2,1)S(1)}, bf16[4,2,32,256]{3,2,1,0:T(8,128)(2,1)S(1)}, u32[]{:S(2)}, u32[]{:S(2)}) collective-permute-start(bf16[4,2,32,256]{3,2,1,0:T(8,128)(2,1)S(1)} %bitcast.18), channel_id=1, source_target_pairs={{0,16},{16,32},{32,48},{48,0},{1,17},{17,33},{33,49},{49,1},{2,18}... | collective-permute-start | bytes 393224 | tf_op jit(solution)/shard_map/ppermute | solution.py:366
  23.6 6.5 %collective-permute-start.4 = (bf16[4,2,32,256]{3,2,1,0:T(8,128)(2,1)S(1)}, bf16[4,2,32,256]{3,2,1,0:T(8,128)(2,1)S(1)}, u32[]{:S(2)}, u32[]{:S(2)}) collective-permute-start(bf16[4,2,32,256]{3,2,1,0:T(8,128)(2,1)S(1)} %bitcast.19), channel_id=1, source_target_pairs={{0,32},{16,48},{32,0},{48,16},{1,33},{17,49},{33,1},{49,17},{2,34}... | collective-permute-start | bytes 393224 | tf_op jit(solution)/shard_map/ppermute | solution.py:366
  26.0 4.6 %collective-permute-start.5 = (bf16[4,2,32,256]{3,2,1,0:T(8,128)(2,1)S(1)}, bf16[4,2,32,256]{3,2,1,0:T(8,128)(2,1)S(1)}, u32[]{:S(2)}, u32[]{:S(2)}) collective-permute-start(bf16[4,2,32,256]{3,2,1,0:T(8,128)(2,1)S(1)} %bitcast.20), channel_id=1, source_target_pairs={{0,48},{16,0},{32,16},{48,32},{1,49},{17,1},{33,17},{49,33},{2,50}... | collective-permute-start | bytes 393224 | tf_op jit(solution)/shard_map/ppermute | solution.py:366
  30.6 15.1 %collective-permute-start.6 = (bf16[1024,256]{1,0:T(8,128)(2,1)S(1)}, bf16[1024,256]{1,0:T(8,128)(2,1)S(1)}, u32[]{:S(2)}, u32[]{:S(2)}) collective-permute-start(bf16[1024,256]{1,0:T(8,128)(2,1)S(1)} %shard_map.112.kv.kv0), channel_id=1, source_target_pairs={{0,1},{1,0},{2,3},{3,2},{4,5},{5,4},{6,7},{7,6},{8,9},{9,8},{10,11... | collective-permute-start | bytes 1572872 | tf_op jit(solution)/shard_map/ppermute | solution.py:366
  34.9 8.2 %collective-permute-start = (bf16[144,384]{1,0:T(8,128)(2,1)S(1)}, bf16[144,384]{1,0:T(8,128)(2,1)S(1)}, u32[]{:S(2)}, u32[]{:S(2)}) collective-permute-start(bf16[144,384]{1,0:T(8,128)(2,1)S(1)} %get-tuple-element.47), channel_id=1, source_target_pairs={{0,4},{4,8},{8,12},{12,0},{1,5},{5,9},{9,13},{13,1},{2,6},{6,10},{... | collective-permute-start | bytes 331784 | tf_op jit(solution)/shard_map/ppermute | solution.py:366
  35.3 7.8 %collective-permute-start.1 = (bf16[144,384]{1,0:T(8,128)(2,1)S(1)}, bf16[144,384]{1,0:T(8,128)(2,1)S(1)}, u32[]{:S(2)}, u32[]{:S(2)}) collective-permute-start(bf16[144,384]{1,0:T(8,128)(2,1)S(1)} %get-tuple-element.48), channel_id=1, source_target_pairs={{0,8},{4,12},{8,0},{12,4},{1,9},{5,13},{9,1},{13,5},{2,10},{6,14},... | collective-permute-start | bytes 331784 | tf_op jit(solution)/shard_map/ppermute | solution.py:366
  37.1 6.4 %collective-permute-start.2 = (bf16[144,384]{1,0:T(8,128)(2,1)S(1)}, bf16[144,384]{1,0:T(8,128)(2,1)S(1)}, u32[]{:S(2)}, u32[]{:S(2)}) collective-permute-start(bf16[144,384]{1,0:T(8,128)(2,1)S(1)} %get-tuple-element.49), channel_id=1, source_target_pairs={{0,12},{4,0},{8,4},{12,8},{1,13},{5,1},{9,5},{13,9},{2,14},{6,2},{... | collective-permute-start | bytes 331784 | tf_op jit(solution)/shard_map/ppermute | solution.py:366
  47.6 6.5 %collective-permute-start.7 = (f32[8,128]{1,0:T(8,128)S(1)}, f32[8,128]{1,0:T(8,128)S(1)}, u32[]{:S(2)}, u32[]{:S(2)}) collective-permute-start(f32[8,128]{1,0:T(8,128)S(1)} %get-tuple-element.61.l0), channel_id=1, source_target_pairs={{0,4},{4,8},{8,12},{12,0},{1,5},{5,9},{9,13},{13,1},{2,6},{6,10},{... | collective-permute-start | bytes 12296 | tf_op jit(solution)/shard_map/ppermute | solution.py:366
  48.9 5.3 %collective-permute-start.8 = (f32[8,128]{1,0:T(8,128)S(1)}, f32[8,128]{1,0:T(8,128)S(1)}, u32[]{:S(2)}, u32[]{:S(2)}) collective-permute-start(f32[8,128]{1,0:T(8,128)S(1)} %get-tuple-element.61.l0), channel_id=1, source_target_pairs={{0,8},{4,12},{8,0},{12,4},{1,9},{5,13},{9,1},{13,5},{2,10},{6,14},... | collective-permute-start | bytes 12296 | tf_op jit(solution)/shard_map/ppermute | solution.py:366
  52.0 2.5 %collective-permute-start.9 = (f32[8,128]{1,0:T(8,128)S(1)}, f32[8,128]{1,0:T(8,128)S(1)}, u32[]{:S(2)}, u32[]{:S(2)}) collective-permute-start(f32[8,128]{1,0:T(8,128)S(1)} %get-tuple-element.61.l0), channel_id=1, source_target_pairs={{0,12},{4,0},{8,4},{12,8},{1,13},{5,1},{9,5},{13,9},{2,14},{6,2},{... | collective-permute-start | bytes 12296 | tf_op jit(solution)/shard_map/ppermute | solution.py:366
  55.4 4.0 %collective-permute-start.10 = (bf16[4,4,2,32,256]{4,3,2,1,0:T(8,128)(2,1)S(1)}, bf16[4,4,2,32,256]{4,3,2,1,0:T(8,128)(2,1)S(1)}, u32[]{:S(2)}, u32[]{:S(2)}) collective-permute-start(bf16[4,4,2,32,256]{4,3,2,1,0:T(8,128)(2,1)S(1)} %get-tuple-element.69), channel_id=1, source_target_pairs={{0,1},{1,0},{2,3},{3,2},{4,5},{5,4},{6,7},{7,6},{8,9},{9,8},{10,11... | collective-permute-start | bytes 1572872 | tf_op jit(solution)/shard_map/ppermute | solution.py:366
  59.7 7.9 %collective-permute-start.11 = (bf16[4,2,32,256]{3,2,1,0:T(8,128)(2,1)S(1)}, bf16[4,2,32,256]{3,2,1,0:T(8,128)(2,1)S(1)}, u32[]{:S(2)}, u32[]{:S(2)}) collective-permute-start(bf16[4,2,32,256]{3,2,1,0:T(8,128)(2,1)S(1)} %get-tuple-element.71), channel_id=1, source_target_pairs={{0,48},{16,0},{32,16},{48,32},{1,49},{17,1},{33,17},{49,33},{2,50}... | collective-permute-start | bytes 393224 | tf_op jit(solution)/shard_map/ppermute | solution.py:366
  62.1 6.2 %collective-permute-start.12 = (bf16[4,2,32,256]{3,2,1,0:T(8,128)(2,1)S(1)}, bf16[4,2,32,256]{3,2,1,0:T(8,128)(2,1)S(1)}, u32[]{:S(2)}, u32[]{:S(2)}) collective-permute-start(bf16[4,2,32,256]{3,2,1,0:T(8,128)(2,1)S(1)} %get-tuple-element.72), channel_id=1, source_target_pairs={{0,32},{16,48},{32,0},{48,16},{1,33},{17,49},{33,1},{49,17},{2,34}... | collective-permute-start | bytes 393224 | tf_op jit(solution)/shard_map/ppermute | solution.py:366
  62.5 9.3 %collective-permute-start.13 = (bf16[4,2,32,256]{3,2,1,0:T(8,128)(2,1)S(1)}, bf16[4,2,32,256]{3,2,1,0:T(8,128)(2,1)S(1)}, u32[]{:S(2)}, u32[]{:S(2)}) collective-permute-start(bf16[4,2,32,256]{3,2,1,0:T(8,128)(2,1)S(1)} %get-tuple-element.73), channel_id=1, source_target_pairs={{0,16},{16,32},{32,48},{48,0},{1,17},{17,33},{33,49},{49,1},{2,18}... | collective-permute-start | bytes 393224 | tf_op jit(solution)/shard_map/ppermute | solution.py:366
  62.8 1.7 %collective-permute-start.14 = (f32[8,128]{1,0:T(8,128)S(1)}, f32[8,128]{1,0:T(8,128)S(1)}, u32[]{:S(2)}, u32[]{:S(2)}) collective-permute-start(f32[8,128]{1,0:T(8,128)S(1)} %get-tuple-element.74.hg), channel_id=1, source_target_pairs={{0,1},{1,0},{2,3},{3,2},{4,5},{5,4},{6,7},{7,6},{8,9},{9,8},{10,11... | collective-permute-start | bytes 12296 | tf_op jit(solution)/shard_map/ppermute | solution.py:366
  72.6 17.2 %all-to-all-start.1 = ((bf16[32,8,384]{2,1,0:T(8,128)(2,1)}), bf16[32,8,384]{2,1,0:T(8,128)(2,1)S(1)}, u32[]{:S(2)}, u32[]{:S(2)}) async-start(bf16[32,8,384]{2,1,0:T(8,128)(2,1)} %bitcast.9), calls=%async_computation.1 | async-start | bytes 393216 | tf_op jit(solution)/shard_map/all_to_all | solution.py:475
  76.5 5.8 %collective-permute-start.15 = (bf16[128,384]{1,0:T(8,128)(2,1)S(1)}, bf16[128,384]{1,0:T(8,128)(2,1)S(1)}, u32[]{:S(2)}, u32[]{:S(2)}) collective-permute-start(bf16[128,384]{1,0:T(8,128)(2,1)S(1)} %get-tuple-element.77), channel_id=1, source_target_pairs={{0,12},{4,0},{8,4},{12,8},{1,13},{5,1},{9,5},{13,9},{2,14},{6,2},{... | collective-permute-start | bytes 294920 | tf_op jit(solution)/shard_map/ppermute | solution.py:366
  79.0 6.0 %collective-permute-start.16 = (bf16[128,384]{1,0:T(8,128)(2,1)S(1)}, bf16[128,384]{1,0:T(8,128)(2,1)S(1)}, u32[]{:S(2)}, u32[]{:S(2)}) collective-permute-start(bf16[128,384]{1,0:T(8,128)(2,1)S(1)} %get-tuple-element.78), channel_id=1, source_target_pairs={{0,8},{4,12},{8,0},{12,4},{1,9},{5,13},{9,1},{13,5},{2,10},{6,14},... | collective-permute-start | bytes 294920 | tf_op jit(solution)/shard_map/ppermute | solution.py:366
  79.5 9.3 %collective-permute-start.17 = (bf16[128,384]{1,0:T(8,128)(2,1)S(1)}, bf16[128,384]{1,0:T(8,128)(2,1)S(1)}, u32[]{:S(2)}, u32[]{:S(2)}) collective-permute-start(bf16[128,384]{1,0:T(8,128)(2,1)S(1)} %get-tuple-element.79), channel_id=1, source_target_pairs={{0,4},{4,8},{8,12},{12,0},{1,5},{5,9},{9,13},{13,1},{2,6},{6,10},{... | collective-permute-start | bytes 294920 | tf_op jit(solution)/shard_map/ppermute | solution.py:366

commit v6 on v5

--- a/solution.py
+++ b/solution.py
@@ -146,9 +146,9 @@
     for ys in range(4):
         top = jnp.full((1, WIDE), NEG, F32)
         for i, ch in enumerate(CHUNKS[ys]):
+            whole = times_t(kv_out[ch * HALF : (ch + 1) * HALF, :HEAD_WIDTH], q[ys])
             for z in range(2):
-                row = ch * HALF + z * BLOCK
-                s = times_t(kv_out[row : row + BLOCK, :HEAD_WIDTH], q[ys])
+                s = whole[z * BLOCK : (z + 1) * BLOCK]
                 if ch == ys:
                     key_at = inner + z * 256
                     ok = key_at <= query_at
@@ -212,23 +212,25 @@
 def middle_kernel(did, w, p0, p1, delta, alpha, kv1, kt0, u0, g0, g1, dq_out, kt1, u1):
     _, _, y, _, _ = coords(did)
     columns_half(w, y, kv1, kt1, u1)
-    for ys in range(4):
+    sides = ((p0, g0, kt0, u0), (p1, g1, kt1, u1))
+    for p, g, kt, u in sides:
+        for ch in range(4):
+            for z in range(2):
+                row = ch * HALF + z * BLOCK
+                ub = jnp.concatenate(
+                    [jnp.broadcast_to(u[row : row + BLOCK, h : h + 1], (BLOCK, BLOCK)) for h in range(GROUP)], axis=1
+                )
+                for ys in range(4):
+                    if ch in CHUNKS[ys]:
+                        at = (P_AT[ys] + CHUNKS[ys].index(ch)) * HALF + z * BLOCK
+                        rows = slice(at, at + BLOCK)
+                        g[rows, :] = (p[rows, :].astype(F32) * (ub - delta[ys, 0:1, :])).astype(BF16)
+    for ys in range(4):
+        keys = slice(CHUNKS[ys][0] * HALF, (CHUNKS[ys][-1] + 1) * HALF)
+        rows = slice(P_AT[ys] * HALF, (P_AT[ys] + len(CHUNKS[ys])) * HALF)
         total = jnp.zeros((HEAD_WIDTH, WIDE), F32)
-        for half, (p, g, kt, u) in enumerate(((p0, g0, kt0, u0), (p1, g1, kt1, u1))):
-            dqt = jnp.zeros((HEAD_WIDTH, WIDE), F32)
-            for i, ch in enumerate(CHUNKS[ys]):
-                at_p = (P_AT[ys] + i) * HALF
-                for z in range(2):
-                    row = ch * HALF + z * BLOCK
-                    at = slice(at_p + z * BLOCK, at_p + (z + 1) * BLOCK)
-                    ub = jnp.concatenate(
-                        [jnp.broadcast_to(u[row : row + BLOCK, h : h + 1], (BLOCK, BLOCK)) for h in range(GROUP)],
-                        axis=1,
-                    )
-                    g[at, :] = (p[at, :].astype(F32) * (ub - delta[ys, 0:1, :])).astype(BF16)
-                dqt = dqt + jnp.dot(
-                    kt[:, ch * HALF : (ch + 1) * HALF], g[at_p : at_p + HALF, :], preferred_element_type=F32
-                )
+        for half, (p, g, kt, u) in enumerate(sides):
+            dqt = jnp.dot(kt[:, keys], g[rows, :], preferred_element_type=F32)
             total = total + dqt * alpha[ys, half : half + 1, :]
         dq_out[ys] = total
 
@@ -238,14 +240,17 @@
         fa = f[ys, 0:1, :] * alpha[ys, half : half + 1, :]
         at16[ys] = (wt[...] * fa).astype(BF16)
         qf[ys] = (qt[ys].astype(F32) * (fa * SCALE)).astype(BF16)
+    dks, dvs = [None] * 4, [None] * 4
+    for ys in range(4):
+        at = slice(P_AT[ys] * HALF, (P_AT[ys] + len(CHUNKS[ys])) * HALF)
+        dk = times_t(g[at, :], qf[ys])
+        dv = times_t(p[at, :], at16[ys])
+        for i, ch in enumerate(CHUNKS[ys]):
+            rows = slice(i * HALF, (i + 1) * HALF)
+            dks[ch] = dk[rows] if dks[ch] is None else dks[ch] + dk[rows]
+            dvs[ch] = dv[rows] if dvs[ch] is None else dvs[ch] + dv[rows]
     for ch in range(4):
-        dk = jnp.zeros((HALF, HEAD_WIDTH), F32)
-        dv = jnp.zeros((HALF, HEAD_WIDTH), F32)
-        for ys in range(4):
-            if ch in CHUNKS[ys]:
-                at = (P_AT[ys] + CHUNKS[ys].index(ch)) * HALF
-                dk = dk + times_t(g[at : at + HALF, :], qf[ys])
-                dv = dv + times_t(p[at : at + HALF, :], at16[ys])
+        dk, dv = dks[ch], dvs[ch]
         both = jnp.concatenate([dk, dv], axis=1).astype(BF16)
         for z in range(2):
             for kx in range(4):

time: 90.9 us -> 90.7 us (level)
  transfers between devices with their start and end apart: 19 -> 19, of which waited for: 13 -> 13; matrix products, arithmetic and copies ran while one was open for 0% -> 0% of each run, Pallas kernels for 9% -> 8%
where the time goes in v6:
time: 90.7 us; the launch traced here: 90.3 us
  starting transfers between devices  29.3 us (32%)
  waiting for transfers between devices  26.5 us (29%)
  blocking collectives  21 us (23%)
  Pallas kernels  12.6 us (14%)
  between operations  0.91 us (1%)
    ppermute x18, waiting for transfers between devices, shift(): return lax.ppermute(v, axis, [(i, (i + k) % size) for i in range(size)])  26.5 us
    ppermute x18, starting transfers between devices, shift(): return lax.ppermute(v, axis, [(i, (i + k) % size) for i in range(size)])  25.5 us
    all_to_all x1, blocking collectives, per_device(): lax.all_to_all(copies.reshape(32, 8, 256), YZ_AXES, 0, 0, tiled=True)  21 us
    all_to_all x1, starting transfers between devices, per_device(): lax.all_to_all(by_z.reshape(32, 8, WIDE), YZ_AXES, 0, 0, tiled=True)  3.86 us
    pallas_call x1, Pallas kernels, per_device(): call(near_kernel, [like((4, WIDE, HEAD_WIDTH), BF16), wide_set, like((HEA...  2.14 us
  transfers between devices with their start and end apart: 19, of which 13 were waited for; matrix products, arithmetic and copies ran while one was open for 0% of the time, Pallas kernels for 8%

profile of v6, /device:TPU:1, one launch (start us, length us, event | category | flops | bytes accessed | tf_op | source)
XLA Modules:
  0.0 90.3 jit_solution(2524410886152540010)
XLA Ops:
  1.4 21.0 %all_to_all.10 = bf16[32,8,256]{2,1,0:T(8,128)(2,1)S(1)} all-to-all(bf16[32,8,256]{2,1,0:T(8,128)(2,1)S(1)} %bitcast.17), channel_id=1, replica_groups=mesh['zl'=4,'x'=4,'y'=4,'zh'=2,'c'=2] {'y','zh','zl'}, dimensions={0} | all-to-all | bytes 262144 | tf_op jit(solution)/shard_map/all_to_all | solution.py:401
  22.4 1.2 %collective-permute-start.3 = (bf16[4,2,32,256]{3,2,1,0:T(8,128)(2,1)S(1)}, bf16[4,2,32,256]{3,2,1,0:T(8,128)(2,1)S(1)}, u32[]{:S(2)}, u32[]{:S(2)}) collective-permute-start(bf16[4,2,32,256]{3,2,1,0:T(8,128)(2,1)S(1)} %bitcast.18), channel_id=1, source_target_pairs={{0,16},{16,32},{32,48},{48,0},{1,17},{17,33},{33,49},{49,1},{2,18}... | collective-permute-start | bytes 393224 | tf_op jit(solution)/shard_map/ppermute | solution.py:371
  23.6 2.5 %collective-permute-start.4 = (bf16[4,2,32,256]{3,2,1,0:T(8,128)(2,1)S(1)}, bf16[4,2,32,256]{3,2,1,0:T(8,128)(2,1)S(1)}, u32[]{:S(2)}, u32[]{:S(2)}) collective-permute-start(bf16[4,2,32,256]{3,2,1,0:T(8,128)(2,1)S(1)} %bitcast.19), channel_id=1, source_target_pairs={{0,32},{16,48},{32,0},{48,16},{1,33},{17,49},{33,1},{49,17},{2,34}... | collective-permute-start | bytes 393224 | tf_op jit(solution)/shard_map/ppermute | solution.py:371
  26.0 1.2 %collective-permute-start.5 = (bf16[4,2,32,256]{3,2,1,0:T(8,128)(2,1)S(1)}, bf16[4,2,32,256]{3,2,1,0:T(8,128)(2,1)S(1)}, u32[]{:S(2)}, u32[]{:S(2)}) collective-permute-start(bf16[4,2,32,256]{3,2,1,0:T(8,128)(2,1)S(1)} %bitcast.20), channel_id=1, source_target_pairs={{0,48},{16,0},{32,16},{48,32},{1,49},{17,1},{33,17},{49,33},{2,50}... | collective-permute-start | bytes 393224 | tf_op jit(solution)/shard_map/ppermute | solution.py:371
  27.4 2.7 %collective-permute-done.4.k2 = bf16[4,2,32,256]{3,2,1,0:T(8,128)(2,1)S(1)} collective-permute-done((bf16[4,2,32,256]{3,2,1,0:T(8,128)(2,1)S(1)}, bf16[4,2,32,256]{3,2,1,0:T(8,128)(2,1)S(1)}, u32[]{:S(2)}, u32[]{:S(2)}) %collective-permute-start.4) | collective-permute-done | bytes 131104 | tf_op jit(solution)/shard_map/ppermute | solution.py:371
  30.6 3.1 %collective-permute-start.6 = (bf16[1024,256]{1,0:T(8,128)(2,1)S(1)}, bf16[1024,256]{1,0:T(8,128)(2,1)S(1)}, u32[]{:S(2)}, u32[]{:S(2)}) collective-permute-start(bf16[1024,256]{1,0:T(8,128)(2,1)S(1)} %shard_map.112.kv.kv0), channel_id=1, source_target_pairs={{0,1},{1,0},{2,3},{3,2},{4,5},{5,4},{6,7},{7,6},{8,9},{9,8},{10,11... | collective-permute-start | bytes 1572872 | tf_op jit(solution)/shard_map/ppermute | solution.py:371
  33.7 1.2 %shard_map.110 = (bf16[144,384]{1,0:T(8,128)(2,1)S(1)}, bf16[144,384]{1,0:T(8,128)(2,1)S(1)}, bf16[144,384]{1,0:T(8,128)(2,1)S(1)}, bf16[144,384]{1,0:T(8,128)(2...) custom-call(s32[1]{0:T(128)} %bitcast.did, s32[1,128]{1,0:T(1,128)} %bitcast.26, s32[1,128]{1,0:T(1,128)} %bitcast.27, ...), custom_call_target="tpu_custom_call" | custom-call | tf_op jit(solution)/shard_map/pallas_call | solution.py:402
  35.3 1.7 %collective-permute-start.1 = (bf16[144,384]{1,0:T(8,128)(2,1)S(1)}, bf16[144,384]{1,0:T(8,128)(2,1)S(1)}, u32[]{:S(2)}, u32[]{:S(2)}) collective-permute-start(bf16[144,384]{1,0:T(8,128)(2,1)S(1)} %get-tuple-element.48), channel_id=1, source_target_pairs={{0,8},{4,12},{8,0},{12,4},{1,9},{5,13},{9,1},{13,5},{2,10},{6,14},... | collective-permute-start | bytes 331784 | tf_op jit(solution)/shard_map/ppermute | solution.py:371
  37.1 1.2 %collective-permute-start.2 = (bf16[144,384]{1,0:T(8,128)(2,1)S(1)}, bf16[144,384]{1,0:T(8,128)(2,1)S(1)}, u32[]{:S(2)}, u32[]{:S(2)}) collective-permute-start(bf16[144,384]{1,0:T(8,128)(2,1)S(1)} %get-tuple-element.49), channel_id=1, source_target_pairs={{0,12},{4,0},{8,4},{12,8},{1,13},{5,1},{9,5},{13,9},{2,14},{6,2},{... | collective-permute-start | bytes 331784 | tf_op jit(solution)/shard_map/ppermute | solution.py:371
  38.2 4.9 %collective-permute-done.q1.g1 = bf16[144,384]{1,0:T(8,128)(2,1)S(1)} collective-permute-done((bf16[144,384]{1,0:T(8,128)(2,1)S(1)}, bf16[144,384]{1,0:T(8,128)(2,1)S(1)}, u32[]{:S(2)}, u32[]{:S(2)}) %collective-permute-start) | collective-permute-done | bytes 110624 | tf_op jit(solution)/shard_map/ppermute | solution.py:371
  43.5 2.1 %shard_map.113 = (bf16[4,384,128]{2,1,0:T(8,128)(2,1)S(1)}, bf16[4,128,384]{2,1,0:T(8,128)(2,1)S(1)}, bf16[128,1024]{1,0:T(8,128)(2,1)S(1)}, f32[1024,128]{1,0:T...) custom-call(s32[1]{0:T(128)} %bitcast.did, ...), custom_call_target="tpu_custom_call" | custom-call | tf_op jit(solution)/shard_map/pallas_call | solution.py:431
  45.6 1.7 %shard_map.114 = (f32[8,128]{1,0:T(8,128)S(1)}, f32[4,8,384]{2,1,0:T(8,128)S(1)}, f32[4,8,384]{2,1,0:T(8,128)S(1)}, f32[4,8,384]{2,1,0:T(8,128)S(1)}, bf16[1792,384]{1,0:T(8,128)(2,1)S(1)}) custom-call(s32[1]{0:T(128)} %bitcast.did, s32[1,2048]{1,0:T(1,128)S(1)} %get-tuple-element.44.seg, f32[2,1536]{1,0:T(2,128)S(1)} %get-tuple-element.45.w, ...), custom_call_target="tpu_custom_call" | custom-call | tf_op jit(solution)/shard_map/pallas_call | solution.py:445
  47.3 1.2 %collective-permute-start.7 = (f32[8,128]{1,0:T(8,128)S(1)}, f32[8,128]{1,0:T(8,128)S(1)}, u32[]{:S(2)}, u32[]{:S(2)}) collective-permute-start(f32[8,128]{1,0:T(8,128)S(1)} %get-tuple-element.61.l0), channel_id=1, source_target_pairs={{0,4},{4,8},{8,12},{12,0},{1,5},{5,9},{9,13},{13,1},{2,6},{6,10},{... | collective-permute-start | bytes 12296 | tf_op jit(solution)/shard_map/ppermute | solution.py:371
  48.6 3.1 %collective-permute-start.8 = (f32[8,128]{1,0:T(8,128)S(1)}, f32[8,128]{1,0:T(8,128)S(1)}, u32[]{:S(2)}, u32[]{:S(2)}) collective-permute-start(f32[8,128]{1,0:T(8,128)S(1)} %get-tuple-element.61.l0), channel_id=1, source_target_pairs={{0,8},{4,12},{8,0},{12,4},{1,9},{5,13},{9,1},{13,5},{2,10},{6,14},... | collective-permute-start | bytes 12296 | tf_op jit(solution)/shard_map/ppermute | solution.py:371
  51.7 1.5 %shard_map.115 = (bf16[1792,384]{1,0:T(8,128)(2,1)S(1)}, bf16[1792,384]{1,0:T(8,128)(2,1)S(1)}, f32[4,128,384]{2,1,0:T(8,128)S(1)}) custom-call(s32[1]{0:T(128)} %bitcast.did, f32[2,1536]{1,0:T(2,128)S(1)} %get-tuple-element.45.w, bf16[1792,384]{1,0:T(8,128)(2,1)S(1)} %get-tuple-element.50.p0, bf16[1792,384]{1,0:T(8,128)(2,1)S(1)} %get-tuple-element.54.p1.p, ...), custom_call_target="tpu_custom_call" | custom-call | tf_op jit(solution)/shard_map/pallas_call | solution.py:454
  53.2 1.0 %collective-permute-done.9.l3 = f32[8,128]{1,0:T(8,128)S(1)} collective-permute-done((f32[8,128]{1,0:T(8,128)S(1)}, f32[8,128]{1,0:T(8,128)S(1)}, u32[]{:S(2)}, u32[]{:S(2)}) %collective-permute-start.9) | collective-permute-done | bytes 4128 | tf_op jit(solution)/shard_map/ppermute | solution.py:371
  54.2 1.0 %shard_map.116 = (bf16[4,4,2,32,256]{4,3,2,1,0:T(8,128)(2,1)S(1)}, f32[4,8,384]{2,1,0:T(8,128)S(1)}, f32[128,384]{1,0:T(8,128)S(1)}, f32[8,128]{1,0:T(8,128)S(1)}) custom-call(s32[1]{0:T(128)} %bitcast.did, f32[2,1536]{1,0:T(2,128)S(1)} %get-tuple-element.45.w, f32[8,128]{1,0:T(8,128)S(1)} %get-tuple-element.61.l0, f32[8,128]{1,0:T(8,128)S(1)} %collective-permute-done.7.l1, ...), custom_call_target="tpu_custom_call" | custom-call | tf_op jit(solution)/shard_map/pallas_call | solution.py:461
  55.2 2.3 %collective-permute-start.10 = (bf16[4,4,2,32,256]{4,3,2,1,0:T(8,128)(2,1)S(1)}, bf16[4,4,2,32,256]{4,3,2,1,0:T(8,128)(2,1)S(1)}, u32[]{:S(2)}, u32[]{:S(2)}) collective-permute-start(bf16[4,4,2,32,256]{4,3,2,1,0:T(8,128)(2,1)S(1)} %get-tuple-element.69), channel_id=1, source_target_pairs={{0,1},{1,0},{2,3},{3,2},{4,5},{5,4},{6,7},{7,6},{8,9},{9,8},{10,11... | collective-permute-start | bytes 1572872 | tf_op jit(solution)/shard_map/ppermute | solution.py:371
  57.4 1.8 %shard_map.117 = (bf16[4,4,2,32,256]{4,3,2,1,0:T(8,128)(2,1)S(1)}, f32[8,128]{1,0:T(8,128)S(1)}, bf16[128,384]{1,0:T(8,128)(2,1)S(1)}, bf16[128,384]{1,0:T(8,128...) custom-call(s32[1]{0:T(128)} %bitcast.did, bf16[1792,384]{1,0:T(8,128)(2,1)S(1)} %get-tuple-element.50.p0, ...), custom_call_target="tpu_custom_call" | custom-call | tf_op jit(solution)/shard_map/pallas_call | solution.py:468
  59.4 2.4 %collective-permute-start.11 = (bf16[4,2,32,256]{3,2,1,0:T(8,128)(2,1)S(1)}, bf16[4,2,32,256]{3,2,1,0:T(8,128)(2,1)S(1)}, u32[]{:S(2)}, u32[]{:S(2)}) collective-permute-start(bf16[4,2,32,256]{3,2,1,0:T(8,128)(2,1)S(1)} %get-tuple-element.71), channel_id=1, source_target_pairs={{0,48},{16,0},{32,16},{48,32},{1,49},{17,1},{33,17},{49,33},{2,50}... | collective-permute-start | bytes 393224 | tf_op jit(solution)/shard_map/ppermute | solution.py:371
  62.6 0.8 collective-permute-start.14
  63.4 0.8 collective-permute-done.14.hg_far
  64.2 3.1 %collective-permute-done.11.b1 = bf16[4,2,32,256]{3,2,1,0:T(8,128)(2,1)S(1)} collective-permute-done((bf16[4,2,32,256]{3,2,1,0:T(8,128)(2,1)S(1)}, bf16[4,2,32,256]{3,2,1,0:T(8,128)(2,1)S(1)}, u32[]{:S(2)}, u32[]{:S(2)}) %collective-permute-start.11) | collective-permute-done | bytes 131104 | tf_op jit(solution)/shard_map/ppermute | solution.py:371
  67.3 0.8 collective-permute-done.12.b2
  68.1 3.5 %collective-permute-done.13.b3 = bf16[4,2,32,256]{3,2,1,0:T(8,128)(2,1)S(1)} collective-permute-done((bf16[4,2,32,256]{3,2,1,0:T(8,128)(2,1)S(1)}, bf16[4,2,32,256]{3,2,1,0:T(8,128)(2,1)S(1)}, u32[]{:S(2)}, u32[]{:S(2)}) %collective-permute-start.13) | collective-permute-done | bytes 131104 | tf_op jit(solution)/shard_map/ppermute | solution.py:371
  71.6 0.8 shard_map.119
  72.4 3.9 %all-to-all-start.1 = ((bf16[32,8,384]{2,1,0:T(8,128)(2,1)}), bf16[32,8,384]{2,1,0:T(8,128)(2,1)S(1)}, u32[]{:S(2)}, u32[]{:S(2)}) async-start(bf16[32,8,384]{2,1,0:T(8,128)(2,1)} %bitcast.9), calls=%async_computation.1 | async-start | bytes 393216 | tf_op jit(solution)/shard_map/all_to_all | solution.py:480
  76.2 2.6 %collective-permute-start.15 = (bf16[128,384]{1,0:T(8,128)(2,1)S(1)}, bf16[128,384]{1,0:T(8,128)(2,1)S(1)}, u32[]{:S(2)}, u32[]{:S(2)}) collective-permute-start(bf16[128,384]{1,0:T(8,128)(2,1)S(1)} %get-tuple-element.77), channel_id=1, source_target_pairs={{0,12},{4,0},{8,4},{12,8},{1,13},{5,1},{9,5},{13,9},{2,14},{6,2},{... | collective-permute-start | bytes 294920 | tf_op jit(solution)/shard_map/ppermute | solution.py:371
  79.9 2.2 %collective-permute-done.15.d1 = bf16[128,384]{1,0:T(8,128)(2,1)S(1)} collective-permute-done((bf16[128,384]{1,0:T(8,128)(2,1)S(1)}, bf16[128,384]{1,0:T(8,128)(2,1)S(1)}, u32[]{:S(2)}, u32[]{:S(2)}) %collective-permute-start.15) | collective-permute-done | bytes 98336 | tf_op jit(solution)/shard_map/ppermute | solution.py:371
  82.1 2.7 %collective-permute-done.16.d2 = bf16[128,384]{1,0:T(8,128)(2,1)S(1)} collective-permute-done((bf16[128,384]{1,0:T(8,128)(2,1)S(1)}, bf16[128,384]{1,0:T(8,128)(2,1)S(1)}, u32[]{:S(2)}, u32[]{:S(2)}) %collective-permute-start.16) | collective-permute-done | bytes 98336 | tf_op jit(solution)/shard_map/ppermute | solution.py:371
  84.8 3.8 %collective-permute-done.17.d3 = bf16[128,384]{1,0:T(8,128)(2,1)S(1)} collective-permute-done((bf16[128,384]{1,0:T(8,128)(2,1)S(1)}, bf16[128,384]{1,0:T(8,128)(2,1)S(1)}, u32[]{:S(2)}, u32[]{:S(2)}) %collective-permute-start.17) | collective-permute-done | bytes 98336 | tf_op jit(solution)/shard_map/ppermute | solution.py:371
  88.6 0.9 %shard_map.121 = f32[128,1536]{1,0:T(8,128)} custom-call(s32[1]{0:T(128)} %bitcast.did, bf16[128,384]{1,0:T(8,128)(2,1)S(1)} %get-tuple-element.76.d0, bf16[128,384]{1,0:T(8,128)(2,1)S(1)} %collective-permute-done.15.d1, bf16[128,384]{1,0:T(8,128)(2,1)S(1)} %collective-permute-done.16.d2, bf16[128,384]{1,0:T(8,128)(2,1)S(1)} %collective-permute-done.17.d3), custom_call_target="tpu_custom_call" | custom-call | tf_op jit(solution)/shard_map/pallas_call | solution.py:484
  (19 shorter events, 4.9 us)
Async XLA Ops:
  22.4 5.0 %collective-permute-start.3 = (bf16[4,2,32,256]{3,2,1,0:T(8,128)(2,1)S(1)}, bf16[4,2,32,256]{3,2,1,0:T(8,128)(2,1)S(1)}, u32[]{:S(2)}, u32[]{:S(2)}) collective-permute-start(bf16[4,2,32,256]{3,2,1,0:T(8,128)(2,1)S(1)} %bitcast.18), channel_id=1, source_target_pairs={{0,16},{16,32},{32,48},{48,0},{1,17},{17,33},{33,49},{49,1},{2,18}... | collective-permute-start | bytes 393224 | tf_op jit(solution)/shard_map/ppermute | solution.py:371
  23.6 6.5 %collective-permute-start.4 = (bf16[4,2,32,256]{3,2,1,0:T(8,128)(2,1)S(1)}, bf16[4,2,32,256]{3,2,1,0:T(8,128)(2,1)S(1)}, u32[]{:S(2)}, u32[]{:S(2)}) collective-permute-start(bf16[4,2,32,256]{3,2,1,0:T(8,128)(2,1)S(1)} %bitcast.19), channel_id=1, source_target_pairs={{0,32},{16,48},{32,0},{48,16},{1,33},{17,49},{33,1},{49,17},{2,34}... | collective-permute-start | bytes 393224 | tf_op jit(solution)/shard_map/ppermute | solution.py:371
  26.0 4.6 %collective-permute-start.5 = (bf16[4,2,32,256]{3,2,1,0:T(8,128)(2,1)S(1)}, bf16[4,2,32,256]{3,2,1,0:T(8,128)(2,1)S(1)}, u32[]{:S(2)}, u32[]{:S(2)}) collective-permute-start(bf16[4,2,32,256]{3,2,1,0:T(8,128)(2,1)S(1)} %bitcast.20), channel_id=1, source_target_pairs={{0,48},{16,0},{32,16},{48,32},{1,49},{17,1},{33,17},{49,33},{2,50}... | collective-permute-start | bytes 393224 | tf_op jit(solution)/shard_map/ppermute | solution.py:371
  30.6 15.0 %collective-permute-start.6 = (bf16[1024,256]{1,0:T(8,128)(2,1)S(1)}, bf16[1024,256]{1,0:T(8,128)(2,1)S(1)}, u32[]{:S(2)}, u32[]{:S(2)}) collective-permute-start(bf16[1024,256]{1,0:T(8,128)(2,1)S(1)} %shard_map.112.kv.kv0), channel_id=1, source_target_pairs={{0,1},{1,0},{2,3},{3,2},{4,5},{5,4},{6,7},{7,6},{8,9},{9,8},{10,11... | collective-permute-start | bytes 1572872 | tf_op jit(solution)/shard_map/ppermute | solution.py:371
  34.9 8.2 %collective-permute-start = (bf16[144,384]{1,0:T(8,128)(2,1)S(1)}, bf16[144,384]{1,0:T(8,128)(2,1)S(1)}, u32[]{:S(2)}, u32[]{:S(2)}) collective-permute-start(bf16[144,384]{1,0:T(8,128)(2,1)S(1)} %get-tuple-element.47), channel_id=1, source_target_pairs={{0,4},{4,8},{8,12},{12,0},{1,5},{5,9},{9,13},{13,1},{2,6},{6,10},{... | collective-permute-start | bytes 331784 | tf_op jit(solution)/shard_map/ppermute | solution.py:371
  35.3 7.8 %collective-permute-start.1 = (bf16[144,384]{1,0:T(8,128)(2,1)S(1)}, bf16[144,384]{1,0:T(8,128)(2,1)S(1)}, u32[]{:S(2)}, u32[]{:S(2)}) collective-permute-start(bf16[144,384]{1,0:T(8,128)(2,1)S(1)} %get-tuple-element.48), channel_id=1, source_target_pairs={{0,8},{4,12},{8,0},{12,4},{1,9},{5,13},{9,1},{13,5},{2,10},{6,14},... | collective-permute-start | bytes 331784 | tf_op jit(solution)/shard_map/ppermute | solution.py:371
  37.1 6.4 %collective-permute-start.2 = (bf16[144,384]{1,0:T(8,128)(2,1)S(1)}, bf16[144,384]{1,0:T(8,128)(2,1)S(1)}, u32[]{:S(2)}, u32[]{:S(2)}) collective-permute-start(bf16[144,384]{1,0:T(8,128)(2,1)S(1)} %get-tuple-element.49), channel_id=1, source_target_pairs={{0,12},{4,0},{8,4},{12,8},{1,13},{5,1},{9,5},{13,9},{2,14},{6,2},{... | collective-permute-start | bytes 331784 | tf_op jit(solution)/shard_map/ppermute | solution.py:371
  47.3 5.8 %collective-permute-start.7 = (f32[8,128]{1,0:T(8,128)S(1)}, f32[8,128]{1,0:T(8,128)S(1)}, u32[]{:S(2)}, u32[]{:S(2)}) collective-permute-start(f32[8,128]{1,0:T(8,128)S(1)} %get-tuple-element.61.l0), channel_id=1, source_target_pairs={{0,4},{4,8},{8,12},{12,0},{1,5},{5,9},{9,13},{13,1},{2,6},{6,10},{... | collective-permute-start | bytes 12296 | tf_op jit(solution)/shard_map/ppermute | solution.py:371
  48.6 4.6 %collective-permute-start.8 = (f32[8,128]{1,0:T(8,128)S(1)}, f32[8,128]{1,0:T(8,128)S(1)}, u32[]{:S(2)}, u32[]{:S(2)}) collective-permute-start(f32[8,128]{1,0:T(8,128)S(1)} %get-tuple-element.61.l0), channel_id=1, source_target_pairs={{0,8},{4,12},{8,0},{12,4},{1,9},{5,13},{9,1},{13,5},{2,10},{6,14},... | collective-permute-start | bytes 12296 | tf_op jit(solution)/shard_map/ppermute | solution.py:371
  51.7 2.5 %collective-permute-start.9 = (f32[8,128]{1,0:T(8,128)S(1)}, f32[8,128]{1,0:T(8,128)S(1)}, u32[]{:S(2)}, u32[]{:S(2)}) collective-permute-start(f32[8,128]{1,0:T(8,128)S(1)} %get-tuple-element.61.l0), channel_id=1, source_target_pairs={{0,12},{4,0},{8,4},{12,8},{1,13},{5,1},{9,5},{13,9},{2,14},{6,2},{... | collective-permute-start | bytes 12296 | tf_op jit(solution)/shard_map/ppermute | solution.py:371
  55.2 4.1 %collective-permute-start.10 = (bf16[4,4,2,32,256]{4,3,2,1,0:T(8,128)(2,1)S(1)}, bf16[4,4,2,32,256]{4,3,2,1,0:T(8,128)(2,1)S(1)}, u32[]{:S(2)}, u32[]{:S(2)}) collective-permute-start(bf16[4,4,2,32,256]{4,3,2,1,0:T(8,128)(2,1)S(1)} %get-tuple-element.69), channel_id=1, source_target_pairs={{0,1},{1,0},{2,3},{3,2},{4,5},{5,4},{6,7},{7,6},{8,9},{9,8},{10,11... | collective-permute-start | bytes 1572872 | tf_op jit(solution)/shard_map/ppermute | solution.py:371
  59.4 7.9 %collective-permute-start.11 = (bf16[4,2,32,256]{3,2,1,0:T(8,128)(2,1)S(1)}, bf16[4,2,32,256]{3,2,1,0:T(8,128)(2,1)S(1)}, u32[]{:S(2)}, u32[]{:S(2)}) collective-permute-start(bf16[4,2,32,256]{3,2,1,0:T(8,128)(2,1)S(1)} %get-tuple-element.71), channel_id=1, source_target_pairs={{0,48},{16,0},{32,16},{48,32},{1,49},{17,1},{33,17},{49,33},{2,50}... | collective-permute-start | bytes 393224 | tf_op jit(solution)/shard_map/ppermute | solution.py:371
  61.9 6.2 %collective-permute-start.12 = (bf16[4,2,32,256]{3,2,1,0:T(8,128)(2,1)S(1)}, bf16[4,2,32,256]{3,2,1,0:T(8,128)(2,1)S(1)}, u32[]{:S(2)}, u32[]{:S(2)}) collective-permute-start(bf16[4,2,32,256]{3,2,1,0:T(8,128)(2,1)S(1)} %get-tuple-element.72), channel_id=1, source_target_pairs={{0,32},{16,48},{32,0},{48,16},{1,33},{17,49},{33,1},{49,17},{2,34}... | collective-permute-start | bytes 393224 | tf_op jit(solution)/shard_map/ppermute | solution.py:371
  62.3 9.3 %collective-permute-start.13 = (bf16[4,2,32,256]{3,2,1,0:T(8,128)(2,1)S(1)}, bf16[4,2,32,256]{3,2,1,0:T(8,128)(2,1)S(1)}, u32[]{:S(2)}, u32[]{:S(2)}) collective-permute-start(bf16[4,2,32,256]{3,2,1,0:T(8,128)(2,1)S(1)} %get-tuple-element.73), channel_id=1, source_target_pairs={{0,16},{16,32},{32,48},{48,0},{1,17},{17,33},{33,49},{49,1},{2,18}... | collective-permute-start | bytes 393224 | tf_op jit(solution)/shard_map/ppermute | solution.py:371
  62.6 1.7 %collective-permute-start.14 = (f32[8,128]{1,0:T(8,128)S(1)}, f32[8,128]{1,0:T(8,128)S(1)}, u32[]{:S(2)}, u32[]{:S(2)}) collective-permute-start(f32[8,128]{1,0:T(8,128)S(1)} %get-tuple-element.74.hg), channel_id=1, source_target_pairs={{0,1},{1,0},{2,3},{3,2},{4,5},{5,4},{6,7},{7,6},{8,9},{9,8},{10,11... | collective-permute-start | bytes 12296 | tf_op jit(solution)/shard_map/ppermute | solution.py:371
  72.4 17.2 %all-to-all-start.1 = ((bf16[32,8,384]{2,1,0:T(8,128)(2,1)}), bf16[32,8,384]{2,1,0:T(8,128)(2,1)S(1)}, u32[]{:S(2)}, u32[]{:S(2)}) async-start(bf16[32,8,384]{2,1,0:T(8,128)(2,1)} %bitcast.9), calls=%async_computation.1 | async-start | bytes 393216 | tf_op jit(solution)/shard_map/all_to_all | solution.py:480
  76.2 5.8 %collective-permute-start.15 = (bf16[128,384]{1,0:T(8,128)(2,1)S(1)}, bf16[128,384]{1,0:T(8,128)(2,1)S(1)}, u32[]{:S(2)}, u32[]{:S(2)}) collective-permute-start(bf16[128,384]{1,0:T(8,128)(2,1)S(1)} %get-tuple-element.77), channel_id=1, source_target_pairs={{0,12},{4,0},{8,4},{12,8},{1,13},{5,1},{9,5},{13,9},{2,14},{6,2},{... | collective-permute-start | bytes 294920 | tf_op jit(solution)/shard_map/ppermute | solution.py:371
  78.8 6.0 %collective-permute-start.16 = (bf16[128,384]{1,0:T(8,128)(2,1)S(1)}, bf16[128,384]{1,0:T(8,128)(2,1)S(1)}, u32[]{:S(2)}, u32[]{:S(2)}) collective-permute-start(bf16[128,384]{1,0:T(8,128)(2,1)S(1)} %get-tuple-element.78), channel_id=1, source_target_pairs={{0,8},{4,12},{8,0},{12,4},{1,9},{5,13},{9,1},{13,5},{2,10},{6,14},... | collective-permute-start | bytes 294920 | tf_op jit(solution)/shard_map/ppermute | solution.py:371
  79.3 9.3 %collective-permute-start.17 = (bf16[128,384]{1,0:T(8,128)(2,1)S(1)}, bf16[128,384]{1,0:T(8,128)(2,1)S(1)}, u32[]{:S(2)}, u32[]{:S(2)}) collective-permute-start(bf16[128,384]{1,0:T(8,128)(2,1)S(1)} %get-tuple-element.79), channel_id=1, source_target_pairs={{0,4},{4,8},{8,12},{12,0},{1,5},{5,9},{9,13},{13,1},{2,6},{6,10},{... | collective-permute-start | bytes 294920 | tf_op jit(solution)/shard_map/ppermute | solution.py:371
